TPU v7x, 32 devices: a whole 2x2x4 slice. The times are simulated.
32 devices in a mesh: expert: 4 (over y, core), fsdp: 8 (over z, x).
Axes of the slice: x: 2, y: 2, z: 4, core: 2. Of those that a mesh axis runs over, the one named last changes fastest.
Arguments:
- tokens: bfloat16 [8, 1024, 768], P('fsdp', 'expert'), may hold values from -40 to 40
- gain_one: bfloat16 [768], P('fsdp'), may hold values from 0.5 to 1.5
- qkv_weight: bfloat16 [768, 2304], P('fsdp'), may hold values from -0.21875 to 0.21875
- out_weight: bfloat16 [768, 768], P('fsdp'), may hold values from -3.5 to 3.5
- gain_two: bfloat16 [768], P('fsdp'), may hold values from 0.5 to 1.5
- router_weight: bfloat16 [768, 8], P('fsdp'), may hold values from -0.109375 to 0.109375
- const_gate: bfloat16 [768, 4], P('fsdp'), may hold values from -0.21875 to 0.21875
- const_value: bfloat16 [768, 2], P('fsdp'), may hold values from -5 to 5
- expert_gate_up: bfloat16 [4, 768, 4096], P('expert', 'fsdp'), may hold values from -0.21875 to 0.21875
- expert_down: bfloat16 [4, 2048, 768], P('expert', 'fsdp'), may hold values from -0.125 to 0.125
- gate_residual: bfloat16 [8, 1024, 8], P('fsdp', 'expert'), may hold values from -3 to 3
- routes: int32 [8, 1024, 2], P('fsdp', 'expert'), may hold values from 0 to 7, all different within a row; in each aligned block of 256 rows (0 to 255, 256 to 511, ..., all dimensions but the last counted through in order) at most 80 rows name the same one
- cotangent: bfloat16 [8, 1024, 768], P('fsdp', 'expert'), may hold values from -6 to 6
Outputs:
- block_output: bfloat16 [8, 1024, 768], P('fsdp', 'expert')
- grad_tokens: bfloat16 [8, 1024, 768], P('fsdp', 'expert')
- grad_gain_one: float32 [768], P('fsdp')
- grad_qkv: float32 [768, 2304], P('fsdp')
- grad_out: float32 [768, 768], P('fsdp')
- grad_gain_two: float32 [768], P('fsdp')
- grad_router: float32 [768, 8], P('fsdp')
- grad_const_gate: float32 [768, 4], P('fsdp')
- grad_const_value: float32 [768, 2], P('fsdp')
- grad_gate_up: float32 [4, 768, 4096], P('expert', 'fsdp')
- grad_down: float32 [4, 2048, 768], P('expert', 'fsdp')
- grad_gate_residual: bfloat16 [8, 1024, 8], P('fsdp', 'expert')
- stream_rms: float32 [8, 2], P('fsdp')
Inputs may be any that keep to these rules, and one draw needn't show every extreme that they name: In each aligned block of 256 rows (one sequence's positions on one index of expert) no expert is named by more than 80 routes; experts 4 to 7 are the zero, copy and constant experts.
All inputs are finite; a program needn't handle non-finite values.
Results may differ from a plain program's by a relative error of at most 0.024.
Values may be sent and summed in bfloat16 or wider, within the bound.
No kernel may reach another device: no remote copies, remote signals or barrier semaphores. Data moves between devices by JAX's collectives and lax.ppermute only.
A program may use at most 192 MiB of HBM per device.

v0:
```python
import functools

import jax
import jax.numpy as jnp
from jax import lax
from jax.experimental import pallas as pl
from jax.experimental.pallas import tpu as pltpu
from jax.sharding import PartitionSpec as P

HEAD = 64
FF = 2048
NCONST = 2
MOST = 80
PAIR = 2 * HEAD
SMALL = 128

epsilon = 1e-06
masked_score = -1e30
BF = jnp.bfloat16
F32 = jnp.float32


def mm(a, b):
    return jnp.dot(a, b, preferred_element_type=F32)


def mm_nt(a, b):
    return lax.dot_general(a, b, (((1,), (1,)), ((), ())), preferred_element_type=F32)


def mm_tn(a, b):
    return lax.dot_general(a, b, (((0,), (0,)), ((), ())), preferred_element_type=F32)


def split_low(values):
    high = values.astype(BF)
    return high, (values - high.astype(F32)).astype(BF)


def lanes(shape):
    return lax.broadcasted_iota(jnp.int32, shape, len(shape) - 1)


def rows_of(shape):
    return lax.broadcasted_iota(jnp.int32, shape, 0)


def rms_scale(values):
    return lax.rsqrt(jnp.mean(values * values, axis=-1, keepdims=True) + epsilon)


def turned(values, cosine, sine):
    lane = lanes(values.shape) % HEAD
    swapped = jnp.where(
        lane < HEAD // 2,
        pltpu.roll(values, PAIR - HEAD // 2, 1),
        pltpu.roll(values, HEAD // 2, 1),
    )
    return values * cosine + swapped * sine


def call(kernel, outs, args, grid=(), in_specs=None, out_specs=None, scratch=(), scalars=1, name=None, micros=2):
    whole = pl.BlockSpec(memory_space=pltpu.VMEM)
    multi = isinstance(outs, (tuple, list))
    if in_specs is None:
        in_specs = [whole] * (len(args) - scalars)
    if out_specs is None:
        out_specs = [whole] * len(outs) if multi else whole
    return pl.pallas_call(
        kernel,
        out_shape=outs,
        grid_spec=pltpu.PrefetchScalarGridSpec(
            num_scalar_prefetch=scalars,
            grid=grid,
            in_specs=in_specs,
            out_specs=out_specs,
            scratch_shapes=list(scratch),
        ),
        compiler_params=pltpu.CompilerParams(vmem_limit_bytes=56 * 1024 * 1024),
        cost_estimate=pl.CostEstimate(
            flops=micros * 90_000_000, transcendentals=0, bytes_accessed=micros * 300_000
        ),
        name=name,
    )(*args)


def shaped(shape, dtype):
    return jax.ShapeDtypeStruct(shape, dtype)


def swap(values, axis, bits):
    size = lax.axis_size(axis)
    return lax.ppermute(values, axis, [(i, i ^ bits) for i in range(size)])


def along(values, pairs):
    return lax.ppermute(
        values, "fsdp", [(2 * i + b, 2 * j + b) for i, j in pairs for b in (0, 1)]
    )


def after(values, *others):
    return lax.optimization_barrier((values,) + tuple(others))[0]


FAR = ((0, 2), (2, 0), (1, 3), (3, 1))
NEAR = ((0, 1), (1, 0), (2, 3), (3, 2))
MIDDLE = ((1, 2), (2, 1))
OUTWARD = ((2, 3), (1, 0))
INWARD = ((0, 1), (3, 2))


def minor_groups(major):
    return [[2 * i + b for i in range(major)] for b in (0, 1)]


def blocks_kernel(where, gate_up, out):
    rows = gate_up.shape[0]
    for block in range(8):
        at = (2 * block + 1 - where[0]) * 256
        out[block * rows : (block + 1) * rows, :] = gate_up[:, pl.ds(pl.multiple_of(at, 256), 256)]


def pack_kernel(where, gate_up, arrived, out):
    rows = gate_up.shape[0]
    mine = where[0]
    for block in range(8):
        at = (2 * block + mine) * 256
        own = pl.ds(pl.multiple_of(2 * block * rows + mine * rows, rows), rows)
        other = pl.ds(pl.multiple_of(2 * block * rows + (1 - mine) * rows, rows), rows)
        out[own, :] = gate_up[:, pl.ds(pl.multiple_of(at, 256), 256)]
        out[other, :] = arrived[block * rows : (block + 1) * rows, :]


def sum_parts_kernel(where, a, b, c, d0, d1, d2, away, kept, down):
    rows = away.shape[0] // 8
    mine = where[0]

    def total(start, size, d, base):
        source, shifted = pl.ds(start, size), pl.ds(start - base, size)
        return (
            a[source, :].astype(F32)
            + b[source, :].astype(F32)
            + c[source, :].astype(F32)
            + d[shifted, :].astype(F32)
        )

    for block in range(8):
        here = slice(block * rows, (block + 1) * rows)
        base = 2 * block * rows
        d, cut = ((d0, 0), (d1, 8 * rows), (d2, 14 * rows))[(block > 3) + (block > 6)]
        own = pl.multiple_of(base + mine * rows, rows)
        other = pl.multiple_of(base + (1 - mine) * rows, rows)
        away[here, :] = total(other, rows, d, cut).astype(BF)
        kept[here, :] = total(own, rows, d, cut)
    for block in range(3):
        base = 16 * rows + block * 256
        down[:, block * 256 : (block + 1) * 256] = total(base, 256, d2, 14 * rows)


def unpack_kernel(where, kept, arrived, out):
    rows = out.shape[0]
    mine = where[0]
    for block in range(8):
        here = slice(block * rows, (block + 1) * rows)
        own = pl.ds(pl.multiple_of((2 * block + mine) * 256, 256), 256)
        other = pl.ds(pl.multiple_of((2 * block + 1 - mine) * 256, 256), 256)
        out[:, own] = kept[here, :]
        out[:, other] = arrived[here, :].astype(F32)


def shared_pack(qkv, out, small_rows):
    core = lax.axis_index("expert") % 2
    half_qkv, half_out = qkv.shape[1] // 2, out.shape[1] // 2
    rows = qkv.shape[0]

    def kernel(where, qkv_ref, out_ref, small_ref, packed):
        packed[:, :half_qkv] = qkv_ref[:, pl.ds(pl.multiple_of(where[0] * half_qkv, 128), half_qkv)]
        packed[:, half_qkv : half_qkv + half_out] = out_ref[
            :, pl.ds(pl.multiple_of(where[0] * half_out, 128), half_out)
        ]
        packed[:32, half_qkv + half_out :] = small_ref[...]
        packed[32:, half_qkv + half_out :] = jnp.zeros((rows - 32, SMALL), BF)

    return call(
        kernel,
        shaped((rows, half_qkv + half_out + SMALL), BF),
        (jnp.stack([core]).astype(jnp.int32), qkv, out, small_rows),
        name="pack_shared",
        micros=1,
    )


def shared_gather(mine, down, early, late):
    me = lax.axis_index("fsdp")
    major = [mine, swap(mine, "fsdp", 2), swap(mine, "fsdp", 4)]
    minor = [swap(mine, "fsdp", 1)]
    major.append(swap(after(mine, minor[0]), "fsdp", 6))
    minor.append(swap(after(major[1], minor[0]), "fsdp", 1))
    minor.append(swap(after(major[2], *early), "fsdp", 1))
    minor.append(swap(after(major[3], minor[1], *late), "fsdp", 1))
    down_near = along(after(down, major[3]), NEAR)
    down_far = along(after(down, major[3]), FAR)
    slots = [2 * j for j in range(4)] + [2 * j + 1 for j in range(4)]
    own = after(jnp.concatenate(major + minor, axis=0), down_near, down_far)
    return own, swap(own, "expert", 1), [me ^ s for s in slots], down_near, down_far


def added(kept, arrived):
    return (kept.astype(F32) + arrived.astype(F32)).astype(BF)


def along_chips(both, gate):
    for axis, bits in (("expert", 2), ("fsdp", 1)):
        half = both.shape[0] // 2
        both = added(after(both[:half], *gate), swap(both[half:], axis, bits))
        gate = ()
    return both


def across_major(parts, rows):
    pieces = [swap(parts[j * rows : (j + 1) * rows], "fsdp", 2 * j) for j in (1, 2, 3)]
    total = parts[:rows].astype(F32)
    for piece in pieces:
        total += piece.astype(F32)
    return total.astype(BF), pieces[0]


def sequence_gather(values, across):
    size = lax.axis_size("expert")
    me = lax.axis_index("expert")
    if size != 4:
        every = lax.all_gather(values, "expert", axis=0, tiled=True)
        middle = every.shape[0] // 2
        return every[:middle], every[middle:], list(range(size))
    pair = jnp.concatenate([values, across], axis=0)
    return pair, swap(pair, "expert", 1), [me, me ^ 2, me ^ 1, me ^ 3]


def exchange(sends):
    half = len(sends) // 2
    received = [swap(v, "expert", j) if j else v for j, v in enumerate(sends)]
    low = swap(jnp.concatenate(received[:half], axis=0), "fsdp", 1)
    high = swap(after(jnp.concatenate(received[half:], axis=0), low), "fsdp", 1)
    return received, low, high


def exchange_back(low, high, size):
    rows = 2 * low.shape[0] // size
    if size == 4:
        upper = swap(high, "expert", 2)
        joined = swap(jnp.concatenate([low[rows:], upper[rows:]], axis=0), "expert", 1)
        return [low[:rows], joined[:rows], upper[:rows], joined[rows:]]
    pieces = [w[i : i + rows] for w in (low, high) for i in range(0, w.shape[0], rows)]
    return [swap(piece, "expert", j) if j else piece for j, piece in enumerate(pieces)]


def sequence_scatter_sum(full, rows):
    size = lax.axis_size("expert")
    me = lax.axis_index("expert")
    if size != 4:
        return lax.psum_scatter(full, "expert", scatter_dimension=0, tiled=True).astype(F32)

    def block(bits):
        return lax.dynamic_slice_in_dim(full, (me ^ bits) * rows, rows, 0)

    away = jnp.concatenate([block(1), block(3)], axis=0)
    kept = jnp.concatenate([block(0), block(2)], axis=0)
    both = kept.astype(F32) + swap(away, "expert", 1).astype(F32)
    return both[:rows] + swap(both[rows:].astype(BF), "expert", 2).astype(F32)


def project_kernel(where, *refs, slots, gain_at, placed):
    if placed:
        tok_a, tok_b, cosine, sine, weight, small_t, q, k, v, normed = refs
    else:
        tok_a, tok_b, cosine, sine, own_ref, other_ref = refs[:6]
        q, k, v, normed, weight, out_ref, small_ref, small_t = refs[6:]
    step = pl.program_id(0)
    rank = where[step]
    own = where[slots]
    width = tok_a.shape[1]

    if not placed:

        @pl.when(step == 0)
        def _():
            first = where[slots + 9] == 0
            rows = width // 8
            half_qkv, half_out = 3 * width // 2, width // 2
            for index in range(8):
                source = pl.ds(index * rows, rows)
                target = pl.ds(pl.multiple_of(where[slots + 1 + index] * rows, rows), rows)
                a, b = own_ref[source, :], other_ref[source, :]
                left = jnp.where(first, a, b)
                right = jnp.where(first, b, a)
                weight[target, :half_qkv] = left[:, :half_qkv]
                weight[target, half_qkv:] = right[:, :half_qkv]
                out_ref[target, :half_out] = left[:, half_qkv : half_qkv + half_out]
                out_ref[target, half_out:] = right[:, half_qkv : half_qkv + half_out]
                of_rows = jnp.zeros((SMALL, SMALL), F32)
                of_rows = jnp.concatenate(
                    [a[:32, half_qkv + half_out :].astype(F32), of_rows[32:]], axis=0
                ).T
                small_ref[target, :] = of_rows[:rows].astype(BF)
            small_t[...] = small_ref[...].astype(F32).T[:32]

    @pl.when(rank > own)
    def _():
        k[...] = jnp.zeros_like(k)
        v[...] = jnp.zeros_like(v)
        normed[...] = jnp.zeros_like(normed)

    @pl.when(rank <= own)
    def _():
        x = jnp.where(step < slots // 2, tok_a[...], tok_b[...]).astype(F32)
        wide = (x * rms_scale(x)) * small_t[gain_at : gain_at + 1, :]
        low = wide.astype(BF)
        normed[...] = low.T
        cos, sin = cosine[...], sine[...]
        keys = mm(low, weight[:, width : 2 * width])
        for at in range(0, width, PAIR):
            k[:, at : at + PAIR] = turned(keys[:, at : at + PAIR], cos, sin).astype(BF)
        v[...] = mm(low, weight[:, 2 * width :]).astype(BF)

        @pl.when(rank == own)
        def _():
            queries = mm(low, weight[:, :width])
            for at in range(0, width, PAIR):
                q[:, at : at + PAIR] = turned(queries[:, at : at + PAIR], cos, sin).astype(BF)


def stacked_heads(values, scale=None):
    lane = lanes(values.shape)
    if scale is not None:
        values = values * jnp.asarray(scale, values.dtype)
    zero = jnp.zeros_like(values)
    return jnp.concatenate(
        [jnp.where(lane < HEAD, values, zero), jnp.where(lane < HEAD, zero, values)], axis=0
    )


def visible_keys(own, keys, count):
    key = lax.broadcasted_iota(jnp.int32, (keys, 2 * count), 0)
    query = lax.broadcasted_iota(jnp.int32, (keys, 2 * count), 1) % count
    return key <= query + own * count


def attend_kernel(where, q, k, v, attended, log_total, *, slots):
    own = where[slots]
    count, keys = q.shape[0], k.shape[0]
    query = stacked_heads(q[...], HEAD ** (-0.5))
    scores = mm_nt(k[...], query)
    scores = jnp.where(visible_keys(own, keys, count), scores, masked_score)
    top = jnp.max(scores, axis=0, keepdims=True)
    weights = jnp.exp(scores - top)
    total = jnp.sum(weights, axis=0, keepdims=True)
    log_total[...] = jnp.broadcast_to(top + jnp.log(total), (8, 2 * count))[None]
    weights = (weights * (1.0 / total)).astype(BF)
    both = mm_tn(weights, v[...])
    lane = lanes((count, PAIR))
    attended[...] = jnp.where(lane < HEAD, both[:count], both[count:]).astype(BF)


def attend_back_kernel(where, q, k, v, grad_att, log_total, cosine, sine, normed, normed_own, dq, dk, dv, away, kept, sums, *, slots, packed):
    step = pl.program_id(0)
    own = where[slots]
    count, keys = q.shape[0], k.shape[0]
    query = stacked_heads(q[...], HEAD ** (-0.5))
    grad_rows = stacked_heads(grad_att[...])
    key_rows = k[...]
    scores = mm_nt(key_rows, query)
    weights = jnp.where(
        visible_keys(own, keys, count), jnp.exp(scores - log_total[0, :1, :]), 0.0
    )
    grad_weights = mm_nt(v[...], grad_rows)
    delta = jnp.sum(weights * grad_weights, axis=0, keepdims=True)
    grad_scores = (weights * (grad_weights - delta)).astype(BF)
    grad_v = mm(weights.astype(BF), grad_rows).astype(BF)
    dv[...] = grad_v
    grad_k = turned(mm(grad_scores, query), cosine[...], -sine[...]).astype(BF)
    dk[...] = grad_k
    both = mm_tn(grad_scores, key_rows)
    lane = lanes((count, PAIR))
    grad_q = jnp.where(lane < HEAD, both[:count], both[count:]) * HEAD ** (-0.5)
    mine = pl.ds(pl.multiple_of(own * count, count), count)
    grad_q = turned(grad_q, cosine[mine, :], -sine[mine, :]).astype(BF)
    dq[...] = grad_q
    of_keys = mm(normed[...], jnp.concatenate([grad_k, grad_v], axis=1))
    of_queries = mm(normed_own[...], grad_q)
    steps = kept.shape[1] // (3 * PAIR)
    for index in range(steps):

        @pl.when(step == index)
        def _():
            for part, values in enumerate((of_queries, of_keys[:, :PAIR], of_keys[:, PAIR:])):
                at = (part * steps + index) * PAIR
                sums[:, at : at + PAIR] = values

    @pl.when(step == steps - 1)
    def _():
        if packed:
            split_rows(where, slots + 1, sums, away, kept)
        else:
            kept[...] = sums[...].astype(BF)
            away[...] = jnp.zeros_like(away)


def split_rows(where, at, values, away, kept):
    core, chip = where[at + 8], where[at + 9]
    rows = values.shape[0] // 32
    for index in range(0, 16, 2):
        target = slice(index * rows, (index + 2) * rows)
        for ref, side in ((kept, core), (away, 1 - core)):
            pieces = []
            for step in (index, index + 1):
                rank = 2 * (chip ^ (step // 8)) + side
                base = (where[at + step % 8] * 4 + rank) * rows
                pieces.append(values[pl.ds(pl.multiple_of(base, 8), rows), :])
            ref[target, :] = jnp.concatenate(pieces, axis=0).astype(BF)


def routing(routes, resid, logits, groups):
    count = routes.shape[0]
    lane = lanes((count, SMALL))
    kind = lanes(resid.shape)
    hot, picked = [], []
    for choice in range(2):
        route = routes[:, choice : choice + 1]
        hot.append(lane == route)
        picked.append(
            jnp.sum(jnp.where(hot[choice], logits, 0.0), axis=-1, keepdims=True)
            + jnp.sum(jnp.where(kind == route, resid, 0.0), axis=-1, keepdims=True)
        )
    top = jnp.maximum(picked[0], picked[1])
    first, second = jnp.exp(picked[0] - top), jnp.exp(picked[1] - top)
    gates = [first / (first + second), second / (first + second)]
    named = jnp.logical_or(hot[0], hot[1]).astype(BF)
    earlier = (lanes((count, count)) < rows_of((count, count))).astype(BF)
    place = mm(earlier, named)
    dispatch = []
    column = lanes((count, groups * MOST))
    for choice in range(2):
        route = routes[:, choice : choice + 1]
        slot = jnp.sum(jnp.where(hot[choice], place, 0.0), axis=-1, keepdims=True)
        target = jnp.where(route < groups, route * MOST + slot.astype(jnp.int32), -1)
        dispatch.append((column == target).astype(BF))
    return gates, hot, dispatch


def route_kernel(where, att, out_weight, tok, small, small_t, resid, routes, cot, hidden_ref, low_ref, *rest, groups, gain_at):
    sends = rest[:groups]
    rows_x, rows_g = rest[groups], rest[groups + 1]
    hidden = tok[...].astype(F32) + mm(att[...], out_weight[...])
    hidden_ref[...] = hidden
    low = ((hidden * rms_scale(hidden)) * small_t[gain_at : gain_at + 1, :]).astype(BF)
    low_ref[...] = low
    logits = mm(low, small[...])
    gates, _, dispatch = routing(routes[...], resid[...].astype(F32), logits, groups)
    grad = cot[...].astype(F32)
    rows_x[...] = mm_tn(dispatch[0] + dispatch[1], low).astype(BF)
    rows_g[...] = (
        mm_tn(dispatch[0], (gates[0] * grad).astype(BF))
        + mm_tn(dispatch[1], (gates[1] * grad).astype(BF))
    ).astype(BF)
    for slot in range(groups):
        source = pl.ds(pl.multiple_of(where[slot] * MOST, MOST), MOST)
        sends[slot][:MOST, :] = rows_x[source, :]
        sends[slot][MOST:, :] = rows_g[source, :]


def expert_kernel(where, *refs, groups, hidden_units, packed):
    refs = list(refs)

    def take(amount):
        taken = refs[:amount]
        del refs[:amount]
        return taken

    received = take(groups) + take(2)
    if packed:
        unit_parts, down_parts = take(5), take(5)
    else:
        gate_up, down = take(2)
    own_out, other_out = take(2), take(2)
    if packed:
        messages = take(4)
    else:
        grad_gate_up, grad_down = take(2)
    rows, grads, out_rows, back_rows, acts, grad_units = take(6)
    if packed:
        gate_up, down = take(2)
    width = rows.shape[1]
    total = 2 * groups * MOST
    index = 0
    for ref in received:
        for base in range(0, ref.shape[0], 2 * MOST):
            target = slice(index * MOST, (index + 1) * MOST)
            rows[target, :] = ref[base : base + MOST, :]
            grads[target, :] = ref[base + MOST : base + 2 * MOST, :]
            index += 1
    if packed:
        part = width // 4

        def place(slot, ref, down_ref):
            target = pl.ds(pl.multiple_of(where[slot] * part, part), part)
            for block in range(8):
                gate_up[target, block * 256 : (block + 1) * 256] = ref[
                    block * part : (block + 1) * part, :
                ]
            down[pl.ds(pl.multiple_of(where[slot] * 256, 256), 256), :] = down_ref[...]

        for slot in range(3):
            place(slot, unit_parts[slot], down_parts[slot])

        @pl.when(where[4] == 1)
        def _():
            place(3, unit_parts[3], down_parts[3])

        @pl.when(where[4] == 0)
        def _():
            place(3, unit_parts[4], down_parts[4])

    x, g = rows[...], grads[...]
    chunk = 256
    out_rows[...] = jnp.zeros_like(out_rows)
    back_rows[...] = jnp.zeros_like(back_rows)

    def forward_back(step, carry):
        first = pl.ds(pl.multiple_of(step * chunk, chunk), chunk)
        second = pl.ds(pl.multiple_of(hidden_units + step * chunk, chunk), chunk)
        gate_w, up_w, down_w = gate_up[:, first], gate_up[:, second], down[first, :]
        gate, up = mm(x, gate_w), mm(x, up_w)
        sig = 1.0 / (1.0 + jnp.exp(-gate))
        silu = gate * sig
        act = (silu * up).astype(BF)
        acts[:, first] = act
        grad_act = mm_nt(g, down_w)
        grad_gate = (grad_act * up * sig * (1.0 + gate * (1.0 - sig))).astype(BF)
        grad_up = (grad_act * silu).astype(BF)
        grad_units[:, first] = grad_gate
        grad_units[:, second] = grad_up
        out_rows[...] += mm(act, down_w)
        back_rows[...] += mm_nt(grad_gate, gate_w) + mm_nt(grad_up, up_w)
        return carry

    lax.fori_loop(0, hidden_units // chunk, forward_back, 0)
    index = 0
    for ref in own_out + other_out:
        for base in range(0, ref.shape[0], 2 * MOST):
            source = slice(index * MOST, (index + 1) * MOST)
            ref[base : base + MOST, :] = out_rows[source, :].astype(ref.dtype)
            ref[base + MOST : base + 2 * MOST, :] = back_rows[source, :].astype(ref.dtype)
            index += 1
    if not packed:
        grad_gate_up[...] = mm_tn(x, grad_units[...]).astype(BF)
        grad_down[...] = mm_tn(acts[...], g).astype(BF)
        return
    part = width // 4

    def weight_grad(step, carry):
        block = pl.ds(pl.multiple_of(step * 512, 512), 512)
        gate_up[:, block] = mm_tn(x, grad_units[:, block]).astype(BF)
        return carry

    lax.fori_loop(0, 4, weight_grad, 0)
    for slot, ref in enumerate(messages):
        source = pl.ds(pl.multiple_of(where[slot] * part, part), part)
        for block in range(8):
            ref[block * part : (block + 1) * part, :] = gate_up[
                source, block * 256 : (block + 1) * 256
            ]
        mine = acts[:, pl.ds(pl.multiple_of(where[slot] * 256, 256), 256)]
        of_down = mm_tn(mine, g).astype(BF)
        for block in range(3):
            base = 8 * part + block * 256
            ref[base : base + 256, :] = of_down[:, block * 256 : (block + 1) * 256]


def combine_kernel(where, *refs, groups, columns, shard_rows, packed):
    backs = refs[:groups]
    (hidden_ref, low_ref, cot, routes, resid, small, small_t, out_weight, att,
     out_ref, grad_hidden_ref, grad_att_ref, grad_away, grad_kept, grad_resid,
     rows_y, rows_d, sums) = refs[groups:]
    kinds, mix_at, value_at, gain_two_at, square_at = columns
    for slot in range(groups):
        target = pl.ds(pl.multiple_of(where[slot] * MOST, MOST), MOST)
        rows_y[target, :] = backs[slot][:MOST, :]
        rows_d[target, :] = backs[slot][MOST:, :]
    hidden, low = hidden_ref[...], low_ref[...]
    count = low.shape[0]
    normed_input = low.astype(F32)
    grad_low_type = cot[...]
    grad = grad_low_type.astype(F32)
    logits = mm(low, small[...])
    grad_small_dot = mm(grad_low_type, small[...])
    route = routes[...]
    gates, hot, dispatch = routing(route, resid[...].astype(F32), logits, groups)
    returned = [mm(dispatch[c], rows_y[...]) for c in range(2)]
    grad_back = mm(dispatch[0] + dispatch[1], rows_d[...])
    grad_dot = jnp.sum(grad * normed_input, axis=-1, keepdims=True)
    is_copy = [(route[:, c : c + 1] == groups + 1).astype(F32) for c in range(2)]
    grad_gates = [
        jnp.sum(grad * returned[c], axis=-1, keepdims=True) + is_copy[c] * grad_dot
        for c in range(2)
    ]
    direct = gates[0] * is_copy[0] + gates[1] * is_copy[1]
    mixture = gates[0] * returned[0] + gates[1] * returned[1]
    lane = lanes((count, SMALL))
    grad_logits = jnp.zeros((count, SMALL), F32)
    value_weights = jnp.zeros((count, SMALL), F32)
    for const in range(NCONST):
        first = logits[:, mix_at + 2 * const : mix_at + 2 * const + 1]
        second = logits[:, mix_at + 2 * const + 1 : mix_at + 2 * const + 2]
        top = jnp.maximum(first, second)
        first, second = jnp.exp(first - top), jnp.exp(second - top)
        mix = [first / (first + second), second / (first + second)]
        value_dot = grad_small_dot[:, value_at + const : value_at + const + 1]
        named = [(route[:, c : c + 1] == groups + 2 + const).astype(F32) for c in range(2)]
        for c in range(2):
            grad_gates[c] += named[c] * (mix[0] * grad_dot + mix[1] * value_dot)
        weight = gates[0] * named[0] + gates[1] * named[1]
        direct += weight * mix[0]
        of_value = weight * mix[1]
        mixture += of_value * small_t[value_at + const : value_at + const + 1, :]
        value_weights = jnp.where(lane == value_at + const, of_value, value_weights)
        grad_mix = [weight * grad_dot, weight * value_dot]
        common = mix[0] * grad_mix[0] + mix[1] * grad_mix[1]
        for c in range(2):
            grad_logits = jnp.where(
                lane == mix_at + 2 * const + c, mix[c] * (grad_mix[c] - common), grad_logits
            )
    outputs = hidden + mixture + direct * normed_input
    out_ref[...] = outputs.astype(BF)
    common = gates[0] * grad_gates[0] + gates[1] * grad_gates[1]
    for c in range(2):
        grad_logits = jnp.where(hot[c], gates[c] * (grad_gates[c] - common), grad_logits)
    grad_resid[...] = grad_logits[:, :kinds].astype(BF)
    high, rest = split_low(grad_logits)
    weights = small[...]
    grad_low = grad_back + direct * grad + mm_nt(high, weights) + mm_nt(rest, weights)
    scale = rms_scale(hidden)
    normed = hidden * scale
    of_gain = split_low(grad_low * normed)
    ones = (lane == gain_two_at).astype(BF)
    value_high, value_rest = split_low(value_weights)
    summed = (
        mm_tn(low, high)
        + mm_tn(low, rest)
        + mm_tn(grad_low_type, value_high)
        + mm_tn(grad_low_type, value_rest)
        + mm_tn(of_gain[0], ones)
        + mm_tn(of_gain[1], ones)
    )
    column, row = lanes(summed.shape), rows_of(summed.shape)
    mine = row // shard_rows == where[groups]
    for index, total in enumerate((jnp.sum(hidden * hidden), jnp.sum(outputs * outputs))):
        for part, value in enumerate(split_low(jnp.full((1, 1), total, F32))):
            spot = jnp.logical_and(mine, column == square_at + 2 * index + part)
            summed = jnp.where(spot, value.astype(F32), summed)
    grad_normed = grad_low * small_t[gain_two_at : gain_two_at + 1, :]
    grad_hidden = grad + scale * (
        grad_normed - normed * jnp.mean(grad_normed * normed, axis=-1, keepdims=True)
    )
    grad_hidden_ref[...] = grad_hidden
    branch = grad_hidden.astype(BF)
    grad_att_ref[...] = mm_nt(branch, out_weight[...]).astype(BF)
    width = branch.shape[1]
    sums[:, :width] = mm_tn(att[...], branch)
    sums[:, width:] = summed
    if packed:
        split_rows(where, groups + 1, sums, grad_away, grad_kept)
    else:
        grad_kept[...] = sums[...].astype(BF)
        grad_away[...] = jnp.zeros_like(grad_away)


def project_back_kernel(where, *refs, slots):
    queries, keys, values = refs[0:2], refs[2:4], refs[4:6]
    weight, rows_back, own_back = refs[6:]
    rank = where[pl.program_id(0)]
    own = where[slots]
    half = keys[0].shape[1]
    width = 2 * half

    def through(parts, base):
        result = mm_nt(parts[0][...], weight[:, base : base + half])
        return result + mm_nt(parts[1][...], weight[:, base + half : base + width])

    @pl.when(rank > own)
    def _():
        rows_back[...] = jnp.zeros_like(rows_back)

    @pl.when(rank <= own)
    def _():
        rows_back[...] = (through(keys, width) + through(values, 2 * width)).astype(BF)

        @pl.when(rank == own)
        def _():
            own_back[...] = through(queries, 0)


def finish_kernel(where, tok, small_t, grad_hidden, own_back, rows_back, out, *, gain_at):
    x = tok[...].astype(F32)
    scale = rms_scale(x)
    normed = x * scale
    grad = (own_back[...] + rows_back[...]) * small_t[gain_at : gain_at + 1, :]
    out[...] = (
        grad_hidden[...]
        + scale * (grad - normed * jnp.mean(grad * normed, axis=-1, keepdims=True))
    ).astype(BF)


def shared_kernel(where, total, other, weight, gain, qkv, out, router, gate, value, gain_one, gain_two, stream, room, *, columns, width, entries, packed):
    kinds, mix_at, value_at, gain_two_at, square_at = columns
    if packed:
        rows = room.shape[0] // 4
        for parts, rank in ((total, where[0]), (other, where[0] ^ 1)):
            both = parts[...].astype(F32)
            room[pl.ds(pl.multiple_of(rank * rows, 8), rows), :] = both[:rows]
            room[pl.ds(pl.multiple_of((rank ^ 2) * rows, 8), rows), :] = both[rows:]
    else:
        room[...] = total[...].astype(F32)
    values = room[...]
    half = width // 2
    for part in range(3):
        for side in range(2):
            at = (3 * side + part) * half
            to = part * width + side * half
            qkv[:, to : to + half] = values[:, at : at + half]
    out[...] = values[:, 3 * width : 4 * width]
    rows = values.shape[0]

    def as_columns(block):
        spare = jnp.zeros((SMALL - rows, SMALL), F32)
        return jnp.concatenate([block, spare], axis=0).T[:, :rows]

    small = values[:, 4 * width :]
    turned_small = as_columns(small)
    router[...] = turned_small[:kinds]
    gate[...] = turned_small[mix_at : mix_at + 2 * NCONST]
    value[...] = turned_small[value_at : value_at + NCONST]
    gain_two[...] = turned_small[gain_two_at : gain_two_at + 1]
    of_gain = jnp.sum(qkv[...] * weight[...].astype(F32), axis=-1, keepdims=True)
    gain_one[...] = as_columns(jnp.broadcast_to(of_gain, (rows, SMALL)))[:1] / gain[...].astype(F32)
    squares = small[:1, square_at : square_at + 4]
    hidden = squares[:, 0:1] + squares[:, 1:2]
    outputs = squares[:, 2:3] + squares[:, 3:4]
    stream[...] = jnp.sqrt(jnp.where(lanes((1, 2)) == 0, hidden, outputs) / entries)


def on_device(
    tokens,
    gain_one,
    qkv_weight,
    out_weight,
    gain_two,
    router_weight,
    const_gate,
    const_value,
    expert_gate_up,
    expert_down,
    gate_residual,
    routes,
    cotangent,
):
    parts = lax.axis_size("fsdp")
    groups = lax.axis_size("expert")
    me_fsdp = lax.axis_index("fsdp").astype(jnp.int32)
    me_expert = lax.axis_index("expert").astype(jnp.int32)
    minor, major, core = me_fsdp % 2, me_fsdp // 2, me_expert % 2
    packed = parts == 8 and groups == 4
    major_count = parts // 2
    tok = tokens[0]
    count, width = tok.shape
    length = groups * count
    pairs = width // PAIR
    kinds = router_weight.shape[1]
    mix_at, value_at = kinds, kinds + 2 * NCONST
    gain_one_at = value_at + NCONST
    gain_two_at = gain_one_at + 1
    square_at = gain_two_at + 1
    shard_rows = width // parts
    unit = FF // parts
    units = FF // 2
    fixed = lambda j, w: (0, 0)
    at_slot = lambda j, w: (j, 0)
    at_rank = lambda j, w: (w[j], 0)
    just_minor = jnp.stack([minor])

    small_rows = jnp.concatenate(
        [router_weight.T, const_gate.T, const_value.T, gain_one[None], gain_two[None]], axis=0
    )
    small_rows = jnp.pad(
        small_rows, ((0, 32 - small_rows.shape[0]), (0, SMALL - small_rows.shape[1]))
    )
    frequency = 10000.0 ** (-jnp.arange(HEAD // 2, dtype=F32) / (HEAD // 2))
    angles = jnp.arange(length, dtype=F32)[:, None] * frequency[None, :]
    cosine, sine = jnp.cos(angles), jnp.sin(angles)
    cosine = jnp.concatenate([cosine, cosine, cosine, cosine], axis=1)
    sine = jnp.concatenate([-sine, sine, -sine, sine], axis=1)

    weight_args, order, across = (), [], None
    if packed:
        shared = shared_pack(qkv_weight, out_weight, small_rows)
        across = swap(tok, "expert", 2)
        tok_a, tok_b, ranks = sequence_gather(tok, across)
        away = call(
            blocks_kernel,
            shaped((8 * shard_rows, 256), BF),
            (just_minor, expert_gate_up[0]),
            name="blocks",
            micros=1,
        )
        arrived = swap(away, "fsdp", 1)
        part = call(
            pack_kernel,
            shaped((16 * shard_rows, 256), BF),
            (just_minor, expert_gate_up[0], arrived),
            name="pack_expert",
            micros=1,
        )
        down = expert_down[0]
        own_half, other_half, order, down_near, down_far = shared_gather(
            shared, down, (across, arrived), (part, tok_b, cosine, sine)
        )
        down_onward = along(down_far, OUTWARD)
        down_middle = along(after(down, down_far), MIDDLE)
        weight_args = (own_half, other_half)
        far, near = along(part, FAR), along(part, NEAR)
    else:
        qkv_full = lax.all_gather(qkv_weight, "fsdp", axis=0, tiled=True)
        out_full = lax.all_gather(out_weight, "fsdp", axis=0, tiled=True)
        small = lax.all_gather(small_rows[:, :shard_rows], "fsdp", axis=1, tiled=True).T
        small = jnp.pad(small, ((0, 0), (0, SMALL - 32)))
        small_t = small.astype(F32).T[:32]
        weight_args = (qkv_full, small_t)
        halves = expert_gate_up[0].reshape(shard_rows, 2, major_count, 2, unit)
        away = lax.dynamic_index_in_dim(halves, 1 - minor, 3, False).reshape(shard_rows, FF)
        kept = lax.dynamic_index_in_dim(halves, minor, 3, False).reshape(shard_rows, FF)
        arrived = swap(away, "fsdp", 1)
        part = jnp.concatenate(
            [jnp.where(minor == 0, kept, arrived), jnp.where(minor == 0, arrived, kept)], axis=0
        )
        gather = functools.partial(
            lax.all_gather,
            axis_name="fsdp",
            axis=0,
            tiled=True,
            axis_index_groups=minor_groups(major_count),
        )
        gate_up_half, down_half = gather(part), gather(expert_down[0])
        tok_a, tok_b, ranks = sequence_gather(tok, across)
    where = jnp.stack(
        [jnp.asarray(r, jnp.int32) for r in ranks] + [me_expert] + order + [core]
    )

    half_columns = 2 * width + SMALL
    outs = [
        shaped((count, width), BF),
        shaped((length, width), BF),
        shaped((length, width), BF),
        shaped((width, length), BF),
    ]
    out_specs = [
        pl.BlockSpec((count, width), fixed),
        pl.BlockSpec((count, width), at_rank),
        pl.BlockSpec((count, width), at_rank),
        pl.BlockSpec((width, count), lambda j, w: (0, w[j])),
    ]
    if packed:
        weight_specs = [pl.BlockSpec((width, half_columns), fixed)] * 2
        outs += [
            shaped((width, 3 * width), BF),
            shaped((width, width), BF),
            shaped((width, SMALL), BF),
            shaped((32, width), F32),
        ]
        out_specs += [pl.BlockSpec(o.shape, fixed) for o in outs[4:]]
    else:
        weight_specs = [pl.BlockSpec((width, 3 * width), fixed), pl.BlockSpec((32, width), fixed)]
    projected = call(
        functools.partial(project_kernel, slots=groups, gain_at=gain_one_at, placed=not packed),
        outs,
        (where, tok_a, tok_b, cosine, sine) + weight_args,
        grid=(groups,),
        in_specs=[
            pl.BlockSpec((count, width), lambda j, w: (jnp.minimum(j, groups // 2 - 1), 0)),
            pl.BlockSpec((count, width), lambda j, w: (jnp.maximum(j - groups // 2, 0), 0)),
            pl.BlockSpec((count, PAIR), at_rank),
            pl.BlockSpec((count, PAIR), at_rank),
        ]
        + weight_specs,
        out_specs=out_specs,
        name="project",
        micros=10,
    )
    q, k_all, v_all, normed = projected[:4]
    if packed:
        qkv_full, out_full, small, small_t = projected[4:]
    head_rows = pl.BlockSpec((count, PAIR), lambda h, w: (0, h))
    head_keys = pl.BlockSpec((length, PAIR), lambda h, w: (0, h))
    head_log = pl.BlockSpec((1, 8, 2 * count), lambda h, w: (h, 0, 0))
    attended, log_total = call(
        functools.partial(attend_kernel, slots=groups),
        [shaped((count, width), BF), shaped((pairs, 8, 2 * count), F32)],
        (where, q, k_all, v_all),
        grid=(pairs,),
        in_specs=[head_rows, head_keys, head_keys],
        out_specs=[head_rows, head_log],
        name="attend",
        micros=12,
    )

    residual, route, cot = gate_residual[0], routes[0], cotangent[0]
    if packed:
        attended = after(attended, down_onward, down_middle)
    owners = [me_fsdp ^ (2 * j + i) for i in (0, 1) for j in range(4)]
    owners += [core, me_expert // 2]
    slots = jnp.stack([me_expert ^ j for j in range(groups)] + [me_fsdp] + owners)
    block = shaped((2 * MOST, width), BF)
    hidden, low_two, *sends = call(
        functools.partial(route_kernel, groups=groups, gain_at=gain_two_at),
        [shaped((count, width), F32), shaped((count, width), BF)] + [block] * groups,
        (slots, attended, out_full, tok, small, small_t, residual, route, cot),
        scratch=[pltpu.VMEM((groups * MOST, width), BF)] * 2,
        name="route",
        micros=5,
    )
    received, other_low, other_high = exchange(sends)
    if packed:
        far, near = lax.optimization_barrier((far, near, low_two))[:2]
        onward = along(far, OUTWARD)
        middle = along(after(part, far), MIDDLE)
        inner = jnp.logical_or(major == 1, major == 2).astype(jnp.int32)
        places = jnp.stack([major, major ^ 1, major ^ 2, major ^ 3, inner])
        weights = (part, near, far, middle, onward)
        weights += (down, down_near, down_far, down_middle, down_onward)
        grads = [shaped((part.shape[0] + 3 * 256, 256), BF)] * 4
        room = [pltpu.VMEM((width, 2 * units), BF), pltpu.VMEM((units, width), BF)]
    else:
        places = just_minor
        weights = (gate_up_half, down_half)
        grads = [shaped((width, 2 * units), BF), shaped((units, width), BF)]
        room = []
    rows_total = 2 * groups * MOST
    results = call(
        functools.partial(expert_kernel, groups=groups, hidden_units=units, packed=packed),
        [shaped((groups * MOST, width), F32)] * 2 + [shaped((groups * MOST, width), BF)] * 2 + grads,
        (places,) + tuple(received) + (other_low, other_high) + weights,
        scratch=[pltpu.VMEM((rows_total, width), BF)] * 2
        + [pltpu.VMEM((rows_total, width), F32)] * 2
        + [pltpu.VMEM((rows_total, units), BF), pltpu.VMEM((rows_total, 2 * units), BF)]
        + room,
        name="expert",
        micros=18,
    )
    own_low, own_high, part_low, part_high = results[:4]
    grads = results[4:]
    high = (own_high + swap(part_high, "fsdp", 1).astype(F32)).astype(BF)
    low = (own_low + swap(part_low, "fsdp", 1).astype(F32)).astype(BF)
    backs = exchange_back(low, high, groups)

    if packed:
        first = along(grads[3], INWARD)
        middle = along(grads[3], MIDDLE)
        sent = added(grads[2], first)
        near = along(after(grads[1], first), NEAR)
        cuts = (0, 8 * shard_rows, 14 * shard_rows, sent.shape[0])
        far = [along(sent[a:b], FAR) for a, b in zip(cuts, cuts[1:])]
        backs[0] = after(backs[0], sent, middle)
    else:
        scatter = lambda v: lax.psum_scatter(
            v,
            "fsdp",
            scatter_dimension=0,
            tiled=True,
            axis_index_groups=minor_groups(major_count),
        ).astype(F32)
        shard_down = scatter(grads[1])
        part = scatter(grads[0]).reshape(2, shard_rows, FF)
        away = lax.dynamic_index_in_dim(part, 1 - minor, 0, False).astype(BF)
        kept = lax.dynamic_index_in_dim(part, minor, 0, False)
        arrived = swap(away, "fsdp", 1).astype(F32)
        first = jnp.where(minor == 0, kept, arrived).reshape(shard_rows, 2, major_count, 1, unit)
        second = jnp.where(minor == 0, arrived, kept).reshape(shard_rows, 2, major_count, 1, unit)
        shard_gate_up = jnp.concatenate([first, second], axis=3).reshape(shard_rows, 2 * FF)

    columns = (kinds, mix_at, value_at, gain_two_at, square_at)
    part_rows = width // 2 if packed else width
    out_part = shaped((part_rows, width + SMALL), BF)
    outputs, grad_hidden, grad_att, out_away, out_kept, grad_residual = call(
        functools.partial(
            combine_kernel, groups=groups, columns=columns, shard_rows=shard_rows, packed=packed
        ),
        [
            shaped((count, width), BF),
            shaped((count, width), F32),
            shaped((count, width), BF),
            out_part,
            out_part,
            shaped((count, kinds), BF),
        ],
        (slots,) + tuple(backs)
        + (hidden, low_two, cot, route, residual, small, small_t, out_full, attended),
        scratch=[pltpu.VMEM((groups * MOST, width), BF)] * 2
        + [pltpu.VMEM((width, width + SMALL), F32)],
        name="combine",
        micros=10,
    )
    head_half = pairs // 2
    back_where = jnp.stack([jnp.asarray(r, jnp.int32) for r in ranks] + [me_expert] + owners)

    def attend_back(part, grad_rows):
        base = part * head_half
        from_rows = pl.BlockSpec((count, PAIR), lambda h, w: (0, base + h))
        from_keys = pl.BlockSpec((length, PAIR), lambda h, w: (0, base + h))
        to_rows = pl.BlockSpec((count, PAIR), lambda h, w: (0, h))
        to_keys = pl.BlockSpec((length, PAIR), lambda h, w: (0, h))
        grads_part = shaped((part_rows, 3 * width // 2), BF)
        return call(
            functools.partial(attend_back_kernel, slots=groups, packed=packed),
            [
                shaped((count, width // 2), BF),
                shaped((length, width // 2), BF),
                shaped((length, width // 2), BF),
                grads_part,
                grads_part,
            ],
            (back_where, q, k_all, v_all, grad_rows, log_total, cosine, sine, normed, normed),
            grid=(head_half,),
            in_specs=[
                from_rows,
                from_keys,
                from_keys,
                from_rows,
                pl.BlockSpec((1, 8, 2 * count), lambda h, w: (base + h, 0, 0)),
                pl.BlockSpec((length, PAIR), fixed),
                pl.BlockSpec((length, PAIR), fixed),
                pl.BlockSpec((width, length), fixed),
                pl.BlockSpec((width, count), lambda h, w: (0, w[groups])),
            ],
            out_specs=[
                to_rows,
                to_keys,
                to_keys,
                pl.BlockSpec(grads_part.shape, fixed),
                pl.BlockSpec(grads_part.shape, fixed),
            ],
            scratch=[pltpu.VMEM((width, 3 * width // 2), F32)],
            name="attend_back",
            micros=11,
        )

    dq_a, dk_a, dv_a, a_away, a_kept = attend_back(0, grad_att)
    if packed:
        a_away, a_kept, out_kept = lax.optimization_barrier(
            (a_away, a_kept, out_kept, far[0], near)
        )[:3]
        out_both = added(out_kept, swap(out_away, "expert", 1))
        a_both = added(a_kept, swap(a_away, "expert", 1))
        grad_att = after(grad_att, a_both, out_both)
    dq_b, dk_b, dv_b, b_away, b_kept = attend_back(1, grad_att)
    def project_back(dq_late):
        half_rows = pl.BlockSpec((count, width // 2), fixed)
        half_keys = pl.BlockSpec((count, width // 2), at_rank)
        return call(
            functools.partial(project_back_kernel, slots=groups),
            [shaped((length, width), BF), shaped((count, width), F32)],
            (back_where, dq_a, dq_late, dk_a, dk_b, dv_a, dv_b, qkv_full),
            grid=(groups,),
            in_specs=[half_rows] * 2 + [half_keys] * 4 + [pl.BlockSpec((width, 3 * width), fixed)],
            out_specs=[pl.BlockSpec((count, width), at_rank), pl.BlockSpec((count, width), fixed)],
            name="project_back",
            micros=6,
        )

    if packed:
        b_away = after(b_away, far[1])
        out_sum, a_sum = along_chips(out_both, (b_kept,)), along_chips(a_both, (b_kept,))
        b_both = added(b_kept, swap(b_away, "expert", 1))
        dq_b = after(dq_b, b_both)
        b_sum = along_chips(b_both, ())
        parts_all = jnp.concatenate([a_sum, b_sum, out_sum], axis=1)
        rows_back, own_back = project_back(dq_b)
        total, piece = across_major(after(parts_all, rows_back), shard_rows // 4)
        own_grads = after(grads[0], piece)
        away, kept, shard_down = call(
            sum_parts_kernel,
            [
                shaped((8 * shard_rows, 256), BF),
                shaped((8 * shard_rows, 256), F32),
                shaped((256, width), F32),
            ],
            (just_minor, own_grads, near, middle) + tuple(far),
            name="sum_parts",
            micros=3,
        )
        shard_gate_up = call(
            unpack_kernel,
            shaped((shard_rows, 2 * FF), F32),
            (just_minor, kept, swap(away, "fsdp", 1)),
            name="unpack_expert",
            micros=2,
        )
    else:
        both = jnp.concatenate([a_kept, b_kept, out_kept], axis=1)
        both = lax.psum_scatter(both, "fsdp", scatter_dimension=0, tiled=True)
        total = lax.psum(both, "expert")
        other = total
        rows_back, own_back = project_back(dq_b)
    rows_sum = sequence_scatter_sum(rows_back, count)
    grad_tokens = call(
        functools.partial(finish_kernel, gain_at=gain_one_at),
        shaped((count, width), BF),
        (just_minor, tok, small_t, grad_hidden, own_back, rows_sum),
        name="finish",
        micros=3,
    )

    if packed:
        total = after(total, grad_tokens, shard_gate_up)
        total = jnp.concatenate([total, swap(total, "expert", 2)], axis=0)
        other = swap(total, "expert", 1)
    shared_grads = call(
        functools.partial(
            shared_kernel, columns=columns, width=width, entries=length * width, packed=packed
        ),
        [
            shaped((shard_rows, 3 * width), F32),
            shaped((shard_rows, width), F32),
            shaped((kinds, shard_rows), F32),
            shaped((2 * NCONST, shard_rows), F32),
            shaped((NCONST, shard_rows), F32),
            shaped((1, shard_rows), F32),
            shaped((1, shard_rows), F32),
            shaped((1, 2), F32),
        ],
        (jnp.stack([me_expert]), total, other, qkv_weight, gain_one[None]),
        scratch=[pltpu.VMEM((shard_rows, 4 * width + SMALL), F32)],
        name="shared_grads",
        micros=3,
    )
    grad_qkv, grad_out, grad_router, grad_gate, grad_value, grad_one, grad_two, stream = shared_grads
    return (
        outputs[None],
        grad_tokens[None],
        grad_one[0],
        grad_qkv,
        grad_out,
        grad_two[0],
        grad_router.T,
        grad_gate.T,
        grad_value.T,
        shard_gate_up[None],
        shard_down[None],
        grad_residual[None],
        stream,
    )


def solution(mesh):
    return jax.shard_map(
        on_device,
        mesh=mesh,
        in_specs=(
            P("fsdp", "expert", None),
            P("fsdp"),
            P("fsdp", None),
            P("fsdp", None),
            P("fsdp"),
            P("fsdp", None),
            P("fsdp", None),
            P("fsdp", None),
            P("expert", "fsdp", None),
            P("expert", "fsdp", None),
            P("fsdp", "expert", None),
            P("fsdp", "expert", None),
            P("fsdp", "expert", None),
        ),
        out_specs=(
            P("fsdp", "expert", None),
            P("fsdp", "expert", None),
            P("fsdp"),
            P("fsdp", None),
            P("fsdp", None),
            P("fsdp"),
            P("fsdp", None),
            P("fsdp", None),
            P("fsdp", None),
            P("expert", "fsdp", None),
            P("expert", "fsdp", None),
            P("fsdp", "expert", None),
            P("fsdp", None),
        ),
        check_vma=False,
    )
```

profile of v0, /device:TPU:0, one launch (start us, length us, event | category | flops | bytes accessed | tf_op | source)
XLA Modules:
  0.0 299.9 jit_solution(5398728496830749010)
XLA Ops:
  20.5 4.8 %collective-permute-done.2 = bf16[96,1664]{1,0:T(8,128)(2,1)S(1)} collective-permute-done((bf16[96,1664]{1,0:T(8,128)(2,1)}, bf16[96,1664]{1,0:T(8,128)(2,1)S(1)}, u32[]{:S(2)}, u32[]{:S(2)}) %collective-permute-start.2) | collective-permute-done | bytes 319520 | tf_op jit(solution)/shard_map/ppermute | solution.py:93
  26.8 5.8 %collective-permute-done.3 = bf16[96,1664]{1,0:T(8,128)(2,1)S(1)} collective-permute-done((bf16[96,1664]{1,0:T(8,128)(2,1)}, bf16[96,1664]{1,0:T(8,128)(2,1)S(1)}, u32[]{:S(2)}, u32[]{:S(2)}) %collective-permute-start.3) | collective-permute-done | bytes 319520 | tf_op jit(solution)/shard_map/ppermute | solution.py:93
  36.3 4.5 %collective-permute-start.11 = (bf16[256,768]{1,0:T(8,128)(2,1)S(1)}, bf16[256,768]{1,0:T(8,128)(2,1)}, u32[]{:S(2)}, u32[]{:S(2)}) collective-permute-start(bf16[256,768]{1,0:T(8,128)(2,1)S(1)} %bitcast.55), channel_id=1, source_target_pairs={{0,4},{1,5},{4,0},{5,1},{2,6},{3,7},{6,2},{7,3},{8,12},{9,13},{12,... | collective-permute-start | bytes 1179656 | tf_op jit(solution)/shard_map/ppermute | solution.py:97
  44.4 7.1 %collective-permute-done.9 = bf16[96,1664]{1,0:T(8,128)(2,1)S(1)} collective-permute-done((bf16[96,1664]{1,0:T(8,128)(2,1)S(1)}, bf16[96,1664]{1,0:T(8,128)(2,1)S(1)}, u32[]{:S(2)}, u32[]{:S(2)}) %collective-permute-start.9) | collective-permute-done | bytes 319520 | tf_op jit(solution)/shard_map/ppermute | solution.py:93
  52.3 6.4 %collective-permute-done.11.refs_13_ = bf16[256,768]{1,0:T(8,128)(2,1)} collective-permute-done((bf16[256,768]{1,0:T(8,128)(2,1)S(1)}, bf16[256,768]{1,0:T(8,128)(2,1)}, u32[]{:S(2)}, u32[]{:S(2)}) %collective-permute-start.11) | collective-permute-done | bytes 393248 | tf_op jit(solution)/shard_map/ppermute | solution.py:97
  65.2 3.4 %collective-permute-start.21 = (bf16[1536,256]{1,0:T(8,128)(2,1)S(1)}, bf16[1536,256]{1,0:T(8,128)(2,1)S(1)}, u32[]{:S(2)}, u32[]{:S(2)}) collective-permute-start(bf16[1536,256]{1,0:T(8,128)(2,1)S(1)} %copy-done.2), channel_id=1, source_target_pairs={{0,2},{1,3},{2,0},{3,1},{4,6},{5,7},{6,4},{7,5},{8,10},{9,11},{10,... | collective-permute-start | bytes 2359304 | tf_op jit(solution)/shard_map/ppermute | solution.py:97
  68.5 11.1 %project.1 = (bf16[256,768]{1,0:T(8,128)(2,1)}, bf16[1024,768]{1,0:T(8,128)(2,1)}, bf16[1024,768]{1,0:T(8,128)(2,1)}, bf16[768,1024]{1,0:T(8,128)(2,1)}, bf16[76...) custom-call(s32[14]{0:T(128)} %stack.129.where, ...), custom_call_target="tpu_custom_call" | custom-call | flops 900000000 | bytes 3000000 | tf_op jit(solution)/shard_map/project/pallas_call | solution.py:69
  79.6 12.3 %attend.1 = (bf16[256,768]{1,0:T(8,128)(2,1)}, f32[6,8,512]{2,1,0:T(8,128)}) custom-call(s32[14]{0:T(128)} %stack.129.where, bf16[256,768]{1,0:T(8,128)(2,1)} %get-tuple-element.97.q, bf16[1024,768]{1,0:T(8,128)(2,1)} %get-tuple-element.98.k, bf16[1024,768]{1,0:T(8,128)(2,1)} %get-tuple-element.99.v), custom_call_target="tpu_custom_call" | custom-call | flops 1080000000 | bytes 3600000 | tf_op jit(solution)/shard_map/attend/pallas_call | solution.py:69
  91.9 4.9 %route.1 = (f32[256,768]{1,0:T(8,128)}, bf16[256,768]{1,0:T(8,128)(2,1)}, bf16[160,768]{1,0:T(8,128)(2,1)}, bf16[160,768]{1,0:T(8,128)(2,1)}, bf16[160,768]{1,0:T(8,128)(2,1)}, /*index=5*/bf16[160,768]{1,0:T(8,128)(2,1)}) custom-call(s32[15]{0:T(128)} %stack.121.where, bf16[256,768]{1,0:T(8,128)(2,1)} %get-tuple-element.102.att.refs_12_, ...), custom_call_target="tpu_custom_call" | custom-call | flops 450000000 | bytes 1500000 | tf_op jit(solution)/shard_map/route/pallas_call | solution.py:69
  103.1 5.3 %collective-permute-done.21.refs_7_ = bf16[1536,256]{1,0:T(8,128)(2,1)S(1)} collective-permute-done((bf16[1536,256]{1,0:T(8,128)(2,1)S(1)}, bf16[1536,256]{1,0:T(8,128)(2,1)S(1)}, u32[]{:S(2)}, u32[]{:S(2)}) %collective-permute-start.21) | collective-permute-done | bytes 786464 | tf_op jit(solution)/shard_map/ppermute | solution.py:97
  117.0 14.3 %collective-permute-done.23.refs_10_ = bf16[1536,256]{1,0:T(8,128)(2,1)} collective-permute-done((bf16[1536,256]{1,0:T(8,128)(2,1)S(1)}, bf16[1536,256]{1,0:T(8,128)(2,1)}, u32[]{:S(2)}, u32[]{:S(2)}) %collective-permute-start.23) | collective-permute-done | bytes 786464 | tf_op jit(solution)/shard_map/ppermute | solution.py:97
  131.3 19.4 %expert.1 = (f32[320,768]{1,0:T(8,128)}, f32[320,768]{1,0:T(8,128)}, bf16[320,768]{1,0:T(8,128)(2,1)}, bf16[320,768]{1,0:T(8,128)(2,1)}, bf16[2304,256]{1,0:T(8,...) custom-call(s32[5]{0:T(128)} %stack.128.where, ...), custom_call_target="tpu_custom_call" | custom-call | flops 1620000000 | bytes 5400000 | tf_op jit(solution)/shard_map/expert/pallas_call | solution.py:69
  155.3 9.8 %collective-permute-done.27 = bf16[320,768]{1,0:T(8,128)(2,1)S(1)} collective-permute-done((bf16[320,768]{1,0:T(8,128)(2,1)}, bf16[320,768]{1,0:T(8,128)(2,1)S(1)}, u32[]{:S(2)}, u32[]{:S(2)}) %collective-permute-start.27) | collective-permute-done | bytes 491552 | tf_op jit(solution)/shard_map/ppermute | solution.py:93
  168.0 5.6 %collective-permute-done.24 = bf16[320,768]{1,0:T(8,128)(2,1)S(1)} collective-permute-done((bf16[320,768]{1,0:T(8,128)(2,1)}, bf16[320,768]{1,0:T(8,128)(2,1)S(1)}, u32[]{:S(2)}, u32[]{:S(2)}) %collective-permute-start.24) | collective-permute-done | bytes 491552 | tf_op jit(solution)/shard_map/ppermute | solution.py:93
  185.1 9.9 %combine.1 = (bf16[256,768]{1,0:T(8,128)(2,1)}, f32[256,768]{1,0:T(8,128)}, bf16[256,768]{1,0:T(8,128)(2,1)}, bf16[384,896]{1,0:T(8,128)(2,1)}, bf16[384,896]{1,0:T(8,128)(2,1)}, /*index=5*/bf16[256,8]{1,0:T(8,128)(2,1)}) custom-call(s32[15]{0:T(128)} %stack.121.where, bf16[160,768]{1,0:T(8,128)(2,1)} %get-tuple-element.119.refs_0_, ...), custom_call_target="tpu_custom_call" | custom-call | flops 900000000 | bytes 3000000 | tf_op jit(solution)/shard_map/combine/pallas_call | solution.py:69
  195.7 13.7 %attend_back.2 = (bf16[256,384]{1,0:T(8,128)(2,1)}, bf16[1024,384]{1,0:T(8,128)(2,1)}, bf16[1024,384]{1,0:T(8,128)(2,1)}, bf16[384,1152]{1,0:T(8,128)(2,1)}, bf16[384,1152]{1,0:T(8,128)(2,1)}) custom-call(s32[15]{0:T(128)} %stack.131.where, bf16[256,768]{1,0:T(8,128)(2,1)} %get-tuple-element.97.q, bf16[1024,768]{1,0:T(8,128)(2,1)} %get-tuple-element.98.k, ...), custom_call_target="tpu_custom_call" | custom-call | flops 990000000 | bytes 3300000 | tf_op jit(solution)/shard_map/attend_back/pallas_call | solution.py:69
  209.4 5.0 %collective-permute-done.30.d0 = bf16[768,256]{1,0:T(8,128)(2,1)S(1)} collective-permute-done((bf16[768,256]{1,0:T(8,128)(2,1)}, bf16[768,256]{1,0:T(8,128)(2,1)S(1)}, u32[]{:S(2)}, u32[]{:S(2)}) %collective-permute-start.30) | collective-permute-done | bytes 393248 | tf_op jit(solution)/shard_map/ppermute | solution.py:97
  219.5 13.5 %attend_back.3 = (bf16[256,384]{1,0:T(8,128)(2,1)}, bf16[1024,384]{1,0:T(8,128)(2,1)}, bf16[1024,384]{1,0:T(8,128)(2,1)}, bf16[384,1152]{1,0:T(8,128)(2,1)}, bf16[384,1152]{1,0:T(8,128)(2,1)}) custom-call(s32[15]{0:T(128)} %stack.131.where, bf16[256,768]{1,0:T(8,128)(2,1)} %get-tuple-element.97.q, bf16[1024,768]{1,0:T(8,128)(2,1)} %get-tuple-element.98.k, ...), custom_call_target="tpu_custom_call" | custom-call | flops 990000000 | bytes 3300000 | tf_op jit(solution)/shard_map/attend_back/pallas_call | solution.py:69
  241.2 4.0 %collective-permute-done.38 = bf16[192,1152]{1,0:T(8,128)(2,1)S(1)} collective-permute-done((bf16[192,1152]{1,0:T(8,128)(2,1)S(1)}, bf16[192,1152]{1,0:T(8,128)(2,1)S(1)}, u32[]{:S(2)}, u32[]{:S(2)}) %collective-permute-start.38) | collective-permute-done | bytes 442400 | tf_op jit(solution)/shard_map/ppermute | solution.py:93
  248.1 3.7 %collective-permute-done.39 = bf16[96,1152]{1,0:T(8,128)(2,1)S(1)} collective-permute-done((bf16[96,1152]{1,0:T(8,128)(2,1)S(1)}, bf16[96,1152]{1,0:T(8,128)(2,1)S(1)}, u32[]{:S(2)}, u32[]{:S(2)}) %collective-permute-start.39) | collective-permute-done | bytes 221216 | tf_op jit(solution)/shard_map/ppermute | solution.py:93
  251.8 7.7 %project_back.1 = (bf16[1024,768]{1,0:T(8,128)(2,1)}, f32[256,768]{1,0:T(8,128)}) custom-call(s32[15]{0:T(128)} %stack.131.where, bf16[256,384]{1,0:T(8,128)(2,1)} %get-tuple-element.128.refs_0_, bf16[256,384]{1,0:T(8,128)(2,1)} %get-tuple-element.143.refs_1_, bf16[1024,384]{1,0:T(8,128)(2,1)} %get-tuple-element.144.refs_2_, ...), custom_call_target="tpu_custom_call" | custom-call | flops 540000000 | bytes 1800000 | tf_op jit(solution)/shard_map/project_back/pallas_call | solution.py:69
  261.7 4.3 %collective-permute-done.41 = bf16[96,1152]{1,0:T(8,128)(2,1)S(1)} collective-permute-done((bf16[96,1152]{1,0:T(8,128)(2,1)S(1)}, bf16[96,1152]{1,0:T(8,128)(2,1)S(1)}, u32[]{:S(2)}, u32[]{:S(2)}) %collective-permute-start.41) | collective-permute-done | bytes 221216 | tf_op jit(solution)/shard_map/ppermute | solution.py:93
  274.6 3.9 %sum_parts.1 = (bf16[768,256]{1,0:T(8,128)(2,1)}, f32[768,256]{1,0:T(8,128)}, f32[256,768]{1,0:T(8,128)}) custom-call(s32[1]{0:T(128)} %bitcast.25.where, bf16[2304,256]{1,0:T(8,128)(2,1)} %get-tuple-element.155.a, bf16[2304,256]{1,0:T(8,128)(2,1)} %collective-permute-done.31.b, bf16[2304,256]{1,0:T(8,128)(2,1)} %copy-done.5, bf16[768,256]{1,0:T(8,128)(2,1)} %copy-done.21, ...), custom_call_target="tpu_custom_call" | custom-call | flops 270000000 | bytes 900000 | tf_op jit(solution)/shard_map/sum_parts/pallas_call | solution.py:69
  291.5 3.5 %collective-permute-done.49 = bf16[24,3200]{1,0:T(8,128)(2,1)S(1)} collective-permute-done((bf16[24,3200]{1,0:T(8,128)(2,1)S(1)}, bf16[24,3200]{1,0:T(8,128)(2,1)S(1)}, u32[]{:S(2)}, u32[]{:S(2)}) %collective-permute-start.49) | collective-permute-done | bytes 153632 | tf_op jit(solution)/shard_map/ppermute | solution.py:93
  (211 shorter events, 114.9 us)
Async XLA Ops:
  4.6 15.7 %collective-permute-start.4 = (bf16[96,1664]{1,0:T(8,128)(2,1)}, bf16[96,1664]{1,0:T(8,128)(2,1)S(1)}, u32[]{:S(2)}, u32[]{:S(2)}) collective-permute-start(bf16[96,1664]{1,0:T(8,128)(2,1)} %pack_shared.1), channel_id=1, source_target_pairs={{0,1},{1,0},{2,3},{3,2},{4,5},{5,4},{6,7},{7,6},{8,9},{9,8},{10,11... | collective-permute-start | bytes 958472 | tf_op jit(solution)/shard_map/ppermute | solution.py:93
  7.5 25.0 %collective-permute-start.3 = (bf16[96,1664]{1,0:T(8,128)(2,1)}, bf16[96,1664]{1,0:T(8,128)(2,1)S(1)}, u32[]{:S(2)}, u32[]{:S(2)}) collective-permute-start(bf16[96,1664]{1,0:T(8,128)(2,1)} %pack_shared.1), channel_id=1, source_target_pairs={{0,4},{1,5},{2,6},{3,7},{4,0},{5,1},{6,2},{7,3},{8,12},{9,13},{10,... | collective-permute-start | bytes 958472 | tf_op jit(solution)/shard_map/ppermute | solution.py:93
  10.1 15.2 %collective-permute-start.2 = (bf16[96,1664]{1,0:T(8,128)(2,1)}, bf16[96,1664]{1,0:T(8,128)(2,1)S(1)}, u32[]{:S(2)}, u32[]{:S(2)}) collective-permute-start(bf16[96,1664]{1,0:T(8,128)(2,1)} %pack_shared.1), channel_id=1, source_target_pairs={{0,2},{1,3},{2,0},{3,1},{4,6},{5,7},{6,4},{7,5},{8,10},{9,11},{10,... | collective-permute-start | bytes 958472 | tf_op jit(solution)/shard_map/ppermute | solution.py:93
  13.6 19.7 %collective-permute-start.7 = (bf16[768,256]{1,0:T(8,128)(2,1)}, bf16[768,256]{1,0:T(8,128)(2,1)S(1)}, u32[]{:S(2)}, u32[]{:S(2)}) collective-permute-start(bf16[768,256]{1,0:T(8,128)(2,1)} %blocks.1), channel_id=1, source_target_pairs={{0,1},{1,0},{2,3},{3,2},{4,5},{5,4},{6,7},{7,6},{8,9},{9,8},{10,11... | collective-permute-start | bytes 1179656 | tf_op jit(solution)/shard_map/ppermute | solution.py:93
  20.3 16.0 %collective-permute-start.5 = (bf16[96,1664]{1,0:T(8,128)(2,1)S(1)}, bf16[96,1664]{1,0:T(8,128)(2,1)S(1)}, u32[]{:S(2)}, u32[]{:S(2)}) collective-permute-start(bf16[96,1664]{1,0:T(8,128)(2,1)S(1)} %copy-done.4), channel_id=1, source_target_pairs={{0,6},{1,7},{2,4},{3,5},{4,2},{5,3},{6,0},{7,1},{8,14},{9,15},{10,... | collective-permute-start | bytes 958472 | tf_op jit(solution)/shard_map/ppermute | solution.py:93
  25.3 17.0 %collective-permute-start.6 = (bf16[96,1664]{1,0:T(8,128)(2,1)S(1)}, bf16[96,1664]{1,0:T(8,128)(2,1)S(1)}, u32[]{:S(2)}, u32[]{:S(2)}) collective-permute-start(bf16[96,1664]{1,0:T(8,128)(2,1)S(1)} %collective-permute-done.2), channel_id=1, source_target_pairs={{0,1},{1,0},{2,3},{3,2},{4,5},{5,4},{6,7},{7,6},{8,9},{9,8},{10,11... | collective-permute-start | bytes 958472 | tf_op jit(solution)/shard_map/ppermute | solution.py:93
  25.9 16.4 %collective-permute-start.1 = (bf16[512,768]{1,0:T(8,128)(2,1)S(1)}, bf16[512,768]{1,0:T(8,128)(2,1)S(1)}, u32[]{:S(2)}, u32[]{:S(2)}) collective-permute-start(bf16[512,768]{1,0:T(8,128)(2,1)S(1)} %pad_maximum_fusion.refs_0_), channel_id=1, source_target_pairs={{0,8},{8,0},{16,24},{24,16},{1,9},{9,1},{17,25},{25,17},{2,10},{10... | collective-permute-start | bytes 2359304 | tf_op jit(solution)/shard_map/ppermute | solution.py:93
  36.3 22.4 %collective-permute-start.11 = (bf16[256,768]{1,0:T(8,128)(2,1)S(1)}, bf16[256,768]{1,0:T(8,128)(2,1)}, u32[]{:S(2)}, u32[]{:S(2)}) collective-permute-start(bf16[256,768]{1,0:T(8,128)(2,1)S(1)} %bitcast.55), channel_id=1, source_target_pairs={{0,4},{1,5},{4,0},{5,1},{2,6},{3,7},{6,2},{7,3},{8,12},{9,13},{12,... | collective-permute-start | bytes 1179656 | tf_op jit(solution)/shard_map/ppermute | solution.py:97
  40.8 18.9 %collective-permute-start.10 = (bf16[256,768]{1,0:T(8,128)(2,1)S(1)}, bf16[256,768]{1,0:T(8,128)(2,1)S(1)}, u32[]{:S(2)}, u32[]{:S(2)}) collective-permute-start(bf16[256,768]{1,0:T(8,128)(2,1)S(1)} %bitcast.56), channel_id=1, source_target_pairs={{0,2},{1,3},{2,0},{3,1},{4,6},{5,7},{6,4},{7,5},{8,10},{9,11},{10,... | collective-permute-start | bytes 1179656 | tf_op jit(solution)/shard_map/ppermute | solution.py:97
  59.7 32.2 %collective-permute-start.14 = (bf16[256,768]{1,0:T(8,128)(2,1)S(1)}, bf16[256,768]{1,0:T(8,128)(2,1)}, u32[]{:S(2)}, u32[]{:S(2)}) collective-permute-start(bf16[256,768]{1,0:T(8,128)(2,1)S(1)} %bitcast.57), channel_id=1, source_target_pairs={{2,4},{3,5},{4,2},{5,3},{10,12},{11,13},{12,10},{13,11},{18,20},{1... | collective-permute-start | bytes 1179656 | tf_op jit(solution)/shard_map/ppermute | solution.py:97
  61.1 30.8 %collective-permute-start.13 = (bf16[256,768]{1,0:T(8,128)(2,1)}, bf16[256,768]{1,0:T(8,128)(2,1)}, u32[]{:S(2)}, u32[]{:S(2)}) collective-permute-start(bf16[256,768]{1,0:T(8,128)(2,1)} %collective-permute-done.11.refs_13_), channel_id=1, source_target_pairs={{4,6},{5,7},{2,0},{3,1},{12,14},{13,15},{10,8},{11,9},{20,22},{21,... | collective-permute-start | bytes 1179656 | tf_op jit(solution)/shard_map/ppermute | solution.py:97
  65.2 43.3 %collective-permute-start.21 = (bf16[1536,256]{1,0:T(8,128)(2,1)S(1)}, bf16[1536,256]{1,0:T(8,128)(2,1)S(1)}, u32[]{:S(2)}, u32[]{:S(2)}) collective-permute-start(bf16[1536,256]{1,0:T(8,128)(2,1)S(1)} %copy-done.2), channel_id=1, source_target_pairs={{0,2},{1,3},{2,0},{3,1},{4,6},{5,7},{6,4},{7,5},{8,10},{9,11},{10,... | collective-permute-start | bytes 2359304 | tf_op jit(solution)/shard_map/ppermute | solution.py:97
  68.5 39.9 %collective-permute-start.20 = (bf16[1536,256]{1,0:T(8,128)(2,1)S(1)}, bf16[1536,256]{1,0:T(8,128)(2,1)S(1)}, u32[]{:S(2)}, u32[]{:S(2)}) collective-permute-start(bf16[1536,256]{1,0:T(8,128)(2,1)S(1)} %copy-done.2), channel_id=1, source_target_pairs={{0,4},{1,5},{4,0},{5,1},{2,6},{3,7},{6,2},{7,3},{8,12},{9,13},{12,... | collective-permute-start | bytes 2359304 | tf_op jit(solution)/shard_map/ppermute | solution.py:97
  110.0 21.3 %collective-permute-start.23 = (bf16[1536,256]{1,0:T(8,128)(2,1)S(1)}, bf16[1536,256]{1,0:T(8,128)(2,1)}, u32[]{:S(2)}, u32[]{:S(2)}) collective-permute-start(bf16[1536,256]{1,0:T(8,128)(2,1)S(1)} %collective-permute-done.20.refs_8_), channel_id=1, source_target_pairs={{4,6},{5,7},{2,0},{3,1},{12,14},{13,15},{10,8},{11,9},{20,22},{21,... | collective-permute-start | bytes 2359304 | tf_op jit(solution)/shard_map/ppermute | solution.py:97
  114.8 16.4 %collective-permute-start.19 = (bf16[320,768]{1,0:T(8,128)(2,1)}, bf16[320,768]{1,0:T(8,128)(2,1)}, u32[]{:S(2)}, u32[]{:S(2)}) collective-permute-start(bf16[320,768]{1,0:T(8,128)(2,1)} %pad_maximum_fusion.6), channel_id=1, source_target_pairs={{0,1},{1,0},{2,3},{3,2},{4,5},{5,4},{6,7},{7,6},{8,9},{9,8},{10,11... | collective-permute-start | bytes 1474568 | tf_op jit(solution)/shard_map/ppermute | solution.py:93
  151.3 22.3 %collective-permute-start.24 = (bf16[320,768]{1,0:T(8,128)(2,1)}, bf16[320,768]{1,0:T(8,128)(2,1)S(1)}, u32[]{:S(2)}, u32[]{:S(2)}) collective-permute-start(bf16[320,768]{1,0:T(8,128)(2,1)} %get-tuple-element.116), channel_id=1, source_target_pairs={{0,1},{1,0},{2,3},{3,2},{4,5},{5,4},{6,7},{7,6},{8,9},{9,8},{10,11... | collective-permute-start | bytes 1474568 | tf_op jit(solution)/shard_map/ppermute | solution.py:93
  152.8 26.8 %collective-permute-start.25 = (bf16[2304,256]{1,0:T(8,128)(2,1)}, bf16[2304,256]{1,0:T(8,128)(2,1)S(1)}, u32[]{:S(2)}, u32[]{:S(2)}) collective-permute-start(bf16[2304,256]{1,0:T(8,128)(2,1)} %get-tuple-element.118), channel_id=1, source_target_pairs={{0,2},{1,3},{6,4},{7,5},{8,10},{9,11},{14,12},{15,13},{16,18},{17,... | collective-permute-start | bytes 3538952 | tf_op jit(solution)/shard_map/ppermute | solution.py:97
  154.5 28.5 %collective-permute-start.26 = (bf16[2304,256]{1,0:T(8,128)(2,1)}, bf16[2304,256]{1,0:T(8,128)(2,1)S(1)}, u32[]{:S(2)}, u32[]{:S(2)}) collective-permute-start(bf16[2304,256]{1,0:T(8,128)(2,1)} %get-tuple-element.118), channel_id=1, source_target_pairs={{2,4},{3,5},{4,2},{5,3},{10,12},{11,13},{12,10},{13,11},{18,20},{1... | collective-permute-start | bytes 3538952 | tf_op jit(solution)/shard_map/ppermute | solution.py:97
  179.6 35.5 %collective-permute-start.31 = (bf16[2304,256]{1,0:T(8,128)(2,1)S(1)}, bf16[2304,256]{1,0:T(8,128)(2,1)}, u32[]{:S(2)}, u32[]{:S(2)}) collective-permute-start(bf16[2304,256]{1,0:T(8,128)(2,1)S(1)} %copy-done.29), channel_id=1, source_target_pairs={{0,2},{1,3},{2,0},{3,1},{4,6},{5,7},{6,4},{7,5},{8,10},{9,11},{10,... | collective-permute-start | bytes 3538952 | tf_op jit(solution)/shard_map/ppermute | solution.py:97
  183.0 31.3 %collective-permute-start.30 = (bf16[768,256]{1,0:T(8,128)(2,1)}, bf16[768,256]{1,0:T(8,128)(2,1)S(1)}, u32[]{:S(2)}, u32[]{:S(2)}) collective-permute-start(bf16[768,256]{1,0:T(8,128)(2,1)} %slice.115), channel_id=1, source_target_pairs={{0,4},{1,5},{4,0},{5,1},{2,6},{3,7},{6,2},{7,3},{8,12},{9,13},{12,... | collective-permute-start | bytes 1179656 | tf_op jit(solution)/shard_map/ppermute | solution.py:97
  195.0 22.8 %collective-permute-start.33 = (bf16[384,896]{1,0:T(8,128)(2,1)}, bf16[384,896]{1,0:T(8,128)(2,1)S(1)}, u32[]{:S(2)}, u32[]{:S(2)}) collective-permute-start(bf16[384,896]{1,0:T(8,128)(2,1)} %get-tuple-element.137), channel_id=1, source_target_pairs={{0,8},{8,0},{16,24},{24,16},{1,9},{9,1},{17,25},{25,17},{2,10},{10... | collective-permute-start | bytes 2064392 | tf_op jit(solution)/shard_map/ppermute | solution.py:93
  215.2 22.1 %collective-permute-start.34 = (bf16[576,256]{1,0:T(8,128)(2,1)S(1)}, bf16[576,256]{1,0:T(8,128)(2,1)S(1)}, u32[]{:S(2)}, u32[]{:S(2)}) collective-permute-start(bf16[576,256]{1,0:T(8,128)(2,1)S(1)} %slice.116), channel_id=1, source_target_pairs={{0,4},{1,5},{4,0},{5,1},{2,6},{3,7},{6,2},{7,3},{8,12},{9,13},{12,... | collective-permute-start | bytes 884744 | tf_op jit(solution)/shard_map/ppermute | solution.py:97
  218.0 15.9 %collective-permute-start.42 = (bf16[192,896]{1,0:T(8,128)(2,1)S(1)}, bf16[192,896]{1,0:T(8,128)(2,1)S(1)}, u32[]{:S(2)}, u32[]{:S(2)}) collective-permute-start(bf16[192,896]{1,0:T(8,128)(2,1)S(1)} %get-tuple-element.191), channel_id=1, source_target_pairs={{0,16},{8,24},{16,0},{24,8},{1,17},{9,25},{17,1},{25,9},{2,18},{10... | collective-permute-start | bytes 1032200 | tf_op jit(solution)/shard_map/ppermute | solution.py:93
  235.7 38.1 %collective-permute-start.47 = (bf16[960,256]{1,0:T(8,128)(2,1)S(1)}, bf16[960,256]{1,0:T(8,128)(2,1)S(1)}, u32[]{:S(2)}, u32[]{:S(2)}) collective-permute-start(bf16[960,256]{1,0:T(8,128)(2,1)S(1)} %slice.131), channel_id=1, source_target_pairs={{0,4},{1,5},{4,0},{5,1},{2,6},{3,7},{6,2},{7,3},{8,12},{9,13},{12,... | collective-permute-start | bytes 1474568 | tf_op jit(solution)/shard_map/ppermute | solution.py:97
  (57 other events, 619.5 us)
where the time goes:
time: 301 us; the launch traced here: 300 us
  Pallas kernels  110 us (37%)
  waiting for transfers between devices  97.5 us (32%)
  starting transfers between devices  60.6 us (20%)
  local copies, waits for them, and re-layouts  19.5 us (6%)
  other arithmetic  10.8 us (4%)
    pallas_call x15, Pallas kernels, call(): pl.pallas_call(kernel, out_shape=outs, grid_spec=pltpu.PrefetchScalarGrid...  110 us
    ppermute x37, waiting for transfers between devices, swap(): return lax.ppermute(values, axis, [(i, i ^ bits) for i in range(size)])  61.6 us
    ppermute x37, starting transfers between devices, swap(): return lax.ppermute(values, axis, [(i, i ^ bits) for i in range(size)])  37 us
    ppermute x14, waiting for transfers between devices, along(): lax.ppermute(values, 'fsdp', [(2 * i + b, 2 * j + b) for i, j in pairs fo...  35.9 us
    ppermute x14, starting transfers between devices, along(): lax.ppermute(values, 'fsdp', [(2 * i + b, 2 * j + b) for i, j in pairs fo...  23.6 us
    unnamed x71, local copies, waits for them, and re-layouts  10.6 us
  transfers between devices with their start and end apart: 51, of which 24 were waited for; matrix products, arithmetic and copies ran while one was open for 8% of the time, Pallas kernels for 28%

commit v1 on v0

--- a/solution.py
+++ b/solution.py
@@ -108,6 +108,8 @@
 MIDDLE = ((1, 2), (2, 1))
 OUTWARD = ((2, 3), (1, 0))
 INWARD = ((0, 1), (3, 2))
+UP = ((0, 1), (1, 2), (2, 3))
+DOWN = ((3, 2), (2, 1), (1, 0))
 
 
 def minor_groups(major):
@@ -132,30 +134,23 @@
         out[other, :] = arrived[block * rows : (block + 1) * rows, :]
 
 
-def sum_parts_kernel(where, a, b, c, d0, d1, d2, away, kept, down):
+def sum_parts_kernel(where, a, b, c, away, kept, down):
     rows = away.shape[0] // 8
     mine = where[0]
 
-    def total(start, size, d, base):
-        source, shifted = pl.ds(start, size), pl.ds(start - base, size)
-        return (
-            a[source, :].astype(F32)
-            + b[source, :].astype(F32)
-            + c[source, :].astype(F32)
-            + d[shifted, :].astype(F32)
-        )
+    def total(source):
+        return a[source, :].astype(F32) + b[source, :].astype(F32) + c[source, :].astype(F32)
 
     for block in range(8):
         here = slice(block * rows, (block + 1) * rows)
         base = 2 * block * rows
-        d, cut = ((d0, 0), (d1, 8 * rows), (d2, 14 * rows))[(block > 3) + (block > 6)]
-        own = pl.multiple_of(base + mine * rows, rows)
-        other = pl.multiple_of(base + (1 - mine) * rows, rows)
-        away[here, :] = total(other, rows, d, cut).astype(BF)
-        kept[here, :] = total(own, rows, d, cut)
+        own = pl.ds(pl.multiple_of(base + mine * rows, rows), rows)
+        other = pl.ds(pl.multiple_of(base + (1 - mine) * rows, rows), rows)
+        away[here, :] = total(other).astype(BF)
+        kept[here, :] = total(own)
     for block in range(3):
         base = 16 * rows + block * 256
-        down[:, block * 256 : (block + 1) * 256] = total(base, 256, d2, 14 * rows)
+        down[:, block * 256 : (block + 1) * 256] = total(slice(base, base + 256))
 
 
 def unpack_kernel(where, kept, arrived, out):
@@ -169,23 +164,29 @@
         out[:, other] = arrived[here, :].astype(F32)
 
 
-def shared_pack(qkv, out, small_rows):
+def shared_pack(qkv, out, small):
     core = lax.axis_index("expert") % 2
     half_qkv, half_out = qkv.shape[1] // 2, out.shape[1] // 2
     rows = qkv.shape[0]
 
-    def kernel(where, qkv_ref, out_ref, small_ref, packed):
+    def kernel(where, qkv_ref, out_ref, *refs):
+        small_refs, (packed, room) = refs[:-2], refs[-2:]
         packed[:, :half_qkv] = qkv_ref[:, pl.ds(pl.multiple_of(where[0] * half_qkv, 128), half_qkv)]
         packed[:, half_qkv : half_qkv + half_out] = out_ref[
             :, pl.ds(pl.multiple_of(where[0] * half_out, 128), half_out)
         ]
-        packed[:32, half_qkv + half_out :] = small_ref[...]
-        packed[32:, half_qkv + half_out :] = jnp.zeros((rows - 32, SMALL), BF)
+        room[...] = jnp.zeros_like(room)
+        at = 0
+        for ref in small_refs:
+            room[at : at + ref.shape[0], : ref.shape[1]] = ref[...].astype(F32)
+            at += ref.shape[0]
+        packed[:, half_qkv + half_out :] = room[...].astype(BF)
 
     return call(
         kernel,
         shaped((rows, half_qkv + half_out + SMALL), BF),
-        (jnp.stack([core]).astype(jnp.int32), qkv, out, small_rows),
+        (jnp.stack([core]).astype(jnp.int32), qkv, out) + small,
+        scratch=[pltpu.VMEM((rows, SMALL), F32)],
         name="pack_shared",
         micros=1,
     )
@@ -220,10 +221,14 @@
 
 def across_major(parts, rows):
     pieces = [swap(parts[j * rows : (j + 1) * rows], "fsdp", 2 * j) for j in (1, 2, 3)]
-    total = parts[:rows].astype(F32)
-    for piece in pieces:
+    return [parts[:rows]] + pieces
+
+
+def summed_up(pieces):
+    total = pieces[0].astype(F32)
+    for piece in pieces[1:]:
         total += piece.astype(F32)
-    return total.astype(BF), pieces[0]
+    return total.astype(BF)
 
 
 def sequence_gather(values, across):
@@ -346,7 +351,7 @@
     return key <= query + own * count
 
 
-def attend_kernel(where, q, k, v, attended, log_total, *, slots):
+def attend_kernel(where, q, k, v, attended, kept, *, slots):
     own = where[slots]
     count, keys = q.shape[0], k.shape[0]
     query = stacked_heads(q[...], HEAD ** (-0.5))
@@ -355,28 +360,26 @@
     top = jnp.max(scores, axis=0, keepdims=True)
     weights = jnp.exp(scores - top)
     total = jnp.sum(weights, axis=0, keepdims=True)
-    log_total[...] = jnp.broadcast_to(top + jnp.log(total), (8, 2 * count))[None]
     weights = (weights * (1.0 / total)).astype(BF)
+    kept[0] = weights
     both = mm_tn(weights, v[...])
     lane = lanes((count, PAIR))
     attended[...] = jnp.where(lane < HEAD, both[:count], both[count:]).astype(BF)
 
 
-def attend_back_kernel(where, q, k, v, grad_att, log_total, cosine, sine, normed, normed_own, dq, dk, dv, away, kept, sums, *, slots, packed):
+def attend_back_kernel(where, q, k, v, grad_att, kept_weights, cosine, sine, normed, normed_own, dq, dk, dv, away, kept, sums, *, slots, packed):
     step = pl.program_id(0)
     own = where[slots]
-    count, keys = q.shape[0], k.shape[0]
+    count = q.shape[0]
     query = stacked_heads(q[...], HEAD ** (-0.5))
     grad_rows = stacked_heads(grad_att[...])
     key_rows = k[...]
-    scores = mm_nt(key_rows, query)
-    weights = jnp.where(
-        visible_keys(own, keys, count), jnp.exp(scores - log_total[0, :1, :]), 0.0
-    )
+    low_weights = kept_weights[0]
+    weights = low_weights.astype(F32)
     grad_weights = mm_nt(v[...], grad_rows)
     delta = jnp.sum(weights * grad_weights, axis=0, keepdims=True)
     grad_scores = (weights * (grad_weights - delta)).astype(BF)
-    grad_v = mm(weights.astype(BF), grad_rows).astype(BF)
+    grad_v = mm(low_weights, grad_rows).astype(BF)
     dv[...] = grad_v
     grad_k = turned(mm(grad_scores, query), cosine[...], -sine[...]).astype(BF)
     dk[...] = grad_k
@@ -420,18 +423,21 @@
             ref[target, :] = jnp.concatenate(pieces, axis=0).astype(BF)
 
 
+def as_lanes(rows):
+    rows = rows.astype(F32)
+    spare = jnp.zeros((SMALL - rows.shape[0], rows.shape[1]), F32)
+    return jnp.concatenate([rows, spare], axis=0).T
+
+
 def routing(routes, resid, logits, groups):
     count = routes.shape[0]
     lane = lanes((count, SMALL))
-    kind = lanes(resid.shape)
+    logits = logits + resid
     hot, picked = [], []
     for choice in range(2):
         route = routes[:, choice : choice + 1]
         hot.append(lane == route)
-        picked.append(
-            jnp.sum(jnp.where(hot[choice], logits, 0.0), axis=-1, keepdims=True)
-            + jnp.sum(jnp.where(kind == route, resid, 0.0), axis=-1, keepdims=True)
-        )
+        picked.append(jnp.sum(jnp.where(hot[choice], logits, 0.0), axis=-1, keepdims=True))
     top = jnp.maximum(picked[0], picked[1])
     first, second = jnp.exp(picked[0] - top), jnp.exp(picked[1] - top)
     gates = [first / (first + second), second / (first + second)]
@@ -456,7 +462,8 @@
     low = ((hidden * rms_scale(hidden)) * small_t[gain_at : gain_at + 1, :]).astype(BF)
     low_ref[...] = low
     logits = mm(low, small[...])
-    gates, _, dispatch = routing(routes[...], resid[...].astype(F32), logits, groups)
+    route = as_lanes(routes[...])[:, :2].astype(jnp.int32)
+    gates, _, dispatch = routing(route, as_lanes(resid[...]), logits, groups)
     grad = cot[...].astype(F32)
     rows_x[...] = mm_tn(dispatch[0] + dispatch[1], low).astype(BF)
     rows_g[...] = (
@@ -594,8 +601,8 @@
     grad = grad_low_type.astype(F32)
     logits = mm(low, small[...])
     grad_small_dot = mm(grad_low_type, small[...])
-    route = routes[...]
-    gates, hot, dispatch = routing(route, resid[...].astype(F32), logits, groups)
+    route = as_lanes(routes[...])[:, :2].astype(jnp.int32)
+    gates, hot, dispatch = routing(route, as_lanes(resid[...]), logits, groups)
     returned = [mm(dispatch[c], rows_y[...]) for c in range(2)]
     grad_back = mm(dispatch[0] + dispatch[1], rows_d[...])
     grad_dot = jnp.sum(grad * normed_input, axis=-1, keepdims=True)
@@ -635,7 +642,7 @@
     common = gates[0] * grad_gates[0] + gates[1] * grad_gates[1]
     for c in range(2):
         grad_logits = jnp.where(hot[c], gates[c] * (grad_gates[c] - common), grad_logits)
-    grad_resid[...] = grad_logits[:, :kinds].astype(BF)
+    grad_resid[...] = grad_logits.T[:kinds].astype(BF)
     high, rest = split_low(grad_logits)
     weights = small[...]
     grad_low = grad_back + direct * grad + mm_nt(high, weights) + mm_nt(rest, weights)
@@ -788,12 +795,7 @@
     at_rank = lambda j, w: (w[j], 0)
     just_minor = jnp.stack([minor])
 
-    small_rows = jnp.concatenate(
-        [router_weight.T, const_gate.T, const_value.T, gain_one[None], gain_two[None]], axis=0
-    )
-    small_rows = jnp.pad(
-        small_rows, ((0, 32 - small_rows.shape[0]), (0, SMALL - small_rows.shape[1]))
-    )
+    small_parts = (router_weight.T, const_gate.T, const_value.T, gain_one[None], gain_two[None])
     frequency = 10000.0 ** (-jnp.arange(HEAD // 2, dtype=F32) / (HEAD // 2))
     angles = jnp.arange(length, dtype=F32)[:, None] * frequency[None, :]
     cosine, sine = jnp.cos(angles), jnp.sin(angles)
@@ -802,7 +804,7 @@
 
     weight_args, order, across = (), [], None
     if packed:
-        shared = shared_pack(qkv_weight, out_weight, small_rows)
+        shared = shared_pack(qkv_weight, out_weight, small_parts)
         across = swap(tok, "expert", 2)
         tok_a, tok_b, ranks = sequence_gather(tok, across)
         away = call(
@@ -831,8 +833,9 @@
     else:
         qkv_full = lax.all_gather(qkv_weight, "fsdp", axis=0, tiled=True)
         out_full = lax.all_gather(out_weight, "fsdp", axis=0, tiled=True)
-        small = lax.all_gather(small_rows[:, :shard_rows], "fsdp", axis=1, tiled=True).T
-        small = jnp.pad(small, ((0, 0), (0, SMALL - 32)))
+        small_rows = jnp.concatenate(small_parts, axis=0)
+        small = lax.all_gather(small_rows, "fsdp", axis=1, tiled=True).T
+        small = jnp.pad(small, ((0, 0), (0, SMALL - small.shape[1])))
         small_t = small.astype(F32).T[:32]
         weight_args = (qkv_full, small_t)
         halves = expert_gate_up[0].reshape(shard_rows, 2, major_count, 2, unit)
@@ -900,19 +903,21 @@
         qkv_full, out_full, small, small_t = projected[4:]
     head_rows = pl.BlockSpec((count, PAIR), lambda h, w: (0, h))
     head_keys = pl.BlockSpec((length, PAIR), lambda h, w: (0, h))
-    head_log = pl.BlockSpec((1, 8, 2 * count), lambda h, w: (h, 0, 0))
-    attended, log_total = call(
+    attended, attend_weights = call(
         functools.partial(attend_kernel, slots=groups),
-        [shaped((count, width), BF), shaped((pairs, 8, 2 * count), F32)],
+        [shaped((count, width), BF), shaped((pairs, length, 2 * count), BF)],
         (where, q, k_all, v_all),
         grid=(pairs,),
         in_specs=[head_rows, head_keys, head_keys],
-        out_specs=[head_rows, head_log],
+        out_specs=[
+            head_rows,
+            pl.BlockSpec((1, length, 2 * count), lambda h, w: (h, 0, 0)),
+        ],
         name="attend",
         micros=12,
     )
 
-    residual, route, cot = gate_residual[0], routes[0], cotangent[0]
+    residual, route, cot = gate_residual[0].T, routes[0].T, cotangent[0]
     if packed:
         attended = after(attended, down_onward, down_middle)
     owners = [me_fsdp ^ (2 * j + i) for i in (0, 1) for j in range(4)]
@@ -963,12 +968,9 @@
 
     if packed:
         first = along(grads[3], INWARD)
-        middle = along(grads[3], MIDDLE)
         sent = added(grads[2], first)
-        near = along(after(grads[1], first), NEAR)
-        cuts = (0, 8 * shard_rows, 14 * shard_rows, sent.shape[0])
-        far = [along(sent[a:b], FAR) for a, b in zip(cuts, cuts[1:])]
-        backs[0] = after(backs[0], sent, middle)
+        up, down_way = along(sent, UP[:2]), along(sent, DOWN[:2])
+        backs[0] = after(backs[0], sent)
     else:
         scatter = lambda v: lax.psum_scatter(
             v,
@@ -999,7 +1001,7 @@
             shaped((count, width), BF),
             out_part,
             out_part,
-            shaped((count, kinds), BF),
+            shaped((kinds, count), BF),
         ],
         (slots,) + tuple(backs)
         + (hidden, low_two, cot, route, residual, small, small_t, out_full, attended),
@@ -1027,14 +1029,14 @@
                 grads_part,
                 grads_part,
             ],
-            (back_where, q, k_all, v_all, grad_rows, log_total, cosine, sine, normed, normed),
+            (back_where, q, k_all, v_all, grad_rows, attend_weights, cosine, sine, normed, normed),
             grid=(head_half,),
             in_specs=[
                 from_rows,
                 from_keys,
                 from_keys,
                 from_rows,
-                pl.BlockSpec((1, 8, 2 * count), lambda h, w: (base + h, 0, 0)),
+                pl.BlockSpec((1, length, 2 * count), lambda h, w: (base + h, 0, 0)),
                 pl.BlockSpec((length, PAIR), fixed),
                 pl.BlockSpec((length, PAIR), fixed),
                 pl.BlockSpec((width, length), fixed),
@@ -1055,8 +1057,10 @@
     dq_a, dk_a, dv_a, a_away, a_kept = attend_back(0, grad_att)
     if packed:
         a_away, a_kept, out_kept = lax.optimization_barrier(
-            (a_away, a_kept, out_kept, far[0], near)
+            (a_away, a_kept, out_kept, up, down_way)
         )[:3]
+        up = along(added(jnp.where(major == 1, grads[3], grads[1]), up), UP)
+        down_way = along(added(jnp.where(major == 2, grads[3], grads[1]), down_way), DOWN)
         out_both = added(out_kept, swap(out_away, "expert", 1))
         a_both = added(a_kept, swap(a_away, "expert", 1))
         grad_att = after(grad_att, a_both, out_both)
@@ -1076,15 +1080,16 @@
         )
 
     if packed:
-        b_away = after(b_away, far[1])
         out_sum, a_sum = along_chips(out_both, (b_kept,)), along_chips(a_both, (b_kept,))
         b_both = added(b_kept, swap(b_away, "expert", 1))
         dq_b = after(dq_b, b_both)
         b_sum = along_chips(b_both, ())
         parts_all = jnp.concatenate([a_sum, b_sum, out_sum], axis=1)
         rows_back, own_back = project_back(dq_b)
-        total, piece = across_major(after(parts_all, rows_back), shard_rows // 4)
-        own_grads = after(grads[0], piece)
+        pieces = across_major(
+            after(parts_all, rows_back, up, down_way), shard_rows // 4
+        )
+        own_grads = after(grads[0], pieces[1])
         away, kept, shard_down = call(
             sum_parts_kernel,
             [
@@ -1092,7 +1097,7 @@
                 shaped((8 * shard_rows, 256), F32),
                 shaped((256, width), F32),
             ],
-            (just_minor, own_grads, near, middle) + tuple(far),
+            (just_minor, own_grads, up, down_way),
             name="sum_parts",
             micros=3,
         )
@@ -1119,7 +1124,7 @@
     )
 
     if packed:
-        total = after(total, grad_tokens, shard_gate_up)
+        total = summed_up(pieces[:3] + [after(pieces[3], away)])
         total = jnp.concatenate([total, swap(total, "expert", 2)], axis=0)
         other = swap(total, "expert", 1)
     shared_grads = call(
@@ -1154,7 +1159,7 @@
         grad_value.T,
         shard_gate_up[None],
         shard_down[None],
-        grad_residual[None],
+        grad_residual.T[None],
         stream,
     )
 

time: 301 us -> 302 us (level)
  local copies, waits for them, and re-layouts: 19.5 us -> 12.6 us
  waiting for transfers between devices: 97.5 us -> 102 us
    ppermute x37, waiting for transfers between devices: 61.6 us -> 67.9 us  [swap(): return lax.ppermute(values, axis, [(i, i ^ bits) for i in range(size)])]
    unnamed x71 -> x63, local copies, waits for them, and re-layouts: 10.6 us -> 7.31 us
    pallas_call x15, Pallas kernels: 110 us -> 107 us  [call(): pl.pallas_call(kernel, out_shape=outs, grid_spec=pltpu.PrefetchScalarGrid...]
    ppermute x14 -> x13, starting transfers between devices: 23.6 us -> 26.1 us  [along(): lax.ppermute(values, 'fsdp', [(2 * i + b, 2 * j + b) for i, j in pairs fo...]
    ppermute x14 -> x13, waiting for transfers between devices: 35.9 us -> 34.5 us  [along(): lax.ppermute(values, 'fsdp', [(2 * i + b, 2 * j + b) for i, j in pairs fo...]
  transfers between devices with their start and end apart: 51 -> 50, of which waited for: 24 -> 23; matrix products, arithmetic and copies ran while one was open for 8% -> 7% of each run, Pallas kernels for 28% -> 28%
where the time goes in v1:
time: 302 us; the launch traced here: 299 us
  Pallas kernels  107 us (35%)
  waiting for transfers between devices  102 us (34%)
  starting transfers between devices  62.6 us (21%)
  other arithmetic  13.1 us (4%)
  local copies, waits for them, and re-layouts  12.6 us (4%)
    pallas_call x15, Pallas kernels, call(): pl.pallas_call(kernel, out_shape=outs, grid_spec=pltpu.PrefetchScalarGrid...  107 us
    ppermute x37, waiting for transfers between devices, swap(): return lax.ppermute(values, axis, [(i, i ^ bits) for i in range(size)])  67.9 us
    ppermute x37, starting transfers between devices, swap(): return lax.ppermute(values, axis, [(i, i ^ bits) for i in range(size)])  36.5 us
    ppermute x13, waiting for transfers between devices, along(): lax.ppermute(values, 'fsdp', [(2 * i + b, 2 * j + b) for i, j in pairs fo...  34.5 us
    ppermute x13, starting transfers between devices, along(): lax.ppermute(values, 'fsdp', [(2 * i + b, 2 * j + b) for i, j in pairs fo...  26.1 us
    unnamed x63, local copies, waits for them, and re-layouts  7.31 us
  transfers between devices with their start and end apart: 50, of which 23 were waited for; matrix products, arithmetic and copies ran while one was open for 7% of the time, Pallas kernels for 28%

profile of v1, /device:TPU:0, one launch (start us, length us, event | category | flops | bytes accessed | tf_op | source)
XLA Modules:
  0.0 299.2 jit_solution(617784482819283258)
XLA Ops:
  18.4 4.9 %collective-permute-done.2 = bf16[96,1664]{1,0:T(8,128)(2,1)} collective-permute-done((bf16[96,1664]{1,0:T(8,128)(2,1)}, bf16[96,1664]{1,0:T(8,128)(2,1)}, u32[]{:S(2)}, u32[]{:S(2)}) %collective-permute-start.2) | collective-permute-done | bytes 319520 | tf_op jit(solution)/shard_map/ppermute | solution.py:93
  25.2 5.5 %collective-permute-done.3 = bf16[96,1664]{1,0:T(8,128)(2,1)} collective-permute-done((bf16[96,1664]{1,0:T(8,128)(2,1)}, bf16[96,1664]{1,0:T(8,128)(2,1)}, u32[]{:S(2)}, u32[]{:S(2)}) %collective-permute-start.3) | collective-permute-done | bytes 319520 | tf_op jit(solution)/shard_map/ppermute | solution.py:93
  34.6 4.1 %collective-permute-start.11 = (bf16[256,768]{1,0:T(8,128)(2,1)}, bf16[256,768]{1,0:T(8,128)(2,1)}, u32[]{:S(2)}, u32[]{:S(2)}) collective-permute-start(bf16[256,768]{1,0:T(8,128)(2,1)} %bitcast.27.refs_11_), channel_id=1, source_target_pairs={{0,4},{1,5},{4,0},{5,1},{2,6},{3,7},{6,2},{7,3},{8,12},{9,13},{12,... | collective-permute-start | bytes 1179656 | tf_op jit(solution)/shard_map/ppermute | solution.py:97
  40.5 8.6 %collective-permute-done.9 = bf16[96,1664]{1,0:T(8,128)(2,1)S(1)} collective-permute-done((bf16[96,1664]{1,0:T(8,128)(2,1)S(1)}, bf16[96,1664]{1,0:T(8,128)(2,1)S(1)}, u32[]{:S(2)}, u32[]{:S(2)}) %collective-permute-start.9) | collective-permute-done | bytes 319520 | tf_op jit(solution)/shard_map/ppermute | solution.py:93
  49.1 7.8 %collective-permute-done.11.refs_13_ = bf16[256,768]{1,0:T(8,128)(2,1)} collective-permute-done((bf16[256,768]{1,0:T(8,128)(2,1)}, bf16[256,768]{1,0:T(8,128)(2,1)}, u32[]{:S(2)}, u32[]{:S(2)}) %collective-permute-start.11) | collective-permute-done | bytes 393248 | tf_op jit(solution)/shard_map/ppermute | solution.py:97
  62.7 3.4 %collective-permute-start.21 = (bf16[1536,256]{1,0:T(8,128)(2,1)S(1)}, bf16[1536,256]{1,0:T(8,128)(2,1)S(1)}, u32[]{:S(2)}, u32[]{:S(2)}) collective-permute-start(bf16[1536,256]{1,0:T(8,128)(2,1)S(1)} %copy-done.3), channel_id=1, source_target_pairs={{0,2},{1,3},{2,0},{3,1},{4,6},{5,7},{6,4},{7,5},{8,10},{9,11},{10,... | collective-permute-start | bytes 2359304 | tf_op jit(solution)/shard_map/ppermute | solution.py:97
  66.0 11.1 %project.1 = (bf16[256,768]{1,0:T(8,128)(2,1)}, bf16[1024,768]{1,0:T(8,128)(2,1)}, bf16[1024,768]{1,0:T(8,128)(2,1)}, bf16[768,1024]{1,0:T(8,128)(2,1)}, bf16[76...) custom-call(s32[14]{0:T(128)} %stack.129.where, ...), custom_call_target="tpu_custom_call" | custom-call | flops 900000000 | bytes 3000000 | tf_op jit(solution)/shard_map/project/pallas_call | solution.py:69
  77.1 12.7 %attend.1 = (bf16[256,768]{1,0:T(8,128)(2,1)}, bf16[6,1024,512]{2,1,0:T(8,128)(2,1)}) custom-call(s32[14]{0:T(128)} %stack.129.where, bf16[256,768]{1,0:T(8,128)(2,1)} %get-tuple-element.95.q, bf16[1024,768]{1,0:T(8,128)(2,1)} %get-tuple-element.96.k, bf16[1024,768]{1,0:T(8,128)(2,1)} %get-tuple-element.97.v), custom_call_target="tpu_custom_call" | custom-call | flops 1080000000 | bytes 3600000 | tf_op jit(solution)/shard_map/attend/pallas_call | solution.py:69
  89.8 5.0 %route.1 = (f32[256,768]{1,0:T(8,128)}, bf16[256,768]{1,0:T(8,128)(2,1)}, bf16[160,768]{1,0:T(8,128)(2,1)}, bf16[160,768]{1,0:T(8,128)(2,1)}, bf16[160,768]{1,0:T(8,128)(2,1)}, /*index=5*/bf16[160,768]{1,0:T(8,128)(2,1)}) custom-call(s32[15]{0:T(128)} %stack.121.where, bf16[256,768]{1,0:T(8,128)(2,1)} %get-tuple-element.100.att.refs_12_, ...), custom_call_target="tpu_custom_call" | custom-call | flops 450000000 | bytes 1500000 | tf_op jit(solution)/shard_map/route/pallas_call | solution.py:69
  101.0 6.4 %collective-permute-done.21.refs_7_ = bf16[1536,256]{1,0:T(8,128)(2,1)S(1)} collective-permute-done((bf16[1536,256]{1,0:T(8,128)(2,1)S(1)}, bf16[1536,256]{1,0:T(8,128)(2,1)S(1)}, u32[]{:S(2)}, u32[]{:S(2)}) %collective-permute-start.21) | collective-permute-done | bytes 786464 | tf_op jit(solution)/shard_map/ppermute | solution.py:97
  114.8 14.7 %collective-permute-done.23.refs_10_ = bf16[1536,256]{1,0:T(8,128)(2,1)S(1)} collective-permute-done((bf16[1536,256]{1,0:T(8,128)(2,1)}, bf16[1536,256]{1,0:T(8,128)(2,1)S(1)}, u32[]{:S(2)}, u32[]{:S(2)}) %collective-permute-start.23) | collective-permute-done | bytes 786464 | tf_op jit(solution)/shard_map/ppermute | solution.py:97
  130.5 19.4 %expert.1 = (f32[320,768]{1,0:T(8,128)}, f32[320,768]{1,0:T(8,128)}, bf16[320,768]{1,0:T(8,128)(2,1)}, bf16[320,768]{1,0:T(8,128)(2,1)}, bf16[2304,256]{1,0:T(8,...) custom-call(s32[5]{0:T(128)} %stack.128.where, ...), custom_call_target="tpu_custom_call" | custom-call | flops 1620000000 | bytes 5400000 | tf_op jit(solution)/shard_map/expert/pallas_call | solution.py:69
  153.6 10.7 %collective-permute-done.26 = bf16[320,768]{1,0:T(8,128)(2,1)S(1)} collective-permute-done((bf16[320,768]{1,0:T(8,128)(2,1)}, bf16[320,768]{1,0:T(8,128)(2,1)S(1)}, u32[]{:S(2)}, u32[]{:S(2)}) %collective-permute-start.26) | collective-permute-done | bytes 491552 | tf_op jit(solution)/shard_map/ppermute | solution.py:93
  167.2 5.6 %collective-permute-done.24 = bf16[320,768]{1,0:T(8,128)(2,1)S(1)} collective-permute-done((bf16[320,768]{1,0:T(8,128)(2,1)}, bf16[320,768]{1,0:T(8,128)(2,1)S(1)}, u32[]{:S(2)}, u32[]{:S(2)}) %collective-permute-start.24) | collective-permute-done | bytes 491552 | tf_op jit(solution)/shard_map/ppermute | solution.py:93
  178.7 4.9 %collective-permute-start.29 = (bf16[2304,256]{1,0:T(8,128)(2,1)S(1)}, bf16[2304,256]{1,0:T(8,128)(2,1)S(1)}, u32[]{:S(2)}, u32[]{:S(2)}) collective-permute-start(bf16[2304,256]{1,0:T(8,128)(2,1)S(1)} %add_convert_fusion.2), channel_id=1, source_target_pairs={{0,2},{1,3},{2,4},{3,5},{8,10},{9,11},{10,12},{11,13},{16,18},{17,... | collective-permute-start | bytes 3538952 | tf_op jit(solution)/shard_map/ppermute | solution.py:97
  186.4 9.9 %combine.1 = (bf16[256,768]{1,0:T(8,128)(2,1)}, f32[256,768]{1,0:T(8,128)}, bf16[256,768]{1,0:T(8,128)(2,1)}, bf16[384,896]{1,0:T(8,128)(2,1)}, bf16[384,896]{1,0:T(8,128)(2,1)}, /*index=5*/bf16[8,256]{1,0:T(8,128)(2,1)}) custom-call(s32[15]{0:T(128)} %stack.121.where, bf16[160,768]{1,0:T(8,128)(2,1)} %get-tuple-element.117.refs_0_, ...), custom_call_target="tpu_custom_call" | custom-call | flops 900000000 | bytes 3000000 | tf_op jit(solution)/shard_map/combine/pallas_call | solution.py:69
  197.2 12.0 %attend_back.2 = (bf16[256,384]{1,0:T(8,128)(2,1)}, bf16[1024,384]{1,0:T(8,128)(2,1)}, bf16[1024,384]{1,0:T(8,128)(2,1)}, bf16[384,1152]{1,0:T(8,128)(2,1)}, bf16[384,1152]{1,0:T(8,128)(2,1)}) custom-call(s32[15]{0:T(128)} %stack.131.where, bf16[256,768]{1,0:T(8,128)(2,1)} %get-tuple-element.95.q, bf16[1024,768]{1,0:T(8,128)(2,1)} %get-tuple-element.96.k, ...), custom_call_target="tpu_custom_call" | custom-call | flops 990000000 | bytes 3300000 | tf_op jit(solution)/shard_map/attend_back/pallas_call | solution.py:69
  213.1 11.8 %attend_back.3 = (bf16[256,384]{1,0:T(8,128)(2,1)}, bf16[1024,384]{1,0:T(8,128)(2,1)}, bf16[1024,384]{1,0:T(8,128)(2,1)}, bf16[384,1152]{1,0:T(8,128)(2,1)}, bf16[384,1152]{1,0:T(8,128)(2,1)}) custom-call(s32[15]{0:T(128)} %stack.131.where, bf16[256,768]{1,0:T(8,128)(2,1)} %get-tuple-element.95.q, bf16[1024,768]{1,0:T(8,128)(2,1)} %get-tuple-element.96.k, ...), custom_call_target="tpu_custom_call" | custom-call | flops 990000000 | bytes 3300000 | tf_op jit(solution)/shard_map/attend_back/pallas_call | solution.py:69
  229.9 5.2 %collective-permute-start.42 = (bf16[2304,256]{1,0:T(8,128)(2,1)S(1)}, bf16[2304,256]{1,0:T(8,128)(2,1)S(1)}, u32[]{:S(2)}, u32[]{:S(2)}) collective-permute-start(bf16[2304,256]{1,0:T(8,128)(2,1)S(1)} %get-tuple-element.166), channel_id=1, source_target_pairs={{0,2},{1,3},{2,4},{3,5},{4,6},{5,7},{8,10},{9,11},{10,12},{11,13},... | collective-permute-start | bytes 3538952 | tf_op jit(solution)/shard_map/ppermute | solution.py:97
  240.6 8.5 %collective-permute-done.38 = bf16[192,1152]{1,0:T(8,128)(2,1)S(1)} collective-permute-done((bf16[192,1152]{1,0:T(8,128)(2,1)S(1)}, bf16[192,1152]{1,0:T(8,128)(2,1)S(1)}, u32[]{:S(2)}, u32[]{:S(2)}) %collective-permute-start.38) | collective-permute-done | bytes 442400 | tf_op jit(solution)/shard_map/ppermute | solution.py:93
  250.4 8.0 %project_back.1 = (bf16[1024,768]{1,0:T(8,128)(2,1)}, f32[256,768]{1,0:T(8,128)}) custom-call(s32[15]{0:T(128)} %stack.131.where, bf16[256,384]{1,0:T(8,128)(2,1)} %get-tuple-element.126.refs_0_, bf16[256,384]{1,0:T(8,128)(2,1)} %get-tuple-element.138.refs_1_, bf16[1024,384]{1,0:T(8,128)(2,1)} %get-tuple-element.139.refs_2_, ...), custom_call_target="tpu_custom_call" | custom-call | flops 540000000 | bytes 1800000 | tf_op jit(solution)/shard_map/project_back/pallas_call | solution.py:69
  269.1 3.5 %sum_parts.1 = (bf16[768,256]{1,0:T(8,128)(2,1)}, f32[768,256]{1,0:T(8,128)}, f32[256,768]{1,0:T(8,128)}) custom-call(s32[1]{0:T(128)} %bitcast.25.where, bf16[2304,256]{1,0:T(8,128)(2,1)} %get-tuple-element.151.a, bf16[2304,256]{1,0:T(8,128)(2,1)} %copy-done.9, bf16[2304,256]{1,0:T(8,128)(2,1)} %copy-done.8), custom_call_target="tpu_custom_call" | custom-call | flops 270000000 | bytes 900000 | tf_op jit(solution)/shard_map/sum_parts/pallas_call | solution.py:69
  272.6 3.4 %collective-permute-done.46 = bf16[24,3200]{1,0:T(8,128)(2,1)S(1)} collective-permute-done((bf16[24,3200]{1,0:T(8,128)(2,1)S(1)}, bf16[24,3200]{1,0:T(8,128)(2,1)S(1)}, u32[]{:S(2)}, u32[]{:S(2)}) %collective-permute-start.46) | collective-permute-done | bytes 153632 | tf_op jit(solution)/shard_map/ppermute | solution.py:93
  284.8 4.1 %collective-permute-done.35 = bf16[256,768]{1,0:T(8,128)(2,1)S(1)} collective-permute-done((bf16[256,768]{1,0:T(8,128)(2,1)S(1)}, bf16[256,768]{1,0:T(8,128)(2,1)S(1)}, u32[]{:S(2)}, u32[]{:S(2)}) %collective-permute-start.35) | collective-permute-done | bytes 393248 | tf_op jit(solution)/shard_map/ppermute | solution.py:93
  (197 shorter events, 106.8 us)
Async XLA Ops:
  2.6 15.1 %collective-permute-start.4 = (bf16[96,1664]{1,0:T(8,128)(2,1)}, bf16[96,1664]{1,0:T(8,128)(2,1)}, u32[]{:S(2)}, u32[]{:S(2)}) collective-permute-start(bf16[96,1664]{1,0:T(8,128)(2,1)} %pack_shared.1), channel_id=1, source_target_pairs={{0,1},{1,0},{2,3},{3,2},{4,5},{5,4},{6,7},{7,6},{8,9},{9,8},{10,11... | collective-permute-start | bytes 958472 | tf_op jit(solution)/shard_map/ppermute | solution.py:93
  5.5 25.1 %collective-permute-start.3 = (bf16[96,1664]{1,0:T(8,128)(2,1)}, bf16[96,1664]{1,0:T(8,128)(2,1)}, u32[]{:S(2)}, u32[]{:S(2)}) collective-permute-start(bf16[96,1664]{1,0:T(8,128)(2,1)} %pack_shared.1), channel_id=1, source_target_pairs={{0,4},{1,5},{2,6},{3,7},{4,0},{5,1},{6,2},{7,3},{8,12},{9,13},{10,... | collective-permute-start | bytes 958472 | tf_op jit(solution)/shard_map/ppermute | solution.py:93
  8.1 15.2 %collective-permute-start.2 = (bf16[96,1664]{1,0:T(8,128)(2,1)}, bf16[96,1664]{1,0:T(8,128)(2,1)}, u32[]{:S(2)}, u32[]{:S(2)}) collective-permute-start(bf16[96,1664]{1,0:T(8,128)(2,1)} %pack_shared.1), channel_id=1, source_target_pairs={{0,2},{1,3},{2,0},{3,1},{4,6},{5,7},{6,4},{7,5},{8,10},{9,11},{10,... | collective-permute-start | bytes 958472 | tf_op jit(solution)/shard_map/ppermute | solution.py:93
  11.6 20.0 %collective-permute-start.7 = (bf16[768,256]{1,0:T(8,128)(2,1)}, bf16[768,256]{1,0:T(8,128)(2,1)S(1)}, u32[]{:S(2)}, u32[]{:S(2)}) collective-permute-start(bf16[768,256]{1,0:T(8,128)(2,1)} %blocks.1), channel_id=1, source_target_pairs={{0,1},{1,0},{2,3},{3,2},{4,5},{5,4},{6,7},{7,6},{8,9},{9,8},{10,11... | collective-permute-start | bytes 1179656 | tf_op jit(solution)/shard_map/ppermute | solution.py:93
  17.7 17.0 %collective-permute-start.5 = (bf16[96,1664]{1,0:T(8,128)(2,1)S(1)}, bf16[96,1664]{1,0:T(8,128)(2,1)S(1)}, u32[]{:S(2)}, u32[]{:S(2)}) collective-permute-start(bf16[96,1664]{1,0:T(8,128)(2,1)S(1)} %copy-done.5), channel_id=1, source_target_pairs={{0,6},{1,7},{2,4},{3,5},{4,2},{5,3},{6,0},{7,1},{8,14},{9,15},{10,... | collective-permute-start | bytes 958472 | tf_op jit(solution)/shard_map/ppermute | solution.py:93
  23.3 16.5 %collective-permute-start.6 = (bf16[96,1664]{1,0:T(8,128)(2,1)}, bf16[96,1664]{1,0:T(8,128)(2,1)S(1)}, u32[]{:S(2)}, u32[]{:S(2)}) collective-permute-start(bf16[96,1664]{1,0:T(8,128)(2,1)} %collective-permute-done.2), channel_id=1, source_target_pairs={{0,1},{1,0},{2,3},{3,2},{4,5},{5,4},{6,7},{7,6},{8,9},{9,8},{10,11... | collective-permute-start | bytes 958472 | tf_op jit(solution)/shard_map/ppermute | solution.py:93
  23.9 15.9 %collective-permute-start.1 = (bf16[512,768]{1,0:T(8,128)(2,1)S(1)}, bf16[512,768]{1,0:T(8,128)(2,1)S(1)}, u32[]{:S(2)}, u32[]{:S(2)}) collective-permute-start(bf16[512,768]{1,0:T(8,128)(2,1)S(1)} %pad_maximum_fusion.refs_0_), channel_id=1, source_target_pairs={{0,8},{8,0},{16,24},{24,16},{1,9},{9,1},{17,25},{25,17},{2,10},{10... | collective-permute-start | bytes 2359304 | tf_op jit(solution)/shard_map/ppermute | solution.py:93
  34.6 22.3 %collective-permute-start.11 = (bf16[256,768]{1,0:T(8,128)(2,1)}, bf16[256,768]{1,0:T(8,128)(2,1)}, u32[]{:S(2)}, u32[]{:S(2)}) collective-permute-start(bf16[256,768]{1,0:T(8,128)(2,1)} %bitcast.27.refs_11_), channel_id=1, source_target_pairs={{0,4},{1,5},{4,0},{5,1},{2,6},{3,7},{6,2},{7,3},{8,12},{9,13},{12,... | collective-permute-start | bytes 1179656 | tf_op jit(solution)/shard_map/ppermute | solution.py:97
  38.8 19.1 %collective-permute-start.10 = (bf16[256,768]{1,0:T(8,128)(2,1)}, bf16[256,768]{1,0:T(8,128)(2,1)S(1)}, u32[]{:S(2)}, u32[]{:S(2)}) collective-permute-start(bf16[256,768]{1,0:T(8,128)(2,1)} %bitcast.27.refs_11_), channel_id=1, source_target_pairs={{0,2},{1,3},{2,0},{3,1},{4,6},{5,7},{6,4},{7,5},{8,10},{9,11},{10,... | collective-permute-start | bytes 1179656 | tf_op jit(solution)/shard_map/ppermute | solution.py:97
  58.7 31.1 %collective-permute-start.14 = (bf16[256,768]{1,0:T(8,128)(2,1)}, bf16[256,768]{1,0:T(8,128)(2,1)}, u32[]{:S(2)}, u32[]{:S(2)}) collective-permute-start(bf16[256,768]{1,0:T(8,128)(2,1)} %bitcast.27.refs_11_), channel_id=1, source_target_pairs={{2,4},{3,5},{4,2},{5,3},{10,12},{11,13},{12,10},{13,11},{18,20},{1... | collective-permute-start | bytes 1179656 | tf_op jit(solution)/shard_map/ppermute | solution.py:97
  60.1 29.7 %collective-permute-start.13 = (bf16[256,768]{1,0:T(8,128)(2,1)}, bf16[256,768]{1,0:T(8,128)(2,1)}, u32[]{:S(2)}, u32[]{:S(2)}) collective-permute-start(bf16[256,768]{1,0:T(8,128)(2,1)} %collective-permute-done.11.refs_13_), channel_id=1, source_target_pairs={{4,6},{5,7},{2,0},{3,1},{12,14},{13,15},{10,8},{11,9},{20,22},{21,... | collective-permute-start | bytes 1179656 | tf_op jit(solution)/shard_map/ppermute | solution.py:97
  62.7 44.8 %collective-permute-start.21 = (bf16[1536,256]{1,0:T(8,128)(2,1)S(1)}, bf16[1536,256]{1,0:T(8,128)(2,1)S(1)}, u32[]{:S(2)}, u32[]{:S(2)}) collective-permute-start(bf16[1536,256]{1,0:T(8,128)(2,1)S(1)} %copy-done.3), channel_id=1, source_target_pairs={{0,2},{1,3},{2,0},{3,1},{4,6},{5,7},{6,4},{7,5},{8,10},{9,11},{10,... | collective-permute-start | bytes 2359304 | tf_op jit(solution)/shard_map/ppermute | solution.py:97
  66.0 41.4 %collective-permute-start.20 = (bf16[1536,256]{1,0:T(8,128)(2,1)S(1)}, bf16[1536,256]{1,0:T(8,128)(2,1)}, u32[]{:S(2)}, u32[]{:S(2)}) collective-permute-start(bf16[1536,256]{1,0:T(8,128)(2,1)S(1)} %copy-done.3), channel_id=1, source_target_pairs={{0,4},{1,5},{4,0},{5,1},{2,6},{3,7},{6,2},{7,3},{8,12},{9,13},{12,... | collective-permute-start | bytes 2359304 | tf_op jit(solution)/shard_map/ppermute | solution.py:97
  97.6 15.1 %collective-permute-start.18 = (bf16[320,768]{1,0:T(8,128)(2,1)S(1)}, bf16[320,768]{1,0:T(8,128)(2,1)}, u32[]{:S(2)}, u32[]{:S(2)}) collective-permute-start(bf16[320,768]{1,0:T(8,128)(2,1)S(1)} %pad_maximum_fusion.5), channel_id=1, source_target_pairs={{0,1},{1,0},{2,3},{3,2},{4,5},{5,4},{6,7},{7,6},{8,9},{9,8},{10,11... | collective-permute-start | bytes 1474568 | tf_op jit(solution)/shard_map/ppermute | solution.py:93
  108.2 21.4 %collective-permute-start.23 = (bf16[1536,256]{1,0:T(8,128)(2,1)}, bf16[1536,256]{1,0:T(8,128)(2,1)S(1)}, u32[]{:S(2)}, u32[]{:S(2)}) collective-permute-start(bf16[1536,256]{1,0:T(8,128)(2,1)} %collective-permute-done.20.refs_8_), channel_id=1, source_target_pairs={{4,6},{5,7},{2,0},{3,1},{12,14},{13,15},{10,8},{11,9},{20,22},{21,... | collective-permute-start | bytes 2359304 | tf_op jit(solution)/shard_map/ppermute | solution.py:97
  112.7 16.9 %collective-permute-start.19 = (bf16[320,768]{1,0:T(8,128)(2,1)}, bf16[320,768]{1,0:T(8,128)(2,1)}, u32[]{:S(2)}, u32[]{:S(2)}) collective-permute-start(bf16[320,768]{1,0:T(8,128)(2,1)} %pad_maximum_fusion.6), channel_id=1, source_target_pairs={{0,1},{1,0},{2,3},{3,2},{4,5},{5,4},{6,7},{7,6},{8,9},{9,8},{10,11... | collective-permute-start | bytes 1474568 | tf_op jit(solution)/shard_map/ppermute | solution.py:93
  149.9 14.4 %collective-permute-start.26 = (bf16[320,768]{1,0:T(8,128)(2,1)}, bf16[320,768]{1,0:T(8,128)(2,1)S(1)}, u32[]{:S(2)}, u32[]{:S(2)}) collective-permute-start(bf16[320,768]{1,0:T(8,128)(2,1)} %get-tuple-element.119), channel_id=1, source_target_pairs={{0,1},{1,0},{2,3},{3,2},{4,5},{5,4},{6,7},{7,6},{8,9},{9,8},{10,11... | collective-permute-start | bytes 1474568 | tf_op jit(solution)/shard_map/ppermute | solution.py:93
  150.5 22.3 %collective-permute-start.24 = (bf16[320,768]{1,0:T(8,128)(2,1)}, bf16[320,768]{1,0:T(8,128)(2,1)S(1)}, u32[]{:S(2)}, u32[]{:S(2)}) collective-permute-start(bf16[320,768]{1,0:T(8,128)(2,1)} %get-tuple-element.114), channel_id=1, source_target_pairs={{0,1},{1,0},{2,3},{3,2},{4,5},{5,4},{6,7},{7,6},{8,9},{9,8},{10,11... | collective-permute-start | bytes 1474568 | tf_op jit(solution)/shard_map/ppermute | solution.py:93
  152.0 25.7 %collective-permute-start.25 = (bf16[2304,256]{1,0:T(8,128)(2,1)}, bf16[2304,256]{1,0:T(8,128)(2,1)S(1)}, u32[]{:S(2)}, u32[]{:S(2)}) collective-permute-start(bf16[2304,256]{1,0:T(8,128)(2,1)} %get-tuple-element.116), channel_id=1, source_target_pairs={{0,2},{1,3},{6,4},{7,5},{8,10},{9,11},{14,12},{15,13},{16,18},{17,... | collective-permute-start | bytes 3538952 | tf_op jit(solution)/shard_map/ppermute | solution.py:97
  178.0 31.2 %collective-permute-start.30 = (bf16[2304,256]{1,0:T(8,128)(2,1)S(1)}, bf16[2304,256]{1,0:T(8,128)(2,1)S(1)}, u32[]{:S(2)}, u32[]{:S(2)}) collective-permute-start(bf16[2304,256]{1,0:T(8,128)(2,1)S(1)} %add_convert_fusion.2), channel_id=1, source_target_pairs={{6,4},{7,5},{4,2},{5,3},{14,12},{15,13},{12,10},{13,11},{22,20},{2... | collective-permute-start | bytes 3538952 | tf_op jit(solution)/shard_map/ppermute | solution.py:97
  178.7 30.5 %collective-permute-start.29 = (bf16[2304,256]{1,0:T(8,128)(2,1)S(1)}, bf16[2304,256]{1,0:T(8,128)(2,1)S(1)}, u32[]{:S(2)}, u32[]{:S(2)}) collective-permute-start(bf16[2304,256]{1,0:T(8,128)(2,1)S(1)} %add_convert_fusion.2), channel_id=1, source_target_pairs={{0,2},{1,3},{2,4},{3,5},{8,10},{9,11},{10,12},{11,13},{16,18},{17,... | collective-permute-start | bytes 3538952 | tf_op jit(solution)/shard_map/ppermute | solution.py:97
  228.5 31.4 %collective-permute-start.43 = (bf16[2304,256]{1,0:T(8,128)(2,1)}, bf16[2304,256]{1,0:T(8,128)(2,1)S(1)}, u32[]{:S(2)}, u32[]{:S(2)}) collective-permute-start(bf16[2304,256]{1,0:T(8,128)(2,1)} %get-tuple-element.165), channel_id=1, source_target_pairs={{6,4},{7,5},{4,2},{5,3},{2,0},{3,1},{14,12},{15,13},{12,10},{13,11... | collective-permute-start | bytes 3538952 | tf_op jit(solution)/shard_map/ppermute | solution.py:97
  229.9 31.0 %collective-permute-start.42 = (bf16[2304,256]{1,0:T(8,128)(2,1)S(1)}, bf16[2304,256]{1,0:T(8,128)(2,1)S(1)}, u32[]{:S(2)}, u32[]{:S(2)}) collective-permute-start(bf16[2304,256]{1,0:T(8,128)(2,1)S(1)} %get-tuple-element.166), channel_id=1, source_target_pairs={{0,2},{1,3},{2,4},{3,5},{4,6},{5,7},{8,10},{9,11},{10,12},{11,13},... | collective-permute-start | bytes 3538952 | tf_op jit(solution)/shard_map/ppermute | solution.py:97
  263.6 14.3 %collective-permute-start.45 = (bf16[24,3200]{1,0:T(8,128)(2,1)S(1)}, bf16[24,3200]{1,0:T(8,128)(2,1)S(1)}, u32[]{:S(2)}, u32[]{:S(2)}) collective-permute-start(bf16[24,3200]{1,0:T(8,128)(2,1)S(1)} %get-tuple-element.177), channel_id=1, source_target_pairs={{0,4},{1,5},{2,6},{3,7},{4,0},{5,1},{6,2},{7,3},{8,12},{9,13},{10,... | collective-permute-start | bytes 460808 | tf_op jit(solution)/shard_map/ppermute | solution.py:93
  (54 other events, 491.3 us)

commit v2 on v1

--- a/solution.py
+++ b/solution.py
@@ -108,8 +108,6 @@
 MIDDLE = ((1, 2), (2, 1))
 OUTWARD = ((2, 3), (1, 0))
 INWARD = ((0, 1), (3, 2))
-UP = ((0, 1), (1, 2), (2, 3))
-DOWN = ((3, 2), (2, 1), (1, 0))
 
 
 def minor_groups(major):
@@ -134,23 +132,30 @@
         out[other, :] = arrived[block * rows : (block + 1) * rows, :]
 
 
-def sum_parts_kernel(where, a, b, c, away, kept, down):
+def sum_parts_kernel(where, a, b, c, d0, d1, d2, away, kept, down):
     rows = away.shape[0] // 8
     mine = where[0]
 
-    def total(source):
-        return a[source, :].astype(F32) + b[source, :].astype(F32) + c[source, :].astype(F32)
+    def total(start, size, d, base):
+        source, shifted = pl.ds(start, size), pl.ds(start - base, size)
+        return (
+            a[source, :].astype(F32)
+            + b[source, :].astype(F32)
+            + c[source, :].astype(F32)
+            + d[shifted, :].astype(F32)
+        )
 
     for block in range(8):
         here = slice(block * rows, (block + 1) * rows)
         base = 2 * block * rows
-        own = pl.ds(pl.multiple_of(base + mine * rows, rows), rows)
-        other = pl.ds(pl.multiple_of(base + (1 - mine) * rows, rows), rows)
-        away[here, :] = total(other).astype(BF)
-        kept[here, :] = total(own)
+        d, cut = ((d0, 0), (d1, 8 * rows), (d2, 14 * rows))[(block > 3) + (block > 6)]
+        own = pl.multiple_of(base + mine * rows, rows)
+        other = pl.multiple_of(base + (1 - mine) * rows, rows)
+        away[here, :] = total(other, rows, d, cut).astype(BF)
+        kept[here, :] = total(own, rows, d, cut)
     for block in range(3):
         base = 16 * rows + block * 256
-        down[:, block * 256 : (block + 1) * 256] = total(slice(base, base + 256))
+        down[:, block * 256 : (block + 1) * 256] = total(base, 256, d2, 14 * rows)
 
 
 def unpack_kernel(where, kept, arrived, out):
@@ -221,14 +226,10 @@
 
 def across_major(parts, rows):
     pieces = [swap(parts[j * rows : (j + 1) * rows], "fsdp", 2 * j) for j in (1, 2, 3)]
-    return [parts[:rows]] + pieces
-
-
-def summed_up(pieces):
-    total = pieces[0].astype(F32)
-    for piece in pieces[1:]:
+    total = parts[:rows].astype(F32)
+    for piece in pieces:
         total += piece.astype(F32)
-    return total.astype(BF)
+    return total.astype(BF), pieces[0]
 
 
 def sequence_gather(values, across):
@@ -362,7 +363,7 @@
     total = jnp.sum(weights, axis=0, keepdims=True)
     weights = (weights * (1.0 / total)).astype(BF)
     kept[0] = weights
-    both = mm_tn(weights, v[...])
+    both = mm_tn(v[...], weights).T
     lane = lanes((count, PAIR))
     attended[...] = jnp.where(lane < HEAD, both[:count], both[count:]).astype(BF)
 
@@ -383,7 +384,7 @@
     dv[...] = grad_v
     grad_k = turned(mm(grad_scores, query), cosine[...], -sine[...]).astype(BF)
     dk[...] = grad_k
-    both = mm_tn(grad_scores, key_rows)
+    both = mm_tn(key_rows, grad_scores).T
     lane = lanes((count, PAIR))
     grad_q = jnp.where(lane < HEAD, both[:count], both[count:]) * HEAD ** (-0.5)
     mine = pl.ds(pl.multiple_of(own * count, count), count)
@@ -496,7 +497,7 @@
         grad_gate_up, grad_down = take(2)
     rows, grads, out_rows, back_rows, acts, grad_units = take(6)
     if packed:
-        gate_up, down = take(2)
+        gate_up, down, rows_t = take(3)
     width = rows.shape[1]
     total = 2 * groups * MOST
     index = 0
@@ -567,9 +568,10 @@
 
     def weight_grad(step, carry):
         block = pl.ds(pl.multiple_of(step * 512, 512), 512)
-        gate_up[:, block] = mm_tn(x, grad_units[:, block]).astype(BF)
+        gate_up[:, block] = mm(rows_t[...], grad_units[:, block]).astype(BF)
         return carry
 
+    rows_t[...] = x.T
     lax.fori_loop(0, 4, weight_grad, 0)
     for slot, ref in enumerate(messages):
         source = pl.ds(pl.multiple_of(where[slot] * part, part), part)
@@ -648,17 +650,14 @@
     grad_low = grad_back + direct * grad + mm_nt(high, weights) + mm_nt(rest, weights)
     scale = rms_scale(hidden)
     normed = hidden * scale
-    of_gain = split_low(grad_low * normed)
-    ones = (lane == gain_two_at).astype(BF)
+    of_gain = jnp.sum((grad_low * normed).reshape(-1, 8, normed.shape[1]), axis=0)
+    of_gain = jnp.sum(of_gain, axis=0, keepdims=True)
     value_high, value_rest = split_low(value_weights)
-    summed = (
-        mm_tn(low, high)
-        + mm_tn(low, rest)
-        + mm_tn(grad_low_type, value_high)
-        + mm_tn(grad_low_type, value_rest)
-        + mm_tn(of_gain[0], ones)
-        + mm_tn(of_gain[1], ones)
-    )
+    summed = mm_tn(low, jnp.concatenate([high, rest], axis=1))
+    summed += mm_tn(grad_low_type, jnp.concatenate([value_high, value_rest], axis=1))
+    summed = summed[:, :SMALL] + summed[:, SMALL:]
+    wide = (SMALL, normed.shape[1])
+    summed += jnp.where(rows_of(wide) == gain_two_at, of_gain, 0.0).T
     column, row = lanes(summed.shape), rows_of(summed.shape)
     mine = row // shard_rows == where[groups]
     for index, total in enumerate((jnp.sum(hidden * hidden), jnp.sum(outputs * outputs))):
@@ -943,6 +942,7 @@
         weights += (down, down_near, down_far, down_middle, down_onward)
         grads = [shaped((part.shape[0] + 3 * 256, 256), BF)] * 4
         room = [pltpu.VMEM((width, 2 * units), BF), pltpu.VMEM((units, width), BF)]
+        room += [pltpu.VMEM((width, 2 * groups * MOST), BF)]
     else:
         places = just_minor
         weights = (gate_up_half, down_half)
@@ -968,9 +968,12 @@
 
     if packed:
         first = along(grads[3], INWARD)
+        middle = along(grads[3], MIDDLE)
         sent = added(grads[2], first)
-        up, down_way = along(sent, UP[:2]), along(sent, DOWN[:2])
-        backs[0] = after(backs[0], sent)
+        near = along(after(grads[1], first), NEAR)
+        cuts = (0, 8 * shard_rows, 14 * shard_rows, sent.shape[0])
+        far = [along(sent[a:b], FAR) for a, b in zip(cuts, cuts[1:])]
+        backs[0] = after(backs[0], sent, middle)
     else:
         scatter = lambda v: lax.psum_scatter(
             v,
@@ -1057,10 +1060,8 @@
     dq_a, dk_a, dv_a, a_away, a_kept = attend_back(0, grad_att)
     if packed:
         a_away, a_kept, out_kept = lax.optimization_barrier(
-            (a_away, a_kept, out_kept, up, down_way)
+            (a_away, a_kept, out_kept, far[0], near)
         )[:3]
-        up = along(added(jnp.where(major == 1, grads[3], grads[1]), up), UP)
-        down_way = along(added(jnp.where(major == 2, grads[3], grads[1]), down_way), DOWN)
         out_both = added(out_kept, swap(out_away, "expert", 1))
         a_both = added(a_kept, swap(a_away, "expert", 1))
         grad_att = after(grad_att, a_both, out_both)
@@ -1080,16 +1081,15 @@
         )
 
     if packed:
+        b_away = after(b_away, far[1])
         out_sum, a_sum = along_chips(out_both, (b_kept,)), along_chips(a_both, (b_kept,))
         b_both = added(b_kept, swap(b_away, "expert", 1))
         dq_b = after(dq_b, b_both)
         b_sum = along_chips(b_both, ())
         parts_all = jnp.concatenate([a_sum, b_sum, out_sum], axis=1)
         rows_back, own_back = project_back(dq_b)
-        pieces = across_major(
-            after(parts_all, rows_back, up, down_way), shard_rows // 4
-        )
-        own_grads = after(grads[0], pieces[1])
+        total, piece = across_major(after(parts_all, rows_back), shard_rows // 4)
+        own_grads = after(grads[0], piece)
         away, kept, shard_down = call(
             sum_parts_kernel,
             [
@@ -1097,7 +1097,7 @@
                 shaped((8 * shard_rows, 256), F32),
                 shaped((256, width), F32),
             ],
-            (just_minor, own_grads, up, down_way),
+            (just_minor, own_grads, near, middle) + tuple(far),
             name="sum_parts",
             micros=3,
         )
@@ -1124,7 +1124,7 @@
     )
 
     if packed:
-        total = summed_up(pieces[:3] + [after(pieces[3], away)])
+        total = after(total, grad_tokens, shard_gate_up)
         total = jnp.concatenate([total, swap(total, "expert", 2)], axis=0)
         other = swap(total, "expert", 1)
     shared_grads = call(

time: 302 us -> 295 us (0.977)
  starting transfers between devices: 62.6 us -> 52.8 us
  waiting for transfers between devices: 102 us -> 107 us
  local copies, waits for them, and re-layouts: 12.6 us -> 16.8 us
    ppermute x13 -> x14, waiting for transfers between devices: 34.5 us -> 43.6 us  [along(): lax.ppermute(values, 'fsdp', [(2 * i + b, 2 * j + b) for i, j in pairs fo...]
    ppermute x37, starting transfers between devices: 36.5 us -> 31.4 us  [swap(): return lax.ppermute(values, axis, [(i, i ^ bits) for i in range(size)])]
    ppermute x37, waiting for transfers between devices: 67.9 us -> 63.2 us  [swap(): return lax.ppermute(values, axis, [(i, i ^ bits) for i in range(size)])]
    ppermute x13 -> x14, starting transfers between devices: 26.1 us -> 21.4 us  [along(): lax.ppermute(values, 'fsdp', [(2 * i + b, 2 * j + b) for i, j in pairs fo...]
    unnamed x63 -> x58, local copies, waits for them, and re-layouts: 7.31 us -> 9.02 us
  transfers between devices with their start and end apart: 50 -> 51, of which waited for: 23 -> 22; matrix products, arithmetic and copies ran while one was open for 7% -> 8% of each run, Pallas kernels for 28% -> 27%
where the time goes in v2:
time: 295 us; the launch traced here: 294 us
  waiting for transfers between devices  107 us (36%)
  Pallas kernels  106 us (36%)
  starting transfers between devices  52.8 us (18%)
  local copies, waits for them, and re-layouts  16.8 us (6%)
  other arithmetic  10.8 us (4%)
    pallas_call x15, Pallas kernels, call(): pl.pallas_call(kernel, out_shape=outs, grid_spec=pltpu.PrefetchScalarGrid...  106 us
    ppermute x37, waiting for transfers between devices, swap(): return lax.ppermute(values, axis, [(i, i ^ bits) for i in range(size)])  63.2 us
    ppermute x14, waiting for transfers between devices, along(): lax.ppermute(values, 'fsdp', [(2 * i + b, 2 * j + b) for i, j in pairs fo...  43.6 us
    ppermute x37, starting transfers between devices, swap(): return lax.ppermute(values, axis, [(i, i ^ bits) for i in range(size)])  31.4 us
    ppermute x14, starting transfers between devices, along(): lax.ppermute(values, 'fsdp', [(2 * i + b, 2 * j + b) for i, j in pairs fo...  21.4 us
    unnamed x58, local copies, waits for them, and re-layouts  9.02 us
  transfers between devices with their start and end apart: 51, of which 22 were waited for; matrix products, arithmetic and copies ran while one was open for 8% of the time, Pallas kernels for 27%

profile of v2, /device:TPU:0, one launch (start us, length us, event | category | flops | bytes accessed | tf_op | source)
XLA Modules:
  0.0 294.2 jit_solution(8505684288576959238)
XLA Ops:
  18.5 4.8 %collective-permute-done.2 = bf16[96,1664]{1,0:T(8,128)(2,1)S(1)} collective-permute-done((bf16[96,1664]{1,0:T(8,128)(2,1)}, bf16[96,1664]{1,0:T(8,128)(2,1)S(1)}, u32[]{:S(2)}, u32[]{:S(2)}) %collective-permute-start.2) | collective-permute-done | bytes 319520 | tf_op jit(solution)/shard_map/ppermute | solution.py:93
  24.8 5.8 %collective-permute-done.3 = bf16[96,1664]{1,0:T(8,128)(2,1)S(1)} collective-permute-done((bf16[96,1664]{1,0:T(8,128)(2,1)}, bf16[96,1664]{1,0:T(8,128)(2,1)S(1)}, u32[]{:S(2)}, u32[]{:S(2)}) %collective-permute-start.3) | collective-permute-done | bytes 319520 | tf_op jit(solution)/shard_map/ppermute | solution.py:93
  34.3 4.5 %collective-permute-start.11 = (bf16[256,768]{1,0:T(8,128)(2,1)S(1)}, bf16[256,768]{1,0:T(8,128)(2,1)}, u32[]{:S(2)}, u32[]{:S(2)}) collective-permute-start(bf16[256,768]{1,0:T(8,128)(2,1)S(1)} %bitcast.57), channel_id=1, source_target_pairs={{0,4},{1,5},{4,0},{5,1},{2,6},{3,7},{6,2},{7,3},{8,12},{9,13},{12,... | collective-permute-start | bytes 1179656 | tf_op jit(solution)/shard_map/ppermute | solution.py:97
  42.4 7.1 %collective-permute-done.9 = bf16[96,1664]{1,0:T(8,128)(2,1)S(1)} collective-permute-done((bf16[96,1664]{1,0:T(8,128)(2,1)S(1)}, bf16[96,1664]{1,0:T(8,128)(2,1)S(1)}, u32[]{:S(2)}, u32[]{:S(2)}) %collective-permute-start.9) | collective-permute-done | bytes 319520 | tf_op jit(solution)/shard_map/ppermute | solution.py:93
  50.3 6.4 %collective-permute-done.11.refs_13_ = bf16[256,768]{1,0:T(8,128)(2,1)} collective-permute-done((bf16[256,768]{1,0:T(8,128)(2,1)S(1)}, bf16[256,768]{1,0:T(8,128)(2,1)}, u32[]{:S(2)}, u32[]{:S(2)}) %collective-permute-start.11) | collective-permute-done | bytes 393248 | tf_op jit(solution)/shard_map/ppermute | solution.py:97
  65.1 11.1 %project.1 = (bf16[256,768]{1,0:T(8,128)(2,1)}, bf16[1024,768]{1,0:T(8,128)(2,1)}, bf16[1024,768]{1,0:T(8,128)(2,1)}, bf16[768,1024]{1,0:T(8,128)(2,1)}, bf16[76...) custom-call(s32[14]{0:T(128)} %stack.129.where, ...), custom_call_target="tpu_custom_call" | custom-call | flops 900000000 | bytes 3000000 | tf_op jit(solution)/shard_map/project/pallas_call | solution.py:69
  76.1 10.2 %attend.1 = (bf16[256,768]{1,0:T(8,128)(2,1)}, bf16[6,1024,512]{2,1,0:T(8,128)(2,1)}) custom-call(s32[14]{0:T(128)} %stack.129.where, bf16[256,768]{1,0:T(8,128)(2,1)} %get-tuple-element.97.q, bf16[1024,768]{1,0:T(8,128)(2,1)} %get-tuple-element.98.k, bf16[1024,768]{1,0:T(8,128)(2,1)} %get-tuple-element.99.v), custom_call_target="tpu_custom_call" | custom-call | flops 1080000000 | bytes 3600000 | tf_op jit(solution)/shard_map/attend/pallas_call | solution.py:69
  86.3 5.0 %route.1 = (f32[256,768]{1,0:T(8,128)}, bf16[256,768]{1,0:T(8,128)(2,1)}, bf16[160,768]{1,0:T(8,128)(2,1)}, bf16[160,768]{1,0:T(8,128)(2,1)}, bf16[160,768]{1,0:T(8,128)(2,1)}, /*index=5*/bf16[160,768]{1,0:T(8,128)(2,1)}) custom-call(s32[15]{0:T(128)} %stack.121.where, bf16[256,768]{1,0:T(8,128)(2,1)} %get-tuple-element.102.att.refs_12_, ...), custom_call_target="tpu_custom_call" | custom-call | flops 450000000 | bytes 1500000 | tf_op jit(solution)/shard_map/route/pallas_call | solution.py:69
  97.6 8.9 %collective-permute-done.21.refs_7_ = bf16[1536,256]{1,0:T(8,128)(2,1)S(1)} collective-permute-done((bf16[1536,256]{1,0:T(8,128)(2,1)S(1)}, bf16[1536,256]{1,0:T(8,128)(2,1)S(1)}, u32[]{:S(2)}, u32[]{:S(2)}) %collective-permute-start.21) | collective-permute-done | bytes 786464 | tf_op jit(solution)/shard_map/ppermute | solution.py:97
  111.5 17.8 %collective-permute-done.23.refs_10_ = bf16[1536,256]{1,0:T(8,128)(2,1)} collective-permute-done((bf16[1536,256]{1,0:T(8,128)(2,1)S(1)}, bf16[1536,256]{1,0:T(8,128)(2,1)}, u32[]{:S(2)}, u32[]{:S(2)}) %collective-permute-start.23) | collective-permute-done | bytes 786464 | tf_op jit(solution)/shard_map/ppermute | solution.py:97
  129.3 19.5 %expert.1 = (f32[320,768]{1,0:T(8,128)}, f32[320,768]{1,0:T(8,128)}, bf16[320,768]{1,0:T(8,128)(2,1)}, bf16[320,768]{1,0:T(8,128)(2,1)}, bf16[2304,256]{1,0:T(8,...) custom-call(s32[5]{0:T(128)} %stack.128.where, ...), custom_call_target="tpu_custom_call" | custom-call | flops 1620000000 | bytes 5400000 | tf_op jit(solution)/shard_map/expert/pallas_call | solution.py:69
  153.1 10.2 %collective-permute-done.27 = bf16[320,768]{1,0:T(8,128)(2,1)S(1)} collective-permute-done((bf16[320,768]{1,0:T(8,128)(2,1)}, bf16[320,768]{1,0:T(8,128)(2,1)S(1)}, u32[]{:S(2)}, u32[]{:S(2)}) %collective-permute-start.27) | collective-permute-done | bytes 491552 | tf_op jit(solution)/shard_map/ppermute | solution.py:93
  166.1 5.6 %collective-permute-done.24 = bf16[320,768]{1,0:T(8,128)(2,1)S(1)} collective-permute-done((bf16[320,768]{1,0:T(8,128)(2,1)}, bf16[320,768]{1,0:T(8,128)(2,1)S(1)}, u32[]{:S(2)}, u32[]{:S(2)}) %collective-permute-start.24) | collective-permute-done | bytes 491552 | tf_op jit(solution)/shard_map/ppermute | solution.py:93
  181.0 9.9 %combine.1 = (bf16[256,768]{1,0:T(8,128)(2,1)}, f32[256,768]{1,0:T(8,128)}, bf16[256,768]{1,0:T(8,128)(2,1)}, bf16[384,896]{1,0:T(8,128)(2,1)}, bf16[384,896]{1,0:T(8,128)(2,1)}, /*index=5*/bf16[8,256]{1,0:T(8,128)(2,1)}) custom-call(s32[15]{0:T(128)} %stack.121.where, bf16[160,768]{1,0:T(8,128)(2,1)} %get-tuple-element.119.refs_0_, ...), custom_call_target="tpu_custom_call" | custom-call | flops 900000000 | bytes 3000000 | tf_op jit(solution)/shard_map/combine/pallas_call | solution.py:69
  191.7 12.4 %attend_back.2 = (bf16[256,384]{1,0:T(8,128)(2,1)}, bf16[1024,384]{1,0:T(8,128)(2,1)}, bf16[1024,384]{1,0:T(8,128)(2,1)}, bf16[384,1152]{1,0:T(8,128)(2,1)}, bf16[384,1152]{1,0:T(8,128)(2,1)}) custom-call(s32[15]{0:T(128)} %stack.131.where, bf16[256,768]{1,0:T(8,128)(2,1)} %get-tuple-element.97.q, bf16[1024,768]{1,0:T(8,128)(2,1)} %get-tuple-element.98.k, ...), custom_call_target="tpu_custom_call" | custom-call | flops 990000000 | bytes 3300000 | tf_op jit(solution)/shard_map/attend_back/pallas_call | solution.py:69
  204.1 6.7 %collective-permute-done.30.d0 = bf16[768,256]{1,0:T(8,128)(2,1)S(1)} collective-permute-done((bf16[768,256]{1,0:T(8,128)(2,1)}, bf16[768,256]{1,0:T(8,128)(2,1)S(1)}, u32[]{:S(2)}, u32[]{:S(2)}) %collective-permute-start.30) | collective-permute-done | bytes 393248 | tf_op jit(solution)/shard_map/ppermute | solution.py:97
  216.9 12.1 %attend_back.3 = (bf16[256,384]{1,0:T(8,128)(2,1)}, bf16[1024,384]{1,0:T(8,128)(2,1)}, bf16[1024,384]{1,0:T(8,128)(2,1)}, bf16[384,1152]{1,0:T(8,128)(2,1)}, bf16[384,1152]{1,0:T(8,128)(2,1)}) custom-call(s32[15]{0:T(128)} %stack.131.where, bf16[256,768]{1,0:T(8,128)(2,1)} %get-tuple-element.97.q, bf16[1024,768]{1,0:T(8,128)(2,1)} %get-tuple-element.98.k, ...), custom_call_target="tpu_custom_call" | custom-call | flops 990000000 | bytes 3300000 | tf_op jit(solution)/shard_map/attend_back/pallas_call | solution.py:69
  231.6 4.3 %collective-permute-done.43 = bf16[96,896]{1,0:T(8,128)(2,1)} collective-permute-done((bf16[96,896]{1,0:T(8,128)(2,1)S(1)}, bf16[96,896]{1,0:T(8,128)(2,1)}, u32[]{:S(2)}, u32[]{:S(2)}) %collective-permute-start.43) | collective-permute-done | bytes 172064 | tf_op jit(solution)/shard_map/ppermute | solution.py:93
  236.9 4.3 %collective-permute-done.38 = bf16[192,1152]{1,0:T(8,128)(2,1)S(1)} collective-permute-done((bf16[192,1152]{1,0:T(8,128)(2,1)S(1)}, bf16[192,1152]{1,0:T(8,128)(2,1)S(1)}, u32[]{:S(2)}, u32[]{:S(2)}) %collective-permute-start.38) | collective-permute-done | bytes 442400 | tf_op jit(solution)/shard_map/ppermute | solution.py:93
  242.8 5.0 %collective-permute-done.39 = bf16[96,1152]{1,0:T(8,128)(2,1)S(1)} collective-permute-done((bf16[96,1152]{1,0:T(8,128)(2,1)S(1)}, bf16[96,1152]{1,0:T(8,128)(2,1)S(1)}, u32[]{:S(2)}, u32[]{:S(2)}) %collective-permute-start.39) | collective-permute-done | bytes 221216 | tf_op jit(solution)/shard_map/ppermute | solution.py:93
  247.8 7.7 %project_back.1 = (bf16[1024,768]{1,0:T(8,128)(2,1)}, f32[256,768]{1,0:T(8,128)}) custom-call(s32[15]{0:T(128)} %stack.131.where, bf16[256,384]{1,0:T(8,128)(2,1)} %get-tuple-element.128.refs_0_, bf16[256,384]{1,0:T(8,128)(2,1)} %get-tuple-element.143.refs_1_, bf16[1024,384]{1,0:T(8,128)(2,1)} %get-tuple-element.144.refs_2_, ...), custom_call_target="tpu_custom_call" | custom-call | flops 540000000 | bytes 1800000 | tf_op jit(solution)/shard_map/project_back/pallas_call | solution.py:69
  257.2 4.7 %collective-permute-done.41 = bf16[96,1152]{1,0:T(8,128)(2,1)S(1)} collective-permute-done((bf16[96,1152]{1,0:T(8,128)(2,1)S(1)}, bf16[96,1152]{1,0:T(8,128)(2,1)S(1)}, u32[]{:S(2)}, u32[]{:S(2)}) %collective-permute-start.41) | collective-permute-done | bytes 221216 | tf_op jit(solution)/shard_map/ppermute | solution.py:93
  268.6 3.9 %sum_parts.1 = (bf16[768,256]{1,0:T(8,128)(2,1)}, f32[768,256]{1,0:T(8,128)}, f32[256,768]{1,0:T(8,128)}) custom-call(s32[1]{0:T(128)} %bitcast.25.where, bf16[2304,256]{1,0:T(8,128)(2,1)} %get-tuple-element.155.a, bf16[2304,256]{1,0:T(8,128)(2,1)} %collective-permute-done.31.b, bf16[2304,256]{1,0:T(8,128)(2,1)} %copy-done.5, bf16[768,256]{1,0:T(8,128)(2,1)} %copy-done.21, ...), custom_call_target="tpu_custom_call" | custom-call | flops 270000000 | bytes 900000 | tf_op jit(solution)/shard_map/sum_parts/pallas_call | solution.py:69
  273.0 3.9 %collective-permute-done.45 = bf16[24,3200]{1,0:T(8,128)(2,1)S(1)} collective-permute-done((bf16[24,3200]{1,0:T(8,128)(2,1)S(1)}, bf16[24,3200]{1,0:T(8,128)(2,1)S(1)}, u32[]{:S(2)}, u32[]{:S(2)}) %collective-permute-start.45) | collective-permute-done | bytes 153632 | tf_op jit(solution)/shard_map/ppermute | solution.py:93
  (196 shorter events, 101.2 us)
Async XLA Ops:
  2.6 15.7 %collective-permute-start.4 = (bf16[96,1664]{1,0:T(8,128)(2,1)}, bf16[96,1664]{1,0:T(8,128)(2,1)S(1)}, u32[]{:S(2)}, u32[]{:S(2)}) collective-permute-start(bf16[96,1664]{1,0:T(8,128)(2,1)} %pack_shared.1), channel_id=1, source_target_pairs={{0,1},{1,0},{2,3},{3,2},{4,5},{5,4},{6,7},{7,6},{8,9},{9,8},{10,11... | collective-permute-start | bytes 958472 | tf_op jit(solution)/shard_map/ppermute | solution.py:93
  5.5 25.0 %collective-permute-start.3 = (bf16[96,1664]{1,0:T(8,128)(2,1)}, bf16[96,1664]{1,0:T(8,128)(2,1)S(1)}, u32[]{:S(2)}, u32[]{:S(2)}) collective-permute-start(bf16[96,1664]{1,0:T(8,128)(2,1)} %pack_shared.1), channel_id=1, source_target_pairs={{0,4},{1,5},{2,6},{3,7},{4,0},{5,1},{6,2},{7,3},{8,12},{9,13},{10,... | collective-permute-start | bytes 958472 | tf_op jit(solution)/shard_map/ppermute | solution.py:93
  8.1 15.2 %collective-permute-start.2 = (bf16[96,1664]{1,0:T(8,128)(2,1)}, bf16[96,1664]{1,0:T(8,128)(2,1)S(1)}, u32[]{:S(2)}, u32[]{:S(2)}) collective-permute-start(bf16[96,1664]{1,0:T(8,128)(2,1)} %pack_shared.1), channel_id=1, source_target_pairs={{0,2},{1,3},{2,0},{3,1},{4,6},{5,7},{6,4},{7,5},{8,10},{9,11},{10,... | collective-permute-start | bytes 958472 | tf_op jit(solution)/shard_map/ppermute | solution.py:93
  11.6 19.7 %collective-permute-start.7 = (bf16[768,256]{1,0:T(8,128)(2,1)}, bf16[768,256]{1,0:T(8,128)(2,1)S(1)}, u32[]{:S(2)}, u32[]{:S(2)}) collective-permute-start(bf16[768,256]{1,0:T(8,128)(2,1)} %blocks.1), channel_id=1, source_target_pairs={{0,1},{1,0},{2,3},{3,2},{4,5},{5,4},{6,7},{7,6},{8,9},{9,8},{10,11... | collective-permute-start | bytes 1179656 | tf_op jit(solution)/shard_map/ppermute | solution.py:93
  18.3 16.0 %collective-permute-start.5 = (bf16[96,1664]{1,0:T(8,128)(2,1)S(1)}, bf16[96,1664]{1,0:T(8,128)(2,1)S(1)}, u32[]{:S(2)}, u32[]{:S(2)}) collective-permute-start(bf16[96,1664]{1,0:T(8,128)(2,1)S(1)} %copy-done.4), channel_id=1, source_target_pairs={{0,6},{1,7},{2,4},{3,5},{4,2},{5,3},{6,0},{7,1},{8,14},{9,15},{10,... | collective-permute-start | bytes 958472 | tf_op jit(solution)/shard_map/ppermute | solution.py:93
  23.3 17.0 %collective-permute-start.6 = (bf16[96,1664]{1,0:T(8,128)(2,1)S(1)}, bf16[96,1664]{1,0:T(8,128)(2,1)S(1)}, u32[]{:S(2)}, u32[]{:S(2)}) collective-permute-start(bf16[96,1664]{1,0:T(8,128)(2,1)S(1)} %collective-permute-done.2), channel_id=1, source_target_pairs={{0,1},{1,0},{2,3},{3,2},{4,5},{5,4},{6,7},{7,6},{8,9},{9,8},{10,11... | collective-permute-start | bytes 958472 | tf_op jit(solution)/shard_map/ppermute | solution.py:93
  23.9 16.4 %collective-permute-start.1 = (bf16[512,768]{1,0:T(8,128)(2,1)S(1)}, bf16[512,768]{1,0:T(8,128)(2,1)S(1)}, u32[]{:S(2)}, u32[]{:S(2)}) collective-permute-start(bf16[512,768]{1,0:T(8,128)(2,1)S(1)} %pad_maximum_fusion.refs_0_), channel_id=1, source_target_pairs={{0,8},{8,0},{16,24},{24,16},{1,9},{9,1},{17,25},{25,17},{2,10},{10... | collective-permute-start | bytes 2359304 | tf_op jit(solution)/shard_map/ppermute | solution.py:93
  34.3 22.4 %collective-permute-start.11 = (bf16[256,768]{1,0:T(8,128)(2,1)S(1)}, bf16[256,768]{1,0:T(8,128)(2,1)}, u32[]{:S(2)}, u32[]{:S(2)}) collective-permute-start(bf16[256,768]{1,0:T(8,128)(2,1)S(1)} %bitcast.57), channel_id=1, source_target_pairs={{0,4},{1,5},{4,0},{5,1},{2,6},{3,7},{6,2},{7,3},{8,12},{9,13},{12,... | collective-permute-start | bytes 1179656 | tf_op jit(solution)/shard_map/ppermute | solution.py:97
  38.8 18.9 %collective-permute-start.10 = (bf16[256,768]{1,0:T(8,128)(2,1)S(1)}, bf16[256,768]{1,0:T(8,128)(2,1)S(1)}, u32[]{:S(2)}, u32[]{:S(2)}) collective-permute-start(bf16[256,768]{1,0:T(8,128)(2,1)S(1)} %bitcast.58), channel_id=1, source_target_pairs={{0,2},{1,3},{2,0},{3,1},{4,6},{5,7},{6,4},{7,5},{8,10},{9,11},{10,... | collective-permute-start | bytes 1179656 | tf_op jit(solution)/shard_map/ppermute | solution.py:97
  57.7 28.6 %collective-permute-start.14 = (bf16[256,768]{1,0:T(8,128)(2,1)S(1)}, bf16[256,768]{1,0:T(8,128)(2,1)}, u32[]{:S(2)}, u32[]{:S(2)}) collective-permute-start(bf16[256,768]{1,0:T(8,128)(2,1)S(1)} %bitcast.59), channel_id=1, source_target_pairs={{2,4},{3,5},{4,2},{5,3},{10,12},{11,13},{12,10},{13,11},{18,20},{1... | collective-permute-start | bytes 1179656 | tf_op jit(solution)/shard_map/ppermute | solution.py:97
  59.1 27.2 %collective-permute-start.13 = (bf16[256,768]{1,0:T(8,128)(2,1)}, bf16[256,768]{1,0:T(8,128)(2,1)}, u32[]{:S(2)}, u32[]{:S(2)}) collective-permute-start(bf16[256,768]{1,0:T(8,128)(2,1)} %collective-permute-done.11.refs_13_), channel_id=1, source_target_pairs={{4,6},{5,7},{2,0},{3,1},{12,14},{13,15},{10,8},{11,9},{20,22},{21,... | collective-permute-start | bytes 1179656 | tf_op jit(solution)/shard_map/ppermute | solution.py:97
  61.7 44.7 %collective-permute-start.21 = (bf16[1536,256]{1,0:T(8,128)(2,1)S(1)}, bf16[1536,256]{1,0:T(8,128)(2,1)S(1)}, u32[]{:S(2)}, u32[]{:S(2)}) collective-permute-start(bf16[1536,256]{1,0:T(8,128)(2,1)S(1)} %copy-done.2), channel_id=1, source_target_pairs={{0,2},{1,3},{2,0},{3,1},{4,6},{5,7},{6,4},{7,5},{8,10},{9,11},{10,... | collective-permute-start | bytes 2359304 | tf_op jit(solution)/shard_map/ppermute | solution.py:97
  65.1 41.4 %collective-permute-start.20 = (bf16[1536,256]{1,0:T(8,128)(2,1)S(1)}, bf16[1536,256]{1,0:T(8,128)(2,1)S(1)}, u32[]{:S(2)}, u32[]{:S(2)}) collective-permute-start(bf16[1536,256]{1,0:T(8,128)(2,1)S(1)} %copy-done.2), channel_id=1, source_target_pairs={{0,4},{1,5},{4,0},{5,1},{2,6},{3,7},{6,2},{7,3},{8,12},{9,13},{12,... | collective-permute-start | bytes 2359304 | tf_op jit(solution)/shard_map/ppermute | solution.py:97
  94.1 16.2 %collective-permute-start.18 = (bf16[320,768]{1,0:T(8,128)(2,1)S(1)}, bf16[320,768]{1,0:T(8,128)(2,1)}, u32[]{:S(2)}, u32[]{:S(2)}) collective-permute-start(bf16[320,768]{1,0:T(8,128)(2,1)S(1)} %pad_maximum_fusion.5), channel_id=1, source_target_pairs={{0,1},{1,0},{2,3},{3,2},{4,5},{5,4},{6,7},{7,6},{8,9},{9,8},{10,11... | collective-permute-start | bytes 1474568 | tf_op jit(solution)/shard_map/ppermute | solution.py:93
  108.0 21.3 %collective-permute-start.23 = (bf16[1536,256]{1,0:T(8,128)(2,1)S(1)}, bf16[1536,256]{1,0:T(8,128)(2,1)}, u32[]{:S(2)}, u32[]{:S(2)}) collective-permute-start(bf16[1536,256]{1,0:T(8,128)(2,1)S(1)} %collective-permute-done.20.refs_8_), channel_id=1, source_target_pairs={{4,6},{5,7},{2,0},{3,1},{12,14},{13,15},{10,8},{11,9},{20,22},{21,... | collective-permute-start | bytes 2359304 | tf_op jit(solution)/shard_map/ppermute | solution.py:97
  110.3 19.0 %collective-permute-start.19 = (bf16[320,768]{1,0:T(8,128)(2,1)}, bf16[320,768]{1,0:T(8,128)(2,1)}, u32[]{:S(2)}, u32[]{:S(2)}) collective-permute-start(bf16[320,768]{1,0:T(8,128)(2,1)} %pad_maximum_fusion.6), channel_id=1, source_target_pairs={{0,1},{1,0},{2,3},{3,2},{4,5},{5,4},{6,7},{7,6},{8,9},{9,8},{10,11... | collective-permute-start | bytes 1474568 | tf_op jit(solution)/shard_map/ppermute | solution.py:93
  149.4 22.3 %collective-permute-start.24 = (bf16[320,768]{1,0:T(8,128)(2,1)}, bf16[320,768]{1,0:T(8,128)(2,1)S(1)}, u32[]{:S(2)}, u32[]{:S(2)}) collective-permute-start(bf16[320,768]{1,0:T(8,128)(2,1)} %get-tuple-element.116), channel_id=1, source_target_pairs={{0,1},{1,0},{2,3},{3,2},{4,5},{5,4},{6,7},{7,6},{8,9},{9,8},{10,11... | collective-permute-start | bytes 1474568 | tf_op jit(solution)/shard_map/ppermute | solution.py:93
  150.9 25.7 %collective-permute-start.25 = (bf16[2304,256]{1,0:T(8,128)(2,1)}, bf16[2304,256]{1,0:T(8,128)(2,1)S(1)}, u32[]{:S(2)}, u32[]{:S(2)}) collective-permute-start(bf16[2304,256]{1,0:T(8,128)(2,1)} %get-tuple-element.118), channel_id=1, source_target_pairs={{0,2},{1,3},{6,4},{7,5},{8,10},{9,11},{14,12},{15,13},{16,18},{17,... | collective-permute-start | bytes 3538952 | tf_op jit(solution)/shard_map/ppermute | solution.py:97
  152.3 27.7 %collective-permute-start.26 = (bf16[2304,256]{1,0:T(8,128)(2,1)}, bf16[2304,256]{1,0:T(8,128)(2,1)S(1)}, u32[]{:S(2)}, u32[]{:S(2)}) collective-permute-start(bf16[2304,256]{1,0:T(8,128)(2,1)} %get-tuple-element.118), channel_id=1, source_target_pairs={{2,4},{3,5},{4,2},{5,3},{10,12},{11,13},{12,10},{13,11},{18,20},{1... | collective-permute-start | bytes 3538952 | tf_op jit(solution)/shard_map/ppermute | solution.py:97
  176.6 35.1 %collective-permute-start.31 = (bf16[2304,256]{1,0:T(8,128)(2,1)}, bf16[2304,256]{1,0:T(8,128)(2,1)}, u32[]{:S(2)}, u32[]{:S(2)}) collective-permute-start(bf16[2304,256]{1,0:T(8,128)(2,1)} %get-tuple-element.133), channel_id=1, source_target_pairs={{0,2},{1,3},{2,0},{3,1},{4,6},{5,7},{6,4},{7,5},{8,10},{9,11},{10,... | collective-permute-start | bytes 3538952 | tf_op jit(solution)/shard_map/ppermute | solution.py:97
  180.0 30.7 %collective-permute-start.30 = (bf16[768,256]{1,0:T(8,128)(2,1)}, bf16[768,256]{1,0:T(8,128)(2,1)S(1)}, u32[]{:S(2)}, u32[]{:S(2)}) collective-permute-start(bf16[768,256]{1,0:T(8,128)(2,1)} %slice.115), channel_id=1, source_target_pairs={{0,4},{1,5},{4,0},{5,1},{2,6},{3,7},{6,2},{7,3},{8,12},{9,13},{12,... | collective-permute-start | bytes 1179656 | tf_op jit(solution)/shard_map/ppermute | solution.py:97
  190.9 23.9 %collective-permute-start.33 = (bf16[384,896]{1,0:T(8,128)(2,1)}, bf16[384,896]{1,0:T(8,128)(2,1)S(1)}, u32[]{:S(2)}, u32[]{:S(2)}) collective-permute-start(bf16[384,896]{1,0:T(8,128)(2,1)} %get-tuple-element.137), channel_id=1, source_target_pairs={{0,8},{8,0},{16,24},{24,16},{1,9},{9,1},{17,25},{25,17},{2,10},{10... | collective-permute-start | bytes 2064392 | tf_op jit(solution)/shard_map/ppermute | solution.py:93
  212.4 19.1 %collective-permute-start.34 = (bf16[576,256]{1,0:T(8,128)(2,1)}, bf16[576,256]{1,0:T(8,128)(2,1)}, u32[]{:S(2)}, u32[]{:S(2)}) collective-permute-start(bf16[576,256]{1,0:T(8,128)(2,1)} %slice.116), channel_id=1, source_target_pairs={{0,4},{1,5},{4,0},{5,1},{2,6},{3,7},{6,2},{7,3},{8,12},{9,13},{12,... | collective-permute-start | bytes 884744 | tf_op jit(solution)/shard_map/ppermute | solution.py:97
  230.5 37.4 %collective-permute-start.47 = (bf16[960,256]{1,0:T(8,128)(2,1)S(1)}, bf16[960,256]{1,0:T(8,128)(2,1)S(1)}, u32[]{:S(2)}, u32[]{:S(2)}) collective-permute-start(bf16[960,256]{1,0:T(8,128)(2,1)S(1)} %slice.131), channel_id=1, source_target_pairs={{0,4},{1,5},{4,0},{5,1},{2,6},{3,7},{6,2},{7,3},{8,12},{9,13},{12,... | collective-permute-start | bytes 1474568 | tf_op jit(solution)/shard_map/ppermute | solution.py:97
  (52 other events, 540.8 us)

commit v3 on v2

--- a/solution.py
+++ b/solution.py
@@ -1124,7 +1124,7 @@
     )
 
     if packed:
-        total = after(total, grad_tokens, shard_gate_up)
+        total = after(total, grad_tokens)
         total = jnp.concatenate([total, swap(total, "expert", 2)], axis=0)
         other = swap(total, "expert", 1)
     shared_grads = call(

time: 295 us -> 293 us (level)
  transfers between devices with their start and end apart: 51 -> 51, of which waited for: 22 -> 21; matrix products, arithmetic and copies ran while one was open for 8% -> 8% of each run, Pallas kernels for 27% -> 28%
where the time goes in v3:
time: 293 us
  Pallas kernels  106 us (36%)
  waiting for transfers between devices  106 us (36%)
  starting transfers between devices  51.8 us (18%)
  local copies, waits for them, and re-layouts  16.8 us (6%)
  other arithmetic  10.8 us (4%)
    pallas_call x15, Pallas kernels, call(): pl.pallas_call(kernel, out_shape=outs, grid_spec=pltpu.PrefetchScalarGrid...  106 us
    ppermute x37, waiting for transfers between devices, swap(): return lax.ppermute(values, axis, [(i, i ^ bits) for i in range(size)])  62.6 us
    ppermute x14, waiting for transfers between devices, along(): lax.ppermute(values, 'fsdp', [(2 * i + b, 2 * j + b) for i, j in pairs fo...  43.6 us
    ppermute x37, starting transfers between devices, swap(): return lax.ppermute(values, axis, [(i, i ^ bits) for i in range(size)])  30.4 us
    ppermute x14, starting transfers between devices, along(): lax.ppermute(values, 'fsdp', [(2 * i + b, 2 * j + b) for i, j in pairs fo...  21.4 us
    unnamed x58, local copies, waits for them, and re-layouts  9 us
  transfers between devices with their start and end apart: 51, of which 21 were waited for; matrix products, arithmetic and copies ran while one was open for 8% of the time, Pallas kernels for 28%

profile of v3, /device:TPU:0, one launch (start us, length us, event | category | flops | bytes accessed | tf_op | source)
XLA Modules:
  0.0 292.6 jit_solution(14744501065922124148)
XLA Ops:
  18.5 4.8 %collective-permute-done.2 = bf16[96,1664]{1,0:T(8,128)(2,1)S(1)} collective-permute-done((bf16[96,1664]{1,0:T(8,128)(2,1)}, bf16[96,1664]{1,0:T(8,128)(2,1)S(1)}, u32[]{:S(2)}, u32[]{:S(2)}) %collective-permute-start.2) | collective-permute-done | bytes 319520 | tf_op jit(solution)/shard_map/ppermute | solution.py:93
  24.8 5.8 %collective-permute-done.3 = bf16[96,1664]{1,0:T(8,128)(2,1)S(1)} collective-permute-done((bf16[96,1664]{1,0:T(8,128)(2,1)}, bf16[96,1664]{1,0:T(8,128)(2,1)S(1)}, u32[]{:S(2)}, u32[]{:S(2)}) %collective-permute-start.3) | collective-permute-done | bytes 319520 | tf_op jit(solution)/shard_map/ppermute | solution.py:93
  34.3 4.5 %collective-permute-start.11 = (bf16[256,768]{1,0:T(8,128)(2,1)S(1)}, bf16[256,768]{1,0:T(8,128)(2,1)}, u32[]{:S(2)}, u32[]{:S(2)}) collective-permute-start(bf16[256,768]{1,0:T(8,128)(2,1)S(1)} %bitcast.57), channel_id=1, source_target_pairs={{0,4},{1,5},{4,0},{5,1},{2,6},{3,7},{6,2},{7,3},{8,12},{9,13},{12,... | collective-permute-start | bytes 1179656 | tf_op jit(solution)/shard_map/ppermute | solution.py:97
  42.4 7.1 %collective-permute-done.9 = bf16[96,1664]{1,0:T(8,128)(2,1)S(1)} collective-permute-done((bf16[96,1664]{1,0:T(8,128)(2,1)S(1)}, bf16[96,1664]{1,0:T(8,128)(2,1)S(1)}, u32[]{:S(2)}, u32[]{:S(2)}) %collective-permute-start.9) | collective-permute-done | bytes 319520 | tf_op jit(solution)/shard_map/ppermute | solution.py:93
  50.3 6.4 %collective-permute-done.11.refs_13_ = bf16[256,768]{1,0:T(8,128)(2,1)} collective-permute-done((bf16[256,768]{1,0:T(8,128)(2,1)S(1)}, bf16[256,768]{1,0:T(8,128)(2,1)}, u32[]{:S(2)}, u32[]{:S(2)}) %collective-permute-start.11) | collective-permute-done | bytes 393248 | tf_op jit(solution)/shard_map/ppermute | solution.py:97
  65.1 11.1 %project.1 = (bf16[256,768]{1,0:T(8,128)(2,1)}, bf16[1024,768]{1,0:T(8,128)(2,1)}, bf16[1024,768]{1,0:T(8,128)(2,1)}, bf16[768,1024]{1,0:T(8,128)(2,1)}, bf16[76...) custom-call(s32[14]{0:T(128)} %stack.129.where, ...), custom_call_target="tpu_custom_call" | custom-call | flops 900000000 | bytes 3000000 | tf_op jit(solution)/shard_map/project/pallas_call | solution.py:69
  76.1 10.2 %attend.1 = (bf16[256,768]{1,0:T(8,128)(2,1)}, bf16[6,1024,512]{2,1,0:T(8,128)(2,1)}) custom-call(s32[14]{0:T(128)} %stack.129.where, bf16[256,768]{1,0:T(8,128)(2,1)} %get-tuple-element.97.q, bf16[1024,768]{1,0:T(8,128)(2,1)} %get-tuple-element.98.k, bf16[1024,768]{1,0:T(8,128)(2,1)} %get-tuple-element.99.v), custom_call_target="tpu_custom_call" | custom-call | flops 1080000000 | bytes 3600000 | tf_op jit(solution)/shard_map/attend/pallas_call | solution.py:69
  86.3 5.0 %route.1 = (f32[256,768]{1,0:T(8,128)}, bf16[256,768]{1,0:T(8,128)(2,1)}, bf16[160,768]{1,0:T(8,128)(2,1)}, bf16[160,768]{1,0:T(8,128)(2,1)}, bf16[160,768]{1,0:T(8,128)(2,1)}, /*index=5*/bf16[160,768]{1,0:T(8,128)(2,1)}) custom-call(s32[15]{0:T(128)} %stack.121.where, bf16[256,768]{1,0:T(8,128)(2,1)} %get-tuple-element.102.att.refs_12_, ...), custom_call_target="tpu_custom_call" | custom-call | flops 450000000 | bytes 1500000 | tf_op jit(solution)/shard_map/route/pallas_call | solution.py:69
  97.6 8.9 %collective-permute-done.21.refs_7_ = bf16[1536,256]{1,0:T(8,128)(2,1)S(1)} collective-permute-done((bf16[1536,256]{1,0:T(8,128)(2,1)S(1)}, bf16[1536,256]{1,0:T(8,128)(2,1)S(1)}, u32[]{:S(2)}, u32[]{:S(2)}) %collective-permute-start.21) | collective-permute-done | bytes 786464 | tf_op jit(solution)/shard_map/ppermute | solution.py:97
  111.5 17.8 %collective-permute-done.23.refs_10_ = bf16[1536,256]{1,0:T(8,128)(2,1)} collective-permute-done((bf16[1536,256]{1,0:T(8,128)(2,1)S(1)}, bf16[1536,256]{1,0:T(8,128)(2,1)}, u32[]{:S(2)}, u32[]{:S(2)}) %collective-permute-start.23) | collective-permute-done | bytes 786464 | tf_op jit(solution)/shard_map/ppermute | solution.py:97
  129.3 19.5 %expert.1 = (f32[320,768]{1,0:T(8,128)}, f32[320,768]{1,0:T(8,128)}, bf16[320,768]{1,0:T(8,128)(2,1)}, bf16[320,768]{1,0:T(8,128)(2,1)}, bf16[2304,256]{1,0:T(8,...) custom-call(s32[5]{0:T(128)} %stack.128.where, ...), custom_call_target="tpu_custom_call" | custom-call | flops 1620000000 | bytes 5400000 | tf_op jit(solution)/shard_map/expert/pallas_call | solution.py:69
  153.1 10.2 %collective-permute-done.27 = bf16[320,768]{1,0:T(8,128)(2,1)S(1)} collective-permute-done((bf16[320,768]{1,0:T(8,128)(2,1)}, bf16[320,768]{1,0:T(8,128)(2,1)S(1)}, u32[]{:S(2)}, u32[]{:S(2)}) %collective-permute-start.27) | collective-permute-done | bytes 491552 | tf_op jit(solution)/shard_map/ppermute | solution.py:93
  166.1 5.6 %collective-permute-done.24 = bf16[320,768]{1,0:T(8,128)(2,1)S(1)} collective-permute-done((bf16[320,768]{1,0:T(8,128)(2,1)}, bf16[320,768]{1,0:T(8,128)(2,1)S(1)}, u32[]{:S(2)}, u32[]{:S(2)}) %collective-permute-start.24) | collective-permute-done | bytes 491552 | tf_op jit(solution)/shard_map/ppermute | solution.py:93
  181.0 9.9 %combine.1 = (bf16[256,768]{1,0:T(8,128)(2,1)}, f32[256,768]{1,0:T(8,128)}, bf16[256,768]{1,0:T(8,128)(2,1)}, bf16[384,896]{1,0:T(8,128)(2,1)}, bf16[384,896]{1,0:T(8,128)(2,1)}, /*index=5*/bf16[8,256]{1,0:T(8,128)(2,1)}) custom-call(s32[15]{0:T(128)} %stack.121.where, bf16[160,768]{1,0:T(8,128)(2,1)} %get-tuple-element.119.refs_0_, ...), custom_call_target="tpu_custom_call" | custom-call | flops 900000000 | bytes 3000000 | tf_op jit(solution)/shard_map/combine/pallas_call | solution.py:69
  191.7 12.4 %attend_back.2 = (bf16[256,384]{1,0:T(8,128)(2,1)}, bf16[1024,384]{1,0:T(8,128)(2,1)}, bf16[1024,384]{1,0:T(8,128)(2,1)}, bf16[384,1152]{1,0:T(8,128)(2,1)}, bf16[384,1152]{1,0:T(8,128)(2,1)}) custom-call(s32[15]{0:T(128)} %stack.131.where, bf16[256,768]{1,0:T(8,128)(2,1)} %get-tuple-element.97.q, bf16[1024,768]{1,0:T(8,128)(2,1)} %get-tuple-element.98.k, ...), custom_call_target="tpu_custom_call" | custom-call | flops 990000000 | bytes 3300000 | tf_op jit(solution)/shard_map/attend_back/pallas_call | solution.py:69
  204.1 6.7 %collective-permute-done.30.d0 = bf16[768,256]{1,0:T(8,128)(2,1)S(1)} collective-permute-done((bf16[768,256]{1,0:T(8,128)(2,1)}, bf16[768,256]{1,0:T(8,128)(2,1)S(1)}, u32[]{:S(2)}, u32[]{:S(2)}) %collective-permute-start.30) | collective-permute-done | bytes 393248 | tf_op jit(solution)/shard_map/ppermute | solution.py:97
  216.9 12.1 %attend_back.3 = (bf16[256,384]{1,0:T(8,128)(2,1)}, bf16[1024,384]{1,0:T(8,128)(2,1)}, bf16[1024,384]{1,0:T(8,128)(2,1)}, bf16[384,1152]{1,0:T(8,128)(2,1)}, bf16[384,1152]{1,0:T(8,128)(2,1)}) custom-call(s32[15]{0:T(128)} %stack.131.where, bf16[256,768]{1,0:T(8,128)(2,1)} %get-tuple-element.97.q, bf16[1024,768]{1,0:T(8,128)(2,1)} %get-tuple-element.98.k, ...), custom_call_target="tpu_custom_call" | custom-call | flops 990000000 | bytes 3300000 | tf_op jit(solution)/shard_map/attend_back/pallas_call | solution.py:69
  231.6 4.3 %collective-permute-done.43 = bf16[96,896]{1,0:T(8,128)(2,1)} collective-permute-done((bf16[96,896]{1,0:T(8,128)(2,1)S(1)}, bf16[96,896]{1,0:T(8,128)(2,1)}, u32[]{:S(2)}, u32[]{:S(2)}) %collective-permute-start.43) | collective-permute-done | bytes 172064 | tf_op jit(solution)/shard_map/ppermute | solution.py:93
  236.9 4.3 %collective-permute-done.38 = bf16[192,1152]{1,0:T(8,128)(2,1)S(1)} collective-permute-done((bf16[192,1152]{1,0:T(8,128)(2,1)S(1)}, bf16[192,1152]{1,0:T(8,128)(2,1)S(1)}, u32[]{:S(2)}, u32[]{:S(2)}) %collective-permute-start.38) | collective-permute-done | bytes 442400 | tf_op jit(solution)/shard_map/ppermute | solution.py:93
  242.8 5.0 %collective-permute-done.39 = bf16[96,1152]{1,0:T(8,128)(2,1)S(1)} collective-permute-done((bf16[96,1152]{1,0:T(8,128)(2,1)S(1)}, bf16[96,1152]{1,0:T(8,128)(2,1)S(1)}, u32[]{:S(2)}, u32[]{:S(2)}) %collective-permute-start.39) | collective-permute-done | bytes 221216 | tf_op jit(solution)/shard_map/ppermute | solution.py:93
  247.8 7.7 %project_back.1 = (bf16[1024,768]{1,0:T(8,128)(2,1)}, f32[256,768]{1,0:T(8,128)}) custom-call(s32[15]{0:T(128)} %stack.131.where, bf16[256,384]{1,0:T(8,128)(2,1)} %get-tuple-element.128.refs_0_, bf16[256,384]{1,0:T(8,128)(2,1)} %get-tuple-element.143.refs_1_, bf16[1024,384]{1,0:T(8,128)(2,1)} %get-tuple-element.144.refs_2_, ...), custom_call_target="tpu_custom_call" | custom-call | flops 540000000 | bytes 1800000 | tf_op jit(solution)/shard_map/project_back/pallas_call | solution.py:69
  257.2 4.7 %collective-permute-done.41 = bf16[96,1152]{1,0:T(8,128)(2,1)S(1)} collective-permute-done((bf16[96,1152]{1,0:T(8,128)(2,1)S(1)}, bf16[96,1152]{1,0:T(8,128)(2,1)S(1)}, u32[]{:S(2)}, u32[]{:S(2)}) %collective-permute-start.41) | collective-permute-done | bytes 221216 | tf_op jit(solution)/shard_map/ppermute | solution.py:93
  268.6 3.9 %sum_parts.1 = (bf16[768,256]{1,0:T(8,128)(2,1)}, f32[768,256]{1,0:T(8,128)}, f32[256,768]{1,0:T(8,128)}) custom-call(s32[1]{0:T(128)} %bitcast.25.where, bf16[2304,256]{1,0:T(8,128)(2,1)} %get-tuple-element.163.a, bf16[2304,256]{1,0:T(8,128)(2,1)} %collective-permute-done.31.b, bf16[2304,256]{1,0:T(8,128)(2,1)} %copy-done.5, bf16[768,256]{1,0:T(8,128)(2,1)} %copy-done.21, ...), custom_call_target="tpu_custom_call" | custom-call | flops 270000000 | bytes 900000 | tf_op jit(solution)/shard_map/sum_parts/pallas_call | solution.py:69
  281.8 4.2 %collective-permute-done.47 = bf16[24,3200]{1,0:T(8,128)(2,1)S(1)} collective-permute-done((bf16[24,3200]{1,0:T(8,128)(2,1)S(1)}, bf16[24,3200]{1,0:T(8,128)(2,1)S(1)}, u32[]{:S(2)}, u32[]{:S(2)}) %collective-permute-start.47) | collective-permute-done | bytes 153632 | tf_op jit(solution)/shard_map/ppermute | solution.py:93
  (196 shorter events, 99.2 us)
Async XLA Ops:
  2.6 15.7 %collective-permute-start.4 = (bf16[96,1664]{1,0:T(8,128)(2,1)}, bf16[96,1664]{1,0:T(8,128)(2,1)S(1)}, u32[]{:S(2)}, u32[]{:S(2)}) collective-permute-start(bf16[96,1664]{1,0:T(8,128)(2,1)} %pack_shared.1), channel_id=1, source_target_pairs={{0,1},{1,0},{2,3},{3,2},{4,5},{5,4},{6,7},{7,6},{8,9},{9,8},{10,11... | collective-permute-start | bytes 958472 | tf_op jit(solution)/shard_map/ppermute | solution.py:93
  5.5 25.0 %collective-permute-start.3 = (bf16[96,1664]{1,0:T(8,128)(2,1)}, bf16[96,1664]{1,0:T(8,128)(2,1)S(1)}, u32[]{:S(2)}, u32[]{:S(2)}) collective-permute-start(bf16[96,1664]{1,0:T(8,128)(2,1)} %pack_shared.1), channel_id=1, source_target_pairs={{0,4},{1,5},{2,6},{3,7},{4,0},{5,1},{6,2},{7,3},{8,12},{9,13},{10,... | collective-permute-start | bytes 958472 | tf_op jit(solution)/shard_map/ppermute | solution.py:93
  8.1 15.2 %collective-permute-start.2 = (bf16[96,1664]{1,0:T(8,128)(2,1)}, bf16[96,1664]{1,0:T(8,128)(2,1)S(1)}, u32[]{:S(2)}, u32[]{:S(2)}) collective-permute-start(bf16[96,1664]{1,0:T(8,128)(2,1)} %pack_shared.1), channel_id=1, source_target_pairs={{0,2},{1,3},{2,0},{3,1},{4,6},{5,7},{6,4},{7,5},{8,10},{9,11},{10,... | collective-permute-start | bytes 958472 | tf_op jit(solution)/shard_map/ppermute | solution.py:93
  11.6 19.7 %collective-permute-start.7 = (bf16[768,256]{1,0:T(8,128)(2,1)}, bf16[768,256]{1,0:T(8,128)(2,1)S(1)}, u32[]{:S(2)}, u32[]{:S(2)}) collective-permute-start(bf16[768,256]{1,0:T(8,128)(2,1)} %blocks.1), channel_id=1, source_target_pairs={{0,1},{1,0},{2,3},{3,2},{4,5},{5,4},{6,7},{7,6},{8,9},{9,8},{10,11... | collective-permute-start | bytes 1179656 | tf_op jit(solution)/shard_map/ppermute | solution.py:93
  18.3 16.0 %collective-permute-start.5 = (bf16[96,1664]{1,0:T(8,128)(2,1)S(1)}, bf16[96,1664]{1,0:T(8,128)(2,1)S(1)}, u32[]{:S(2)}, u32[]{:S(2)}) collective-permute-start(bf16[96,1664]{1,0:T(8,128)(2,1)S(1)} %copy-done.4), channel_id=1, source_target_pairs={{0,6},{1,7},{2,4},{3,5},{4,2},{5,3},{6,0},{7,1},{8,14},{9,15},{10,... | collective-permute-start | bytes 958472 | tf_op jit(solution)/shard_map/ppermute | solution.py:93
  23.3 17.0 %collective-permute-start.6 = (bf16[96,1664]{1,0:T(8,128)(2,1)S(1)}, bf16[96,1664]{1,0:T(8,128)(2,1)S(1)}, u32[]{:S(2)}, u32[]{:S(2)}) collective-permute-start(bf16[96,1664]{1,0:T(8,128)(2,1)S(1)} %collective-permute-done.2), channel_id=1, source_target_pairs={{0,1},{1,0},{2,3},{3,2},{4,5},{5,4},{6,7},{7,6},{8,9},{9,8},{10,11... | collective-permute-start | bytes 958472 | tf_op jit(solution)/shard_map/ppermute | solution.py:93
  23.9 16.4 %collective-permute-start.1 = (bf16[512,768]{1,0:T(8,128)(2,1)S(1)}, bf16[512,768]{1,0:T(8,128)(2,1)S(1)}, u32[]{:S(2)}, u32[]{:S(2)}) collective-permute-start(bf16[512,768]{1,0:T(8,128)(2,1)S(1)} %pad_maximum_fusion.refs_0_), channel_id=1, source_target_pairs={{0,8},{8,0},{16,24},{24,16},{1,9},{9,1},{17,25},{25,17},{2,10},{10... | collective-permute-start | bytes 2359304 | tf_op jit(solution)/shard_map/ppermute | solution.py:93
  34.3 22.4 %collective-permute-start.11 = (bf16[256,768]{1,0:T(8,128)(2,1)S(1)}, bf16[256,768]{1,0:T(8,128)(2,1)}, u32[]{:S(2)}, u32[]{:S(2)}) collective-permute-start(bf16[256,768]{1,0:T(8,128)(2,1)S(1)} %bitcast.57), channel_id=1, source_target_pairs={{0,4},{1,5},{4,0},{5,1},{2,6},{3,7},{6,2},{7,3},{8,12},{9,13},{12,... | collective-permute-start | bytes 1179656 | tf_op jit(solution)/shard_map/ppermute | solution.py:97
  38.8 18.9 %collective-permute-start.10 = (bf16[256,768]{1,0:T(8,128)(2,1)S(1)}, bf16[256,768]{1,0:T(8,128)(2,1)S(1)}, u32[]{:S(2)}, u32[]{:S(2)}) collective-permute-start(bf16[256,768]{1,0:T(8,128)(2,1)S(1)} %bitcast.58), channel_id=1, source_target_pairs={{0,2},{1,3},{2,0},{3,1},{4,6},{5,7},{6,4},{7,5},{8,10},{9,11},{10,... | collective-permute-start | bytes 1179656 | tf_op jit(solution)/shard_map/ppermute | solution.py:97
  57.7 28.6 %collective-permute-start.14 = (bf16[256,768]{1,0:T(8,128)(2,1)S(1)}, bf16[256,768]{1,0:T(8,128)(2,1)}, u32[]{:S(2)}, u32[]{:S(2)}) collective-permute-start(bf16[256,768]{1,0:T(8,128)(2,1)S(1)} %bitcast.59), channel_id=1, source_target_pairs={{2,4},{3,5},{4,2},{5,3},{10,12},{11,13},{12,10},{13,11},{18,20},{1... | collective-permute-start | bytes 1179656 | tf_op jit(solution)/shard_map/ppermute | solution.py:97
  59.1 27.2 %collective-permute-start.13 = (bf16[256,768]{1,0:T(8,128)(2,1)}, bf16[256,768]{1,0:T(8,128)(2,1)}, u32[]{:S(2)}, u32[]{:S(2)}) collective-permute-start(bf16[256,768]{1,0:T(8,128)(2,1)} %collective-permute-done.11.refs_13_), channel_id=1, source_target_pairs={{4,6},{5,7},{2,0},{3,1},{12,14},{13,15},{10,8},{11,9},{20,22},{21,... | collective-permute-start | bytes 1179656 | tf_op jit(solution)/shard_map/ppermute | solution.py:97
  61.7 44.7 %collective-permute-start.21 = (bf16[1536,256]{1,0:T(8,128)(2,1)S(1)}, bf16[1536,256]{1,0:T(8,128)(2,1)S(1)}, u32[]{:S(2)}, u32[]{:S(2)}) collective-permute-start(bf16[1536,256]{1,0:T(8,128)(2,1)S(1)} %copy-done.2), channel_id=1, source_target_pairs={{0,2},{1,3},{2,0},{3,1},{4,6},{5,7},{6,4},{7,5},{8,10},{9,11},{10,... | collective-permute-start | bytes 2359304 | tf_op jit(solution)/shard_map/ppermute | solution.py:97
  65.1 41.4 %collective-permute-start.20 = (bf16[1536,256]{1,0:T(8,128)(2,1)S(1)}, bf16[1536,256]{1,0:T(8,128)(2,1)S(1)}, u32[]{:S(2)}, u32[]{:S(2)}) collective-permute-start(bf16[1536,256]{1,0:T(8,128)(2,1)S(1)} %copy-done.2), channel_id=1, source_target_pairs={{0,4},{1,5},{4,0},{5,1},{2,6},{3,7},{6,2},{7,3},{8,12},{9,13},{12,... | collective-permute-start | bytes 2359304 | tf_op jit(solution)/shard_map/ppermute | solution.py:97
  94.1 16.2 %collective-permute-start.18 = (bf16[320,768]{1,0:T(8,128)(2,1)S(1)}, bf16[320,768]{1,0:T(8,128)(2,1)}, u32[]{:S(2)}, u32[]{:S(2)}) collective-permute-start(bf16[320,768]{1,0:T(8,128)(2,1)S(1)} %pad_maximum_fusion.5), channel_id=1, source_target_pairs={{0,1},{1,0},{2,3},{3,2},{4,5},{5,4},{6,7},{7,6},{8,9},{9,8},{10,11... | collective-permute-start | bytes 1474568 | tf_op jit(solution)/shard_map/ppermute | solution.py:93
  108.0 21.3 %collective-permute-start.23 = (bf16[1536,256]{1,0:T(8,128)(2,1)S(1)}, bf16[1536,256]{1,0:T(8,128)(2,1)}, u32[]{:S(2)}, u32[]{:S(2)}) collective-permute-start(bf16[1536,256]{1,0:T(8,128)(2,1)S(1)} %collective-permute-done.20.refs_8_), channel_id=1, source_target_pairs={{4,6},{5,7},{2,0},{3,1},{12,14},{13,15},{10,8},{11,9},{20,22},{21,... | collective-permute-start | bytes 2359304 | tf_op jit(solution)/shard_map/ppermute | solution.py:97
  110.3 19.0 %collective-permute-start.19 = (bf16[320,768]{1,0:T(8,128)(2,1)}, bf16[320,768]{1,0:T(8,128)(2,1)}, u32[]{:S(2)}, u32[]{:S(2)}) collective-permute-start(bf16[320,768]{1,0:T(8,128)(2,1)} %pad_maximum_fusion.6), channel_id=1, source_target_pairs={{0,1},{1,0},{2,3},{3,2},{4,5},{5,4},{6,7},{7,6},{8,9},{9,8},{10,11... | collective-permute-start | bytes 1474568 | tf_op jit(solution)/shard_map/ppermute | solution.py:93
  149.4 22.3 %collective-permute-start.24 = (bf16[320,768]{1,0:T(8,128)(2,1)}, bf16[320,768]{1,0:T(8,128)(2,1)S(1)}, u32[]{:S(2)}, u32[]{:S(2)}) collective-permute-start(bf16[320,768]{1,0:T(8,128)(2,1)} %get-tuple-element.116), channel_id=1, source_target_pairs={{0,1},{1,0},{2,3},{3,2},{4,5},{5,4},{6,7},{7,6},{8,9},{9,8},{10,11... | collective-permute-start | bytes 1474568 | tf_op jit(solution)/shard_map/ppermute | solution.py:93
  150.9 25.7 %collective-permute-start.25 = (bf16[2304,256]{1,0:T(8,128)(2,1)}, bf16[2304,256]{1,0:T(8,128)(2,1)S(1)}, u32[]{:S(2)}, u32[]{:S(2)}) collective-permute-start(bf16[2304,256]{1,0:T(8,128)(2,1)} %get-tuple-element.118), channel_id=1, source_target_pairs={{0,2},{1,3},{6,4},{7,5},{8,10},{9,11},{14,12},{15,13},{16,18},{17,... | collective-permute-start | bytes 3538952 | tf_op jit(solution)/shard_map/ppermute | solution.py:97
  152.3 27.7 %collective-permute-start.26 = (bf16[2304,256]{1,0:T(8,128)(2,1)}, bf16[2304,256]{1,0:T(8,128)(2,1)S(1)}, u32[]{:S(2)}, u32[]{:S(2)}) collective-permute-start(bf16[2304,256]{1,0:T(8,128)(2,1)} %get-tuple-element.118), channel_id=1, source_target_pairs={{2,4},{3,5},{4,2},{5,3},{10,12},{11,13},{12,10},{13,11},{18,20},{1... | collective-permute-start | bytes 3538952 | tf_op jit(solution)/shard_map/ppermute | solution.py:97
  176.6 35.1 %collective-permute-start.31 = (bf16[2304,256]{1,0:T(8,128)(2,1)}, bf16[2304,256]{1,0:T(8,128)(2,1)}, u32[]{:S(2)}, u32[]{:S(2)}) collective-permute-start(bf16[2304,256]{1,0:T(8,128)(2,1)} %get-tuple-element.133), channel_id=1, source_target_pairs={{0,2},{1,3},{2,0},{3,1},{4,6},{5,7},{6,4},{7,5},{8,10},{9,11},{10,... | collective-permute-start | bytes 3538952 | tf_op jit(solution)/shard_map/ppermute | solution.py:97
  180.0 30.7 %collective-permute-start.30 = (bf16[768,256]{1,0:T(8,128)(2,1)}, bf16[768,256]{1,0:T(8,128)(2,1)S(1)}, u32[]{:S(2)}, u32[]{:S(2)}) collective-permute-start(bf16[768,256]{1,0:T(8,128)(2,1)} %slice.115), channel_id=1, source_target_pairs={{0,4},{1,5},{4,0},{5,1},{2,6},{3,7},{6,2},{7,3},{8,12},{9,13},{12,... | collective-permute-start | bytes 1179656 | tf_op jit(solution)/shard_map/ppermute | solution.py:97
  190.9 23.9 %collective-permute-start.33 = (bf16[384,896]{1,0:T(8,128)(2,1)}, bf16[384,896]{1,0:T(8,128)(2,1)S(1)}, u32[]{:S(2)}, u32[]{:S(2)}) collective-permute-start(bf16[384,896]{1,0:T(8,128)(2,1)} %get-tuple-element.137), channel_id=1, source_target_pairs={{0,8},{8,0},{16,24},{24,16},{1,9},{9,1},{17,25},{25,17},{2,10},{10... | collective-permute-start | bytes 2064392 | tf_op jit(solution)/shard_map/ppermute | solution.py:93
  212.4 19.1 %collective-permute-start.34 = (bf16[576,256]{1,0:T(8,128)(2,1)}, bf16[576,256]{1,0:T(8,128)(2,1)}, u32[]{:S(2)}, u32[]{:S(2)}) collective-permute-start(bf16[576,256]{1,0:T(8,128)(2,1)} %slice.116), channel_id=1, source_target_pairs={{0,4},{1,5},{4,0},{5,1},{2,6},{3,7},{6,2},{7,3},{8,12},{9,13},{12,... | collective-permute-start | bytes 884744 | tf_op jit(solution)/shard_map/ppermute | solution.py:97
  230.5 37.4 %collective-permute-start.49 = (bf16[960,256]{1,0:T(8,128)(2,1)S(1)}, bf16[960,256]{1,0:T(8,128)(2,1)S(1)}, u32[]{:S(2)}, u32[]{:S(2)}) collective-permute-start(bf16[960,256]{1,0:T(8,128)(2,1)S(1)} %slice.131), channel_id=1, source_target_pairs={{0,4},{1,5},{4,0},{5,1},{2,6},{3,7},{6,2},{7,3},{8,12},{9,13},{12,... | collective-permute-start | bytes 1474568 | tf_op jit(solution)/shard_map/ppermute | solution.py:97
  (52 other events, 549.4 us)

commit v4 on v3

--- a/solution.py
+++ b/solution.py
@@ -148,14 +148,14 @@
     for block in range(8):
         here = slice(block * rows, (block + 1) * rows)
         base = 2 * block * rows
-        d, cut = ((d0, 0), (d1, 8 * rows), (d2, 14 * rows))[(block > 3) + (block > 6)]
+        d, cut = ((d0, 0), (d1, 4 * rows), (d2, 10 * rows))[(block > 1) + (block > 4)]
         own = pl.multiple_of(base + mine * rows, rows)
         other = pl.multiple_of(base + (1 - mine) * rows, rows)
         away[here, :] = total(other, rows, d, cut).astype(BF)
         kept[here, :] = total(own, rows, d, cut)
     for block in range(3):
         base = 16 * rows + block * 256
-        down[:, block * 256 : (block + 1) * 256] = total(base, 256, d2, 14 * rows)
+        down[:, block * 256 : (block + 1) * 256] = total(base, 256, d2, 10 * rows)
 
 
 def unpack_kernel(where, kept, arrived, out):
@@ -971,7 +971,7 @@
         middle = along(grads[3], MIDDLE)
         sent = added(grads[2], first)
         near = along(after(grads[1], first), NEAR)
-        cuts = (0, 8 * shard_rows, 14 * shard_rows, sent.shape[0])
+        cuts = (0, 4 * shard_rows, 10 * shard_rows, sent.shape[0])
         far = [along(sent[a:b], FAR) for a, b in zip(cuts, cuts[1:])]
         backs[0] = after(backs[0], sent, middle)
     else:

time: 293 us -> 289 us (0.986)
  waiting for transfers between devices: 106 us -> 100 us
    ppermute x14, waiting for transfers between devices: 43.6 us -> 39.5 us  [along(): lax.ppermute(values, 'fsdp', [(2 * i + b, 2 * j + b) for i, j in pairs fo...]
    unnamed x58 -> x60, local copies, waits for them, and re-layouts: 9 us -> 9.07 us
where the time goes in v4:
time: 289 us; the launch traced here: 288 us
  Pallas kernels  106 us (37%)
  waiting for transfers between devices  100 us (35%)
  starting transfers between devices  53.6 us (19%)
  local copies, waits for them, and re-layouts  16.7 us (6%)
  other arithmetic  10.9 us (4%)
    pallas_call x15, Pallas kernels, call(): pl.pallas_call(kernel, out_shape=outs, grid_spec=pltpu.PrefetchScalarGrid...  106 us
    ppermute x37, waiting for transfers between devices, swap(): return lax.ppermute(values, axis, [(i, i ^ bits) for i in range(size)])  60.6 us
    ppermute x14, waiting for transfers between devices, along(): lax.ppermute(values, 'fsdp', [(2 * i + b, 2 * j + b) for i, j in pairs fo...  39.5 us
    ppermute x37, starting transfers between devices, swap(): return lax.ppermute(values, axis, [(i, i ^ bits) for i in range(size)])  31.5 us
    ppermute x14, starting transfers between devices, along(): lax.ppermute(values, 'fsdp', [(2 * i + b, 2 * j + b) for i, j in pairs fo...  22.1 us
    unnamed x60, local copies, waits for them, and re-layouts  9.07 us
  transfers between devices with their start and end apart: 51, of which 21 were waited for; matrix products, arithmetic and copies ran while one was open for 8% of the time, Pallas kernels for 28%

profile of v4, /device:TPU:0, one launch (start us, length us, event | category | flops | bytes accessed | tf_op | source)
XLA Modules:
  0.0 288.2 jit_solution(18087014408010888758)
XLA Ops:
  18.6 4.7 %collective-permute-done.2 = bf16[96,1664]{1,0:T(8,128)(2,1)S(1)} collective-permute-done((bf16[96,1664]{1,0:T(8,128)(2,1)}, bf16[96,1664]{1,0:T(8,128)(2,1)S(1)}, u32[]{:S(2)}, u32[]{:S(2)}) %collective-permute-start.2) | collective-permute-done | bytes 319520 | tf_op jit(solution)/shard_map/ppermute | solution.py:93
  24.8 5.8 %collective-permute-done.3 = bf16[96,1664]{1,0:T(8,128)(2,1)S(1)} collective-permute-done((bf16[96,1664]{1,0:T(8,128)(2,1)}, bf16[96,1664]{1,0:T(8,128)(2,1)S(1)}, u32[]{:S(2)}, u32[]{:S(2)}) %collective-permute-start.3) | collective-permute-done | bytes 319520 | tf_op jit(solution)/shard_map/ppermute | solution.py:93
  34.3 4.5 %collective-permute-start.11 = (bf16[256,768]{1,0:T(8,128)(2,1)S(1)}, bf16[256,768]{1,0:T(8,128)(2,1)}, u32[]{:S(2)}, u32[]{:S(2)}) collective-permute-start(bf16[256,768]{1,0:T(8,128)(2,1)S(1)} %bitcast.57), channel_id=1, source_target_pairs={{0,4},{1,5},{4,0},{5,1},{2,6},{3,7},{6,2},{7,3},{8,12},{9,13},{12,... | collective-permute-start | bytes 1179656 | tf_op jit(solution)/shard_map/ppermute | solution.py:97
  42.4 7.1 %collective-permute-done.9 = bf16[96,1664]{1,0:T(8,128)(2,1)S(1)} collective-permute-done((bf16[96,1664]{1,0:T(8,128)(2,1)S(1)}, bf16[96,1664]{1,0:T(8,128)(2,1)S(1)}, u32[]{:S(2)}, u32[]{:S(2)}) %collective-permute-start.9) | collective-permute-done | bytes 319520 | tf_op jit(solution)/shard_map/ppermute | solution.py:93
  50.3 6.4 %collective-permute-done.11.refs_13_ = bf16[256,768]{1,0:T(8,128)(2,1)} collective-permute-done((bf16[256,768]{1,0:T(8,128)(2,1)S(1)}, bf16[256,768]{1,0:T(8,128)(2,1)}, u32[]{:S(2)}, u32[]{:S(2)}) %collective-permute-start.11) | collective-permute-done | bytes 393248 | tf_op jit(solution)/shard_map/ppermute | solution.py:97
  61.8 3.4 %collective-permute-start.21 = (bf16[1536,256]{1,0:T(8,128)(2,1)S(1)}, bf16[1536,256]{1,0:T(8,128)(2,1)S(1)}, u32[]{:S(2)}, u32[]{:S(2)}) collective-permute-start(bf16[1536,256]{1,0:T(8,128)(2,1)S(1)} %copy-done.2), channel_id=1, source_target_pairs={{0,2},{1,3},{2,0},{3,1},{4,6},{5,7},{6,4},{7,5},{8,10},{9,11},{10,... | collective-permute-start | bytes 2359304 | tf_op jit(solution)/shard_map/ppermute | solution.py:97
  65.2 11.0 %project.1 = (bf16[256,768]{1,0:T(8,128)(2,1)}, bf16[1024,768]{1,0:T(8,128)(2,1)}, bf16[1024,768]{1,0:T(8,128)(2,1)}, bf16[768,1024]{1,0:T(8,128)(2,1)}, bf16[76...) custom-call(s32[14]{0:T(128)} %stack.129.where, ...), custom_call_target="tpu_custom_call" | custom-call | flops 900000000 | bytes 3000000 | tf_op jit(solution)/shard_map/project/pallas_call | solution.py:69
  76.2 10.2 %attend.1 = (bf16[256,768]{1,0:T(8,128)(2,1)}, bf16[6,1024,512]{2,1,0:T(8,128)(2,1)}) custom-call(s32[14]{0:T(128)} %stack.129.where, bf16[256,768]{1,0:T(8,128)(2,1)} %get-tuple-element.97.q, bf16[1024,768]{1,0:T(8,128)(2,1)} %get-tuple-element.98.k, bf16[1024,768]{1,0:T(8,128)(2,1)} %get-tuple-element.99.v), custom_call_target="tpu_custom_call" | custom-call | flops 1080000000 | bytes 3600000 | tf_op jit(solution)/shard_map/attend/pallas_call | solution.py:69
  86.4 5.0 %route.1 = (f32[256,768]{1,0:T(8,128)}, bf16[256,768]{1,0:T(8,128)(2,1)}, bf16[160,768]{1,0:T(8,128)(2,1)}, bf16[160,768]{1,0:T(8,128)(2,1)}, bf16[160,768]{1,0:T(8,128)(2,1)}, /*index=5*/bf16[160,768]{1,0:T(8,128)(2,1)}) custom-call(s32[15]{0:T(128)} %stack.121.where, bf16[256,768]{1,0:T(8,128)(2,1)} %get-tuple-element.102.att.refs_12_, ...), custom_call_target="tpu_custom_call" | custom-call | flops 450000000 | bytes 1500000 | tf_op jit(solution)/shard_map/route/pallas_call | solution.py:69
  97.6 8.9 %collective-permute-done.21.refs_7_ = bf16[1536,256]{1,0:T(8,128)(2,1)S(1)} collective-permute-done((bf16[1536,256]{1,0:T(8,128)(2,1)S(1)}, bf16[1536,256]{1,0:T(8,128)(2,1)S(1)}, u32[]{:S(2)}, u32[]{:S(2)}) %collective-permute-start.21) | collective-permute-done | bytes 786464 | tf_op jit(solution)/shard_map/ppermute | solution.py:97
  111.5 17.8 %collective-permute-done.23.refs_10_ = bf16[1536,256]{1,0:T(8,128)(2,1)} collective-permute-done((bf16[1536,256]{1,0:T(8,128)(2,1)S(1)}, bf16[1536,256]{1,0:T(8,128)(2,1)}, u32[]{:S(2)}, u32[]{:S(2)}) %collective-permute-start.23) | collective-permute-done | bytes 786464 | tf_op jit(solution)/shard_map/ppermute | solution.py:97
  129.3 19.5 %expert.1 = (f32[320,768]{1,0:T(8,128)}, f32[320,768]{1,0:T(8,128)}, bf16[320,768]{1,0:T(8,128)(2,1)}, bf16[320,768]{1,0:T(8,128)(2,1)}, bf16[2304,256]{1,0:T(8,...) custom-call(s32[5]{0:T(128)} %stack.128.where, ...), custom_call_target="tpu_custom_call" | custom-call | flops 1620000000 | bytes 5400000 | tf_op jit(solution)/shard_map/expert/pallas_call | solution.py:69
  153.1 10.2 %collective-permute-done.27 = bf16[320,768]{1,0:T(8,128)(2,1)S(1)} collective-permute-done((bf16[320,768]{1,0:T(8,128)(2,1)}, bf16[320,768]{1,0:T(8,128)(2,1)S(1)}, u32[]{:S(2)}, u32[]{:S(2)}) %collective-permute-start.27) | collective-permute-done | bytes 491552 | tf_op jit(solution)/shard_map/ppermute | solution.py:93
  166.2 5.6 %collective-permute-done.24 = bf16[320,768]{1,0:T(8,128)(2,1)S(1)} collective-permute-done((bf16[320,768]{1,0:T(8,128)(2,1)}, bf16[320,768]{1,0:T(8,128)(2,1)S(1)}, u32[]{:S(2)}, u32[]{:S(2)}) %collective-permute-start.24) | collective-permute-done | bytes 491552 | tf_op jit(solution)/shard_map/ppermute | solution.py:93
  180.2 9.9 %combine.1 = (bf16[256,768]{1,0:T(8,128)(2,1)}, f32[256,768]{1,0:T(8,128)}, bf16[256,768]{1,0:T(8,128)(2,1)}, bf16[384,896]{1,0:T(8,128)(2,1)}, bf16[384,896]{1,0:T(8,128)(2,1)}, /*index=5*/bf16[8,256]{1,0:T(8,128)(2,1)}) custom-call(s32[15]{0:T(128)} %stack.121.where, bf16[160,768]{1,0:T(8,128)(2,1)} %get-tuple-element.119.refs_0_, ...), custom_call_target="tpu_custom_call" | custom-call | flops 900000000 | bytes 3000000 | tf_op jit(solution)/shard_map/combine/pallas_call | solution.py:69
  191.5 12.4 %attend_back.2 = (bf16[256,384]{1,0:T(8,128)(2,1)}, bf16[1024,384]{1,0:T(8,128)(2,1)}, bf16[1024,384]{1,0:T(8,128)(2,1)}, bf16[384,1152]{1,0:T(8,128)(2,1)}, bf16[384,1152]{1,0:T(8,128)(2,1)}) custom-call(s32[15]{0:T(128)} %stack.131.where, bf16[256,768]{1,0:T(8,128)(2,1)} %get-tuple-element.97.q, bf16[1024,768]{1,0:T(8,128)(2,1)} %get-tuple-element.98.k, ...), custom_call_target="tpu_custom_call" | custom-call | flops 990000000 | bytes 3300000 | tf_op jit(solution)/shard_map/attend_back/pallas_call | solution.py:69
  212.5 12.1 %attend_back.3 = (bf16[256,384]{1,0:T(8,128)(2,1)}, bf16[1024,384]{1,0:T(8,128)(2,1)}, bf16[1024,384]{1,0:T(8,128)(2,1)}, bf16[384,1152]{1,0:T(8,128)(2,1)}, bf16[384,1152]{1,0:T(8,128)(2,1)}) custom-call(s32[15]{0:T(128)} %stack.131.where, bf16[256,768]{1,0:T(8,128)(2,1)} %get-tuple-element.97.q, bf16[1024,768]{1,0:T(8,128)(2,1)} %get-tuple-element.98.k, ...), custom_call_target="tpu_custom_call" | custom-call | flops 990000000 | bytes 3300000 | tf_op jit(solution)/shard_map/attend_back/pallas_call | solution.py:69
  227.7 4.5 %collective-permute-done.43 = bf16[96,896]{1,0:T(8,128)(2,1)} collective-permute-done((bf16[96,896]{1,0:T(8,128)(2,1)}, bf16[96,896]{1,0:T(8,128)(2,1)}, u32[]{:S(2)}, u32[]{:S(2)}) %collective-permute-start.43) | collective-permute-done | bytes 172064 | tf_op jit(solution)/shard_map/ppermute | solution.py:93
  233.2 3.5 %collective-permute-done.38 = bf16[192,1152]{1,0:T(8,128)(2,1)S(1)} collective-permute-done((bf16[192,1152]{1,0:T(8,128)(2,1)S(1)}, bf16[192,1152]{1,0:T(8,128)(2,1)S(1)}, u32[]{:S(2)}, u32[]{:S(2)}) %collective-permute-start.38) | collective-permute-done | bytes 442400 | tf_op jit(solution)/shard_map/ppermute | solution.py:93
  238.3 4.9 %collective-permute-done.39 = bf16[96,1152]{1,0:T(8,128)(2,1)S(1)} collective-permute-done((bf16[96,1152]{1,0:T(8,128)(2,1)S(1)}, bf16[96,1152]{1,0:T(8,128)(2,1)S(1)}, u32[]{:S(2)}, u32[]{:S(2)}) %collective-permute-start.39) | collective-permute-done | bytes 221216 | tf_op jit(solution)/shard_map/ppermute | solution.py:93
  243.3 7.7 %project_back.1 = (bf16[1024,768]{1,0:T(8,128)(2,1)}, f32[256,768]{1,0:T(8,128)}) custom-call(s32[15]{0:T(128)} %stack.131.where, bf16[256,384]{1,0:T(8,128)(2,1)} %get-tuple-element.128.refs_0_, bf16[256,384]{1,0:T(8,128)(2,1)} %get-tuple-element.143.refs_1_, bf16[1024,384]{1,0:T(8,128)(2,1)} %get-tuple-element.144.refs_2_, ...), custom_call_target="tpu_custom_call" | custom-call | flops 540000000 | bytes 1800000 | tf_op jit(solution)/shard_map/project_back/pallas_call | solution.py:69
  252.7 4.7 %collective-permute-done.41 = bf16[96,1152]{1,0:T(8,128)(2,1)S(1)} collective-permute-done((bf16[96,1152]{1,0:T(8,128)(2,1)S(1)}, bf16[96,1152]{1,0:T(8,128)(2,1)S(1)}, u32[]{:S(2)}, u32[]{:S(2)}) %collective-permute-start.41) | collective-permute-done | bytes 221216 | tf_op jit(solution)/shard_map/ppermute | solution.py:93
  264.6 3.9 %sum_parts.1 = (bf16[768,256]{1,0:T(8,128)(2,1)}, f32[768,256]{1,0:T(8,128)}, f32[256,768]{1,0:T(8,128)}) custom-call(s32[1]{0:T(128)} %bitcast.25.where, bf16[2304,256]{1,0:T(8,128)(2,1)} %get-tuple-element.163.a, bf16[2304,256]{1,0:T(8,128)(2,1)} %collective-permute-done.31.b, bf16[2304,256]{1,0:T(8,128)(2,1)} %copy-done.5, bf16[384,256]{1,0:T(8,128)(2,1)} %copy-done.24, ...), custom_call_target="tpu_custom_call" | custom-call | flops 270000000 | bytes 900000 | tf_op jit(solution)/shard_map/sum_parts/pallas_call | solution.py:69
  277.6 4.0 %collective-permute-done.47 = bf16[24,3200]{1,0:T(8,128)(2,1)S(1)} collective-permute-done((bf16[24,3200]{1,0:T(8,128)(2,1)S(1)}, bf16[24,3200]{1,0:T(8,128)(2,1)S(1)}, u32[]{:S(2)}, u32[]{:S(2)}) %collective-permute-start.47) | collective-permute-done | bytes 153632 | tf_op jit(solution)/shard_map/ppermute | solution.py:93
  (198 shorter events, 99.2 us)
Async XLA Ops:
  2.6 15.8 %collective-permute-start.4 = (bf16[96,1664]{1,0:T(8,128)(2,1)}, bf16[96,1664]{1,0:T(8,128)(2,1)S(1)}, u32[]{:S(2)}, u32[]{:S(2)}) collective-permute-start(bf16[96,1664]{1,0:T(8,128)(2,1)} %pack_shared.1), channel_id=1, source_target_pairs={{0,1},{1,0},{2,3},{3,2},{4,5},{5,4},{6,7},{7,6},{8,9},{9,8},{10,11... | collective-permute-start | bytes 958472 | tf_op jit(solution)/shard_map/ppermute | solution.py:93
  5.5 25.0 %collective-permute-start.3 = (bf16[96,1664]{1,0:T(8,128)(2,1)}, bf16[96,1664]{1,0:T(8,128)(2,1)S(1)}, u32[]{:S(2)}, u32[]{:S(2)}) collective-permute-start(bf16[96,1664]{1,0:T(8,128)(2,1)} %pack_shared.1), channel_id=1, source_target_pairs={{0,4},{1,5},{2,6},{3,7},{4,0},{5,1},{6,2},{7,3},{8,12},{9,13},{10,... | collective-permute-start | bytes 958472 | tf_op jit(solution)/shard_map/ppermute | solution.py:93
  8.1 15.2 %collective-permute-start.2 = (bf16[96,1664]{1,0:T(8,128)(2,1)}, bf16[96,1664]{1,0:T(8,128)(2,1)S(1)}, u32[]{:S(2)}, u32[]{:S(2)}) collective-permute-start(bf16[96,1664]{1,0:T(8,128)(2,1)} %pack_shared.1), channel_id=1, source_target_pairs={{0,2},{1,3},{2,0},{3,1},{4,6},{5,7},{6,4},{7,5},{8,10},{9,11},{10,... | collective-permute-start | bytes 958472 | tf_op jit(solution)/shard_map/ppermute | solution.py:93
  11.6 19.7 %collective-permute-start.7 = (bf16[768,256]{1,0:T(8,128)(2,1)}, bf16[768,256]{1,0:T(8,128)(2,1)S(1)}, u32[]{:S(2)}, u32[]{:S(2)}) collective-permute-start(bf16[768,256]{1,0:T(8,128)(2,1)} %blocks.1), channel_id=1, source_target_pairs={{0,1},{1,0},{2,3},{3,2},{4,5},{5,4},{6,7},{7,6},{8,9},{9,8},{10,11... | collective-permute-start | bytes 1179656 | tf_op jit(solution)/shard_map/ppermute | solution.py:93
  18.4 15.9 %collective-permute-start.5 = (bf16[96,1664]{1,0:T(8,128)(2,1)S(1)}, bf16[96,1664]{1,0:T(8,128)(2,1)S(1)}, u32[]{:S(2)}, u32[]{:S(2)}) collective-permute-start(bf16[96,1664]{1,0:T(8,128)(2,1)S(1)} %copy-done.4), channel_id=1, source_target_pairs={{0,6},{1,7},{2,4},{3,5},{4,2},{5,3},{6,0},{7,1},{8,14},{9,15},{10,... | collective-permute-start | bytes 958472 | tf_op jit(solution)/shard_map/ppermute | solution.py:93
  23.3 17.0 %collective-permute-start.6 = (bf16[96,1664]{1,0:T(8,128)(2,1)S(1)}, bf16[96,1664]{1,0:T(8,128)(2,1)S(1)}, u32[]{:S(2)}, u32[]{:S(2)}) collective-permute-start(bf16[96,1664]{1,0:T(8,128)(2,1)S(1)} %collective-permute-done.2), channel_id=1, source_target_pairs={{0,1},{1,0},{2,3},{3,2},{4,5},{5,4},{6,7},{7,6},{8,9},{9,8},{10,11... | collective-permute-start | bytes 958472 | tf_op jit(solution)/shard_map/ppermute | solution.py:93
  23.9 16.4 %collective-permute-start.1 = (bf16[512,768]{1,0:T(8,128)(2,1)S(1)}, bf16[512,768]{1,0:T(8,128)(2,1)S(1)}, u32[]{:S(2)}, u32[]{:S(2)}) collective-permute-start(bf16[512,768]{1,0:T(8,128)(2,1)S(1)} %pad_maximum_fusion.refs_0_), channel_id=1, source_target_pairs={{0,8},{8,0},{16,24},{24,16},{1,9},{9,1},{17,25},{25,17},{2,10},{10... | collective-permute-start | bytes 2359304 | tf_op jit(solution)/shard_map/ppermute | solution.py:93
  34.3 22.4 %collective-permute-start.11 = (bf16[256,768]{1,0:T(8,128)(2,1)S(1)}, bf16[256,768]{1,0:T(8,128)(2,1)}, u32[]{:S(2)}, u32[]{:S(2)}) collective-permute-start(bf16[256,768]{1,0:T(8,128)(2,1)S(1)} %bitcast.57), channel_id=1, source_target_pairs={{0,4},{1,5},{4,0},{5,1},{2,6},{3,7},{6,2},{7,3},{8,12},{9,13},{12,... | collective-permute-start | bytes 1179656 | tf_op jit(solution)/shard_map/ppermute | solution.py:97
  38.8 18.9 %collective-permute-start.10 = (bf16[256,768]{1,0:T(8,128)(2,1)S(1)}, bf16[256,768]{1,0:T(8,128)(2,1)S(1)}, u32[]{:S(2)}, u32[]{:S(2)}) collective-permute-start(bf16[256,768]{1,0:T(8,128)(2,1)S(1)} %bitcast.58), channel_id=1, source_target_pairs={{0,2},{1,3},{2,0},{3,1},{4,6},{5,7},{6,4},{7,5},{8,10},{9,11},{10,... | collective-permute-start | bytes 1179656 | tf_op jit(solution)/shard_map/ppermute | solution.py:97
  57.7 28.7 %collective-permute-start.14 = (bf16[256,768]{1,0:T(8,128)(2,1)S(1)}, bf16[256,768]{1,0:T(8,128)(2,1)}, u32[]{:S(2)}, u32[]{:S(2)}) collective-permute-start(bf16[256,768]{1,0:T(8,128)(2,1)S(1)} %bitcast.59), channel_id=1, source_target_pairs={{2,4},{3,5},{4,2},{5,3},{10,12},{11,13},{12,10},{13,11},{18,20},{1... | collective-permute-start | bytes 1179656 | tf_op jit(solution)/shard_map/ppermute | solution.py:97
  59.2 27.2 %collective-permute-start.13 = (bf16[256,768]{1,0:T(8,128)(2,1)}, bf16[256,768]{1,0:T(8,128)(2,1)}, u32[]{:S(2)}, u32[]{:S(2)}) collective-permute-start(bf16[256,768]{1,0:T(8,128)(2,1)} %collective-permute-done.11.refs_13_), channel_id=1, source_target_pairs={{4,6},{5,7},{2,0},{3,1},{12,14},{13,15},{10,8},{11,9},{20,22},{21,... | collective-permute-start | bytes 1179656 | tf_op jit(solution)/shard_map/ppermute | solution.py:97
  61.8 44.7 %collective-permute-start.21 = (bf16[1536,256]{1,0:T(8,128)(2,1)S(1)}, bf16[1536,256]{1,0:T(8,128)(2,1)S(1)}, u32[]{:S(2)}, u32[]{:S(2)}) collective-permute-start(bf16[1536,256]{1,0:T(8,128)(2,1)S(1)} %copy-done.2), channel_id=1, source_target_pairs={{0,2},{1,3},{2,0},{3,1},{4,6},{5,7},{6,4},{7,5},{8,10},{9,11},{10,... | collective-permute-start | bytes 2359304 | tf_op jit(solution)/shard_map/ppermute | solution.py:97
  65.2 41.3 %collective-permute-start.20 = (bf16[1536,256]{1,0:T(8,128)(2,1)S(1)}, bf16[1536,256]{1,0:T(8,128)(2,1)S(1)}, u32[]{:S(2)}, u32[]{:S(2)}) collective-permute-start(bf16[1536,256]{1,0:T(8,128)(2,1)S(1)} %copy-done.2), channel_id=1, source_target_pairs={{0,4},{1,5},{4,0},{5,1},{2,6},{3,7},{6,2},{7,3},{8,12},{9,13},{12,... | collective-permute-start | bytes 2359304 | tf_op jit(solution)/shard_map/ppermute | solution.py:97
  94.2 16.1 %collective-permute-start.18 = (bf16[320,768]{1,0:T(8,128)(2,1)S(1)}, bf16[320,768]{1,0:T(8,128)(2,1)}, u32[]{:S(2)}, u32[]{:S(2)}) collective-permute-start(bf16[320,768]{1,0:T(8,128)(2,1)S(1)} %pad_maximum_fusion.5), channel_id=1, source_target_pairs={{0,1},{1,0},{2,3},{3,2},{4,5},{5,4},{6,7},{7,6},{8,9},{9,8},{10,11... | collective-permute-start | bytes 1474568 | tf_op jit(solution)/shard_map/ppermute | solution.py:93
  108.0 21.3 %collective-permute-start.23 = (bf16[1536,256]{1,0:T(8,128)(2,1)S(1)}, bf16[1536,256]{1,0:T(8,128)(2,1)}, u32[]{:S(2)}, u32[]{:S(2)}) collective-permute-start(bf16[1536,256]{1,0:T(8,128)(2,1)S(1)} %collective-permute-done.20.refs_8_), channel_id=1, source_target_pairs={{4,6},{5,7},{2,0},{3,1},{12,14},{13,15},{10,8},{11,9},{20,22},{21,... | collective-permute-start | bytes 2359304 | tf_op jit(solution)/shard_map/ppermute | solution.py:97
  110.3 19.0 %collective-permute-start.19 = (bf16[320,768]{1,0:T(8,128)(2,1)}, bf16[320,768]{1,0:T(8,128)(2,1)}, u32[]{:S(2)}, u32[]{:S(2)}) collective-permute-start(bf16[320,768]{1,0:T(8,128)(2,1)} %pad_maximum_fusion.6), channel_id=1, source_target_pairs={{0,1},{1,0},{2,3},{3,2},{4,5},{5,4},{6,7},{7,6},{8,9},{9,8},{10,11... | collective-permute-start | bytes 1474568 | tf_op jit(solution)/shard_map/ppermute | solution.py:93
  149.5 22.3 %collective-permute-start.24 = (bf16[320,768]{1,0:T(8,128)(2,1)}, bf16[320,768]{1,0:T(8,128)(2,1)S(1)}, u32[]{:S(2)}, u32[]{:S(2)}) collective-permute-start(bf16[320,768]{1,0:T(8,128)(2,1)} %get-tuple-element.116), channel_id=1, source_target_pairs={{0,1},{1,0},{2,3},{3,2},{4,5},{5,4},{6,7},{7,6},{8,9},{9,8},{10,11... | collective-permute-start | bytes 1474568 | tf_op jit(solution)/shard_map/ppermute | solution.py:93
  150.9 25.7 %collective-permute-start.25 = (bf16[2304,256]{1,0:T(8,128)(2,1)}, bf16[2304,256]{1,0:T(8,128)(2,1)S(1)}, u32[]{:S(2)}, u32[]{:S(2)}) collective-permute-start(bf16[2304,256]{1,0:T(8,128)(2,1)} %get-tuple-element.118), channel_id=1, source_target_pairs={{0,2},{1,3},{6,4},{7,5},{8,10},{9,11},{14,12},{15,13},{16,18},{17,... | collective-permute-start | bytes 3538952 | tf_op jit(solution)/shard_map/ppermute | solution.py:97
  152.4 26.9 %collective-permute-start.26 = (bf16[2304,256]{1,0:T(8,128)(2,1)}, bf16[2304,256]{1,0:T(8,128)(2,1)S(1)}, u32[]{:S(2)}, u32[]{:S(2)}) collective-permute-start(bf16[2304,256]{1,0:T(8,128)(2,1)} %get-tuple-element.118), channel_id=1, source_target_pairs={{2,4},{3,5},{4,2},{5,3},{10,12},{11,13},{12,10},{13,11},{18,20},{1... | collective-permute-start | bytes 3538952 | tf_op jit(solution)/shard_map/ppermute | solution.py:97
  176.6 30.7 %collective-permute-start.31 = (bf16[2304,256]{1,0:T(8,128)(2,1)S(1)}, bf16[2304,256]{1,0:T(8,128)(2,1)}, u32[]{:S(2)}, u32[]{:S(2)}) collective-permute-start(bf16[2304,256]{1,0:T(8,128)(2,1)S(1)} %copy-done.25), channel_id=1, source_target_pairs={{0,2},{1,3},{2,0},{3,1},{4,6},{5,7},{6,4},{7,5},{8,10},{9,11},{10,... | collective-permute-start | bytes 3538952 | tf_op jit(solution)/shard_map/ppermute | solution.py:97
  190.1 20.4 %collective-permute-start.33 = (bf16[384,896]{1,0:T(8,128)(2,1)}, bf16[384,896]{1,0:T(8,128)(2,1)S(1)}, u32[]{:S(2)}, u32[]{:S(2)}) collective-permute-start(bf16[384,896]{1,0:T(8,128)(2,1)} %get-tuple-element.137), channel_id=1, source_target_pairs={{0,8},{8,0},{16,24},{24,16},{1,9},{9,1},{17,25},{25,17},{2,10},{10... | collective-permute-start | bytes 2064392 | tf_op jit(solution)/shard_map/ppermute | solution.py:93
  190.2 16.1 %collective-permute-start.30 = (bf16[384,256]{1,0:T(8,128)(2,1)S(1)}, bf16[384,256]{1,0:T(8,128)(2,1)S(1)}, u32[]{:S(2)}, u32[]{:S(2)}) collective-permute-start(bf16[384,256]{1,0:T(8,128)(2,1)S(1)} %slice.115), channel_id=1, source_target_pairs={{0,4},{1,5},{4,0},{5,1},{2,6},{3,7},{6,2},{7,3},{8,12},{9,13},{12,... | collective-permute-start | bytes 589832 | tf_op jit(solution)/shard_map/ppermute | solution.py:97
  208.0 19.7 %collective-permute-start.34 = (bf16[576,256]{1,0:T(8,128)(2,1)}, bf16[576,256]{1,0:T(8,128)(2,1)}, u32[]{:S(2)}, u32[]{:S(2)}) collective-permute-start(bf16[576,256]{1,0:T(8,128)(2,1)} %slice.116), channel_id=1, source_target_pairs={{0,4},{1,5},{4,0},{5,1},{2,6},{3,7},{6,2},{7,3},{8,12},{9,13},{12,... | collective-permute-start | bytes 884744 | tf_op jit(solution)/shard_map/ppermute | solution.py:97
  226.6 37.1 %collective-permute-start.49 = (bf16[1344,256]{1,0:T(8,128)(2,1)S(1)}, bf16[1344,256]{1,0:T(8,128)(2,1)S(1)}, u32[]{:S(2)}, u32[]{:S(2)}) collective-permute-start(bf16[1344,256]{1,0:T(8,128)(2,1)S(1)} %slice.131), channel_id=1, source_target_pairs={{0,4},{1,5},{4,0},{5,1},{2,6},{3,7},{6,2},{7,3},{8,12},{9,13},{12,... | collective-permute-start | bytes 2064392 | tf_op jit(solution)/shard_map/ppermute | solution.py:97
  (53 other events, 549.8 us)
